TPU v7x, 32 devices: a whole 2x2x4 slice. The times are simulated.
32 devices in a mesh: wide: 8 (over z, y), narrow: 4 (over x, core).
Axes of the slice: x: 2, y: 2, z: 4, core: 2. Of those that a mesh axis runs over, the one named last changes fastest.
Arguments:
- passages: bfloat16 [24, 512, 768], P('wide', 'narrow'), may hold values from -6 to 6
- queries: bfloat16 [8, 512, 768], P('wide', 'narrow'), may hold values from -6 to 6
- passage_cot: bfloat16 [24, 512, 768], P('wide', 'narrow'), may hold values from -3 to 3
- query_cot: bfloat16 [8, 512, 768], P('wide', 'narrow'), may hold values from -3 to 3
- passage_lengths: int32 [24, 5], P('wide'), may hold values from 1 to 400, as said below
- query_lengths: int32 [8, 17], P('wide'), may hold values from 1 to 40, 512 in all within a row
- labels: int32 [128], P('wide'), may hold values from 0 to 95
- w_qkv: bfloat16 [2, 768, 2304], P(None, ('wide', 'narrow')), may hold values from -0.3125 to 0.3125
- w_out: bfloat16 [2, 768, 768], P(None, ('wide', 'narrow')), may hold values from -0.875 to 0.875
- w_in: bfloat16 [2, 768, 3072], P(None, ('wide', 'narrow')), may hold values from -0.21875 to 0.21875
- w_back: bfloat16 [2, 3072, 768], P(None, ('wide', 'narrow')), may hold values from -0.15625 to 0.15625
- biases: bfloat16 [2, 6, 768], P(None, None, ('wide', 'narrow')), may hold values from -1 to 1
- norm_gains: bfloat16 [2, 2, 768], P(None, None, ('wide', 'narrow')), may hold values from 0.5 to 1.5
- in_bias: bfloat16 [2, 3072], P(None, ('wide', 'narrow')), may hold values from -1 to 1
Outputs:
- passage_out: bfloat16 [24, 512, 768], P('wide', 'narrow')
- query_out: bfloat16 [8, 512, 768], P('wide', 'narrow')
- passage_grad: bfloat16 [24, 512, 768], P('wide', 'narrow')
- query_grad: bfloat16 [8, 512, 768], P('wide', 'narrow')
- grad_w_qkv: float32 [2, 768, 2304], P(None, 'wide', 'narrow')
- grad_w_out: float32 [2, 768, 768], P(None, 'wide', 'narrow')
- grad_w_in: float32 [2, 768, 3072], P(None, 'wide', 'narrow')
- grad_w_back: float32 [2, 3072, 768], P(None, 'wide', 'narrow')
- grad_biases: float32 [2, 6, 768], P(None, None, ('wide', 'narrow'))
- grad_gains: float32 [2, 2, 768], P(None, None, ('wide', 'narrow'))
- grad_in_bias: float32 [2, 3072], P(None, ('wide', 'narrow'))
- rms_stats: float32 [2, 4], replicated
Inputs may be any that keep to these rules, and one draw needn't show every extreme that they name: `passage_lengths`: entries s < 4 of a row are its passages' lengths, the last entry its padding's; each row sums to 512. Among the 3 rows of each index of wide, one row, drawn from the seed, begins with a passage of exactly 400 tokens. `query_lengths`: entries s < 16 of a row are its queries' lengths, the last entry its padding's; each row sums to 512, and some row of every draw has an entry of exactly 40. `labels`: query r * 16 + s is segment s of query row r; passage r * 4 + s is segment s of passage row r.
All inputs are finite; a program needn't handle non-finite values.
Results may differ from a plain program's by a relative error of at most 0.015.
Values may be sent and summed in bfloat16 or wider, within the bound.
No kernel may reach another device: no remote copies, remote signals or barrier semaphores. Data moves between devices by JAX's collectives and lax.ppermute only.
A program may use at most 256 MiB of HBM per device.

v0:
```python
import functools
import math

import jax
import jax.numpy as jnp
from jax import lax
from jax.experimental import pallas as pl
from jax.experimental.pallas import tpu as pltpu
from jax.sharding import PartitionSpec as P

HEAD_DIM = 64
LEVELS = 4
GROUP = 4
POOL = 32
STEP = 128
VMEM = 58 << 20
OTHERS = ((1, 1), (1, 0), (0, 1))


def cost(us):
    return pl.CostEstimate(flops=int(us * 1.15e9), bytes_accessed=1024, transcendentals=0)


EPSILON = 1e-05
SCORE_DIV = 12.0
MASKED = -1e30
BF = jnp.bfloat16
F32 = jnp.float32
BOTH = ("wide", "narrow")


def matmul(left, right):
    return jnp.dot(left, right, preferred_element_type=F32)


def inner_rows(left, right):
    return lax.dot_general(left, right, (((0,), (0,)), ((), ())), preferred_element_type=F32)


def inner_cols(left, right):
    return lax.dot_general(left, right, (((1,), (1,)), ((), ())), preferred_element_type=F32)


def flip(x, axis, mask):
    size = lax.axis_size(axis)
    return lax.ppermute(x, axis, [(i, i ^ mask) for i in range(size)])


def flip_both(x, wide_mask, narrow_mask):
    wide, narrow = lax.axis_size("wide"), lax.axis_size("narrow")
    mask = wide_mask * narrow + narrow_mask
    return lax.ppermute(x, BOTH, [(i, i ^ mask) for i in range(wide * narrow)])


def phase(*values):
    return lax.optimization_barrier(values)


def across_levels(x, stride):
    groups = [[k * stride + i for k in range(LEVELS)] for i in range(stride)]
    return lax.all_to_all(x, "wide", 0, 0, axis_index_groups=groups, tiled=True)


def swap_levels(x, k, stride):
    pairs = []
    for i in range(stride):
        pairs += [(i, k * stride + i), (k * stride + i, i)]
    return lax.ppermute(x, "wide", pairs)


def bits_of(size):
    return [1 << b for b in range(size.bit_length() - 1)]


class Place:
    def __init__(self):
        self.wide = lax.axis_size("wide")
        self.narrow = lax.axis_size("narrow")
        self.stride = self.wide // LEVELS
        self.w = lax.axis_index("wide")
        self.n = lax.axis_index("narrow")
        self.z = self.w // self.stride
        self.y = self.w % self.stride
        self.me = self.w * self.narrow + self.n


def swap_in(place, pass_part, query_part):
    query = jnp.broadcast_to(query_part, (LEVELS, *query_part.shape[1:]))
    first = jnp.concatenate([query_part, pass_part])
    return across_levels(jnp.where(place.z == 0, first, query), place.stride)


def swap_in_directly(place, pass_part, query_part):
    return [
        swap_levels(jnp.where(place.z == 0, pass_part[k - 1], query_part[0]), k, place.stride)
        for k in range(1, LEVELS)
    ]


def join_swapped(place, query_part, got):
    first = jnp.where(place.z == 0, query_part[0], got[0] + got[1] + got[2])
    return jnp.stack([first] + got)


def to_row(place, pass_part, query_part, got):
    four = jnp.where(place.z == 0, got, jnp.concatenate([pass_part, got[:1]]))
    mine = lax.all_to_all(four, "narrow", 0, 0, tiled=True)
    return mine.reshape(-1, mine.shape[-1])


def row_pieces(place, row):
    return lax.all_to_all(
        row.reshape(place.narrow, -1, row.shape[-1]), "narrow", 0, 0, tiled=True
    )


def swap_out(place, four):
    last = jnp.broadcast_to(four[3:], four.shape)
    return across_levels(jnp.where(place.z == 0, four, last), place.stride)


def from_row(place, four, got):
    pass_part = jnp.where(place.z == 0, got[1:], four[:3])
    query_part = jnp.where(place.z == 0, four[:1], got[:1])
    return pass_part, query_part


def toggle(places, mask):
    return [(p[0], p[1] ^ mask) if isinstance(p, tuple) else p ^ mask for p in places]


def block_of(me, place, level):
    if isinstance(place, tuple):
        return ((me & (level - 1)) ^ place[1]) + place[0] * level
    return me ^ place


def assemble_kernel(plan, layout, level, me_ref, *refs):
    pieces, outs, sems = refs[: len(plan)], refs[len(plan) : -1], refs[-1]
    me = me_ref[0]
    copies = []
    for piece, masks in zip(pieces, plan):
        for slot, mask in enumerate(masks):
            for out, part, row, column in layout:
                target = outs[out].at[part, block_of(me, mask, level)]
                rows, columns = outs[out].shape[2:]
                source = piece.at[slot, pl.ds(row, rows), pl.ds(column, columns)]
                copies.append(pltpu.make_async_copy(source, target, sems.at[len(copies)]))
    for copy in copies:
        copy.start()
    for copy in copies:
        copy.wait()


def assemble(place, pieces, plan, layout, outs):
    total = place.wide * place.narrow
    made = pl.pallas_call(
        functools.partial(assemble_kernel, plan, layout, total // LEVELS),
        out_shape=[jax.ShapeDtypeStruct((out[0], total, *out[1:]), BF) for out in outs],
        in_specs=[pl.BlockSpec(memory_space=pltpu.SMEM)]
        + [pl.BlockSpec(memory_space=pl.ANY)] * len(pieces),
        out_specs=[pl.BlockSpec(memory_space=pltpu.VMEM)] * len(outs),
        scratch_shapes=[pltpu.SemaphoreType.DMA((total * len(layout),))],
        cost_estimate=cost(0.1),
        compiler_params=pltpu.CompilerParams(vmem_limit_bytes=VMEM),
    )(place.me.reshape(1), *pieces)
    return [out.reshape(out.shape[0], -1, out.shape[3]) for out in made]


def pick_kernel(z_ref, w_ref, bias_ref, gain_ref, inb_ref, ints_ref, *refs):
    outs, small = refs[:-1], refs[-1]
    rows, width = w_ref.shape[1], small.shape[1]
    n_bias, n_gain = bias_ref.shape[1], gain_ref.shape[1]
    for k, out in enumerate(outs):
        tower = jnp.where(z_ref[0] == k, 1, 0)
        for part in range(3):
            out[part * rows : (part + 1) * rows] = w_ref[tower, :, part * width : (part + 1) * width]
        small[...] = jnp.zeros(small.shape, F32)
        small[:n_bias, : bias_ref.shape[2]] = bias_ref[tower].astype(F32)
        small[n_bias : n_bias + n_gain, : gain_ref.shape[2]] = gain_ref[tower].astype(F32)
        small[:1, 128 : 128 + inb_ref.shape[2]] = inb_ref[tower].astype(F32)
        small[:1, 256 : 256 + ints_ref.shape[1]] = ints_ref[...].astype(F32)
        out[3 * rows :] = small[...].astype(BF)


def pick_towers(place, w_qkv, biases, norm_gains, in_bias, ints):
    width = w_qkv.shape[2] // 3
    vmem = pl.BlockSpec(memory_space=pltpu.VMEM)
    return calls(
        pick_kernel,
        [((3 * w_qkv.shape[1] + 8, width), BF)] * LEVELS,
        2,
        in_specs=[pl.BlockSpec(memory_space=pltpu.SMEM)] + [vmem] * 5,
        scratch_shapes=[pltpu.VMEM((8, width), F32)],
    )(place.z.reshape(1), w_qkv, biases, norm_gains, in_bias[:, None], ints[None])


def gather_levels(place, pair):
    first = lax.broadcasted_iota(jnp.int32, (LEVELS, 1, 1), 0) == 0
    return across_levels(jnp.where(first, pair[1:], pair[:1]), place.stride)


def gather_columns(place, levels, own=None):
    s, narrow = place.stride, place.narrow
    if own is None:
        own = [(level, 0) for level in range(LEVELS)]
    pieces, plan = [levels], [own]
    if s == 2:
        for dx, dy in OTHERS:
            pieces.append(flip_both(levels, dy, 2 * dx))
            plan.append(toggle(own, dy * narrow + 2 * dx))
    else:
        for b in bits_of(s):
            for i in range(len(pieces)):
                pieces.append(flip(pieces[i], "wide", b))
                plan.append(toggle(plan[i], b * narrow))
        for i in range(len(pieces)):
            pieces.append(flip(pieces[i], "narrow", 2))
            plan.append(toggle(plan[i], 2))
    return pieces, plan


def gather_cores(pieces, plan):
    others = [flip(piece, "narrow", 1) for piece in pieces]
    return list(pieces) + others, plan + [toggle(places, 1) for places in plan]


def pick(x, index, dim):
    return lax.dynamic_index_in_dim(x, index, dim, keepdims=False)


def halve(x, place, axis, mask, dim):
    index = place.n if axis == "narrow" else place.w
    bit = jnp.where((index & mask) != 0, 1, 0)
    got = flip(pick(x, 1 - bit, dim).astype(BF), axis, mask)
    return pick(x, bit, dim) + got.astype(F32)


def scatter_tower(place, partial):
    s = place.stride
    rows, narrow, cols = partial.shape
    per = rows // place.wide
    x = partial.reshape(rows, 2, 2, cols)
    x = halve(x, place, "narrow", 1, 2)
    x = x.reshape(LEVELS, s, per, 2, cols)
    first, second = x[:2], x[2:]

    def over_columns(part):
        for b in reversed(bits_of(s)):
            shape = part.shape
            part = part.reshape(shape[0], 2, shape[1] // 2, *shape[2:])
            part = halve(part, place, "wide", b, 1)
        return part[:, 0]

    first = over_columns(halve(first, place, "narrow", 2, 3))
    second = halve(over_columns(second), place, "narrow", 2, 2)
    return jnp.stack(sum_levels(place, send_levels(place, jnp.concatenate([first, second]))))


def send_levels(place, levels):
    slots = [None] * LEVELS
    slots[0] = pick(levels, place.z, 0)
    for k in (3, 2, 1):
        slots[k] = flip(pick(levels, place.z ^ k, 0).astype(BF), "wide", k * place.stride)
    return slots


def sum_levels(place, slots):
    tower0 = sum(jnp.where(place.z == k, 0.0, slots[k].astype(F32)) for k in range(LEVELS))
    tower1 = sum(jnp.where(place.z == k, slots[k].astype(F32), 0.0) for k in range(LEVELS))
    return tower0, tower1


def share_kernel(at_ref, keep_ref, got_ref, own_ref, *sent_refs):
    x, y = at_ref[0], at_ref[1]

    def share(dx, dy):
        at = (x ^ dx, 0, y ^ dy)
        return keep_ref[at].astype(F32) + got_ref[at].astype(F32)

    own_ref[0] = share(0, 0)
    for ref, (dx, dy) in zip(sent_refs, OTHERS):
        ref[0] = share(dx, dy).astype(BF)


def column_shares(place, keep, got):
    r, c = got.shape[2:]
    block = pl.BlockSpec((2, 1, place.stride, r, c), lambda i, at: (0, i, 0, 0, 0))
    out = pl.BlockSpec((1, r, c), lambda i, at: (i, 0, 0))
    shape = (2, LEVELS, place.stride, r, c)
    return pl.pallas_call(
        share_kernel,
        grid_spec=pltpu.PrefetchScalarGridSpec(
            num_scalar_prefetch=1, grid=(LEVELS,), in_specs=[block] * 2, out_specs=[out] * 4
        ),
        out_shape=[jax.ShapeDtypeStruct((LEVELS, r, c), F32)]
        + [jax.ShapeDtypeStruct((LEVELS, r, c), BF)] * 3,
        compiler_params=pltpu.CompilerParams(vmem_limit_bytes=VMEM),
        cost_estimate=cost(1),
    )(jnp.stack([place.n // 2, place.y]), keep.reshape(shape), got.reshape(shape))


def send_columns(shares):
    return [shares[0]] + [
        flip_both(sent, dy, 2 * dx) for sent, (dx, dy) in zip(shares[1:], OTHERS)
    ]


def level_kernel(z_ref, own_ref, *refs):
    got_refs, (sum_ref, *sent_refs) = refs[:3], refs[3:]
    for k in range(LEVELS):
        at = z_ref[0] ^ k
        total = own_ref[at]
        for ref in got_refs:
            total = total + ref[at].astype(F32)
        if k == 0:
            sum_ref[...] = total
        else:
            sent_refs[k - 1][...] = total.astype(BF)


def level_shares(place, columns):
    r, c = columns[0].shape[1:]
    vmem = pl.BlockSpec(memory_space=pltpu.VMEM)
    return pl.pallas_call(
        level_kernel,
        in_specs=[pl.BlockSpec(memory_space=pltpu.SMEM)] + [vmem] * 4,
        out_specs=[vmem] * 4,
        out_shape=[jax.ShapeDtypeStruct((r, c), F32)] + [jax.ShapeDtypeStruct((r, c), BF)] * 3,
        compiler_params=pltpu.CompilerParams(vmem_limit_bytes=VMEM),
        cost_estimate=cost(1),
    )(place.z.reshape(1), *columns)


def level_sums_kernel(*refs):
    for at in range(LEVELS):
        refs[-1][at] = sum(ref[at].astype(F32) for ref in refs[:-1]).astype(BF)


def level_sums(columns):
    shape = columns[0].shape
    return calls(level_sums_kernel, [(shape, BF)], 3)(*columns)[0]


def swap_shares(place, shares):
    slots = [shares[0], None, None, None]
    for k in (3, 2, 1):
        slots[k] = flip(shares[k], "wide", k * place.stride)
    return slots


def product_kernel(step, me_ref, *refs):
    send_ref, keep_ref = refs[-2:]
    left_refs = refs[:-2]
    to_send = pl.program_id(0) < 2

    @pl.when(to_send)
    def _():
        step(left_refs, lambda at, v: send_ref.__setitem__((0, *at), v.astype(BF)))

    @pl.when(jnp.logical_not(to_send))
    def _():
        step(left_refs, lambda at, v: keep_ref.__setitem__((0, *at), v.astype(BF)))


def products(place, step, operands, specs, block):
    def target(j, me):
        return (j % 2) * 2 + jnp.where(j < 2, 1 - me[0] % 2, me[0] % 2)

    wide = place.wide
    grid_spec = pltpu.PrefetchScalarGridSpec(
        num_scalar_prefetch=1,
        grid=(4,),
        in_specs=specs(target),
        out_specs=[
            pl.BlockSpec((1, wide, *block), lambda j, me: (jnp.minimum(j, 1), 0, 0, 0)),
            pl.BlockSpec((1, wide, *block), lambda j, me: (jnp.maximum(j - 2, 0), 0, 0, 0)),
        ],
    )
    return pl.pallas_call(
        functools.partial(product_kernel, step),
        grid_spec=grid_spec,
        out_shape=[
            jax.ShapeDtypeStruct((2, wide, *block), BF),
            jax.ShapeDtypeStruct((2, wide, *block), BF),
        ],
        compiler_params=pltpu.CompilerParams(vmem_limit_bytes=VMEM),
        cost_estimate=cost(8),
    )(place.n.reshape(1), *operands)


def whole(shape):
    return pl.BlockSpec(shape, lambda j, me: (0,) * len(shape))


def grad_blocks(left, right, narrow):
    out = inner_rows(left, right)
    return out.reshape(out.shape[0], narrow, -1)


def products_back_kernel(core_ref, left_ref, right_ref, send_ref, keep_ref, turned_ref):
    @pl.when(pl.program_id(0) == 0)
    def _():
        turned_ref[...] = right_ref[...].T

    value = matmul(turned_ref[...], left_ref[...]).astype(BF)
    cols = send_ref.shape[2]
    first = core_ref[0] == 0
    for x in range(2):
        even = value[2 * x * cols : (2 * x + 1) * cols]
        odd = value[(2 * x + 1) * cols : (2 * x + 2) * cols]
        keep_ref[x, 0] = jnp.where(first, even, odd)
        send_ref[x, 0] = jnp.where(first, odd, even)


def products_back(place, active, grad_ffn):
    t, ff = active.shape
    d = grad_ffn.shape[1]
    cols, rows = d // place.narrow, ff // place.wide
    out = pl.BlockSpec((2, 1, cols, rows), lambda j, core: (0, j, 0, 0))
    return pl.pallas_call(
        products_back_kernel,
        grid_spec=pltpu.PrefetchScalarGridSpec(
            num_scalar_prefetch=1,
            grid=(place.wide,),
            in_specs=[pl.BlockSpec((t, rows), lambda j, core: (0, j)), whole((t, d))],
            out_specs=[out, out],
            scratch_shapes=[pltpu.VMEM((d, t), BF)],
        ),
        out_shape=[jax.ShapeDtypeStruct((2, place.wide, cols, rows), BF)] * 2,
        compiler_params=pltpu.CompilerParams(vmem_limit_bytes=VMEM),
        cost_estimate=cost(7),
    )((place.n % 2).reshape(1), active, grad_ffn)


def finish_back(levels):
    levels = levels.astype(F32)
    return jnp.stack([(levels[1] + levels[2] + levels[3]).T, levels[0].T])


def products_out_in(place, context, blocks, normed, grad_hidden):
    narrow = place.narrow
    t, d = context.shape
    rows = d // place.wide
    cols_out, cols_in = blocks.shape[2], grad_hidden.shape[1] // narrow
    fold = cols_in // cols_out
    low = rows // fold

    def step(refs, store):
        context_ref, branch_ref, normed_ref, hidden_ref = refs
        value = inner_rows(normed_ref[...], hidden_ref[...])
        for w in range(place.wide):
            store((w, slice(0, rows)), value[w * rows : (w + 1) * rows])
        value = inner_rows(context_ref[...], branch_ref[0])
        for w in range(place.wide):
            for g in range(fold):
                store(
                    (w, slice(rows, rows + low), slice(g * cols_out, (g + 1) * cols_out)),
                    value[w * rows + g * low : w * rows + (g + 1) * low],
                )

    return products(
        place,
        step,
        (context, blocks, normed, grad_hidden),
        lambda target: [
            whole((t, d)),
            pl.BlockSpec((1, t, cols_out), lambda j, me: (target(j, me), 0, 0)),
            whole((t, d)),
            pl.BlockSpec((t, cols_in), lambda j, me: (0, target(j, me))),
        ],
        (rows + low, cols_in),
    )


def finish_out_in(place, slots, rows):
    parts = sum_levels(place, slots)
    low, cols = parts[0].shape[0] - rows, parts[0].shape[1]
    fold = rows // low
    grad_in = jnp.stack([part[:rows] for part in parts])
    grad_out = [
        jnp.moveaxis(part[rows:].reshape(low, fold, -1), 1, 0).reshape(rows, -1) for part in parts
    ]
    return jnp.stack(grad_out), grad_in


def products_qkv(place, inputs, blocks):
    t, d = inputs.shape
    rows, cols = d // place.wide, blocks.shape[2]
    half = rows // 2

    def step(refs, store):
        left, right = refs
        value = inner_rows(left[...], right[0])
        for w in range(place.wide):
            for g in range(2):
                store(
                    (w, slice(None), slice(g * cols, (g + 1) * cols)),
                    value[w * rows + g * half : w * rows + (g + 1) * half],
                )

    return products(
        place,
        step,
        (inputs, blocks),
        lambda target: [
            whole((t, d)),
            pl.BlockSpec((1, t, cols), lambda j, me: (target(j, me), 0, 0)),
        ],
        (half, 2 * cols),
    )


def finish_qkv(place, slots):
    parts = sum_levels(place, slots)
    cols = parts[0].shape[1] // 2
    return jnp.stack([jnp.concatenate([p[:, :cols], p[:, cols:]]) for p in parts])


def attend_kernel(x_ref, w_ref, rows_ref, seg_row_ref, seg_col_ref, qkv_ref, ctx_ref, lse_ref):
    x = x_ref[...]
    same = seg_col_ref[...] == seg_row_ref[...]

    def project(part, carry):
        bias = jnp.where(part == 0, rows_ref[0:1], jnp.where(part == 2, rows_ref[1:2], 0.0))
        qkv_ref[part] = (matmul(x, w_ref[part]) + bias).astype(BF)
        return carry

    lax.fori_loop(0, 3, project, 0)

    def pair(p, carry):
        at = pl.ds(pl.multiple_of(p * 2 * HEAD_DIM, 2 * HEAD_DIM), 2 * HEAD_DIM)
        queries, keys, values = qkv_ref[0, :, at], qkv_ref[1, :, at], qkv_ref[2, :, at]
        contexts = []
        for h in range(2):
            lanes = slice(h * HEAD_DIM, (h + 1) * HEAD_DIM)
            q, k, v = queries[:, lanes], keys[:, lanes], values[:, lanes]
            scores = jnp.where(same, inner_cols(k, q) * HEAD_DIM ** (-0.5), MASKED)
            top = jnp.max(scores, axis=0, keepdims=True)
            shifted = jnp.exp(scores - top)
            total = jnp.sum(shifted, axis=0, keepdims=True)
            probs = (shifted * (1.0 / total)).astype(BF)
            contexts.append(inner_rows(probs, v).astype(BF))
            lse_ref[0, pl.ds(2 * p + h, 1), :] = top + jnp.log(total)
        ctx_ref[:, at] = jnp.concatenate(contexts, axis=1)
        return carry

    lax.fori_loop(0, GROUP // 2, pair, 0)


def attend(x, w_qkv, rows, segment):
    t, d = x.shape
    width = GROUP * HEAD_DIM
    steps = d // width
    return pl.pallas_call(
        attend_kernel,
        grid=(steps,),
        in_specs=[
            pl.BlockSpec((t, d), lambda j: (0, 0)),
            pl.BlockSpec((3, d, width), lambda j: (0, 0, j)),
            pl.BlockSpec((8, width), lambda j: (0, j)),
            pl.BlockSpec((1, t), lambda j: (0, 0)),
            pl.BlockSpec((t, 1), lambda j: (0, 0)),
        ],
        out_specs=[
            pl.BlockSpec((3, t, width), lambda j: (0, 0, j)),
            pl.BlockSpec((t, width), lambda j: (0, j)),
            pl.BlockSpec((1, GROUP, t), lambda j: (j, 0, 0)),
        ],
        out_shape=[
            jax.ShapeDtypeStruct((3, t, d), BF),
            jax.ShapeDtypeStruct((t, d), BF),
            jax.ShapeDtypeStruct((steps, GROUP, t), F32),
        ],
        compiler_params=pltpu.CompilerParams(vmem_limit_bytes=VMEM),
        cost_estimate=cost(0.1),
    )(x, w_qkv, rows, segment.reshape(1, t), segment.reshape(t, 1))


def attend_back_kernel(
    gb_ref, w_ref, qkv_ref, lse_ref, seg_row_ref, seg_col_ref, out_ref, blocks_ref, sums_ref, grad_ref
):
    scale = HEAD_DIM ** (-0.5)
    same = seg_col_ref[...] == seg_row_ref[...]
    grad_ref[...] = inner_cols(gb_ref[...], w_ref[...]).astype(BF)

    def pair(p, carry):
        at = pl.ds(pl.multiple_of(p * 2 * HEAD_DIM, 2 * HEAD_DIM), 2 * HEAD_DIM)
        queries, keys, values = qkv_ref[0, :, at], qkv_ref[1, :, at], qkv_ref[2, :, at]
        grads, outs = grad_ref[:, at], []
        for h in range(2):
            lanes = slice(h * HEAD_DIM, (h + 1) * HEAD_DIM)
            q, k, v, g = queries[:, lanes], keys[:, lanes], values[:, lanes], grads[:, lanes]
            scores = jnp.where(same, inner_cols(k, q) * scale, MASKED)
            probs = jnp.exp(scores - lse_ref[0, pl.ds(2 * p + h, 1), :])
            grad_probs = inner_cols(v, g)
            delta = jnp.sum(probs * grad_probs, axis=0, keepdims=True)
            grad_scores = (probs * (grad_probs - delta)).astype(BF)
            outs.append(
                (
                    (inner_rows(grad_scores, k) * scale).astype(BF),
                    (matmul(grad_scores, q) * scale).astype(BF),
                    matmul(probs.astype(BF), g).astype(BF),
                )
            )
        for part in range(3):
            out_ref[part, :, at] = jnp.concatenate([outs[0][part], outs[1][part]], axis=1)
        return carry

    lax.fori_loop(0, GROUP // 2, pair, 0)
    sums_ref[0:1] = jnp.sum(out_ref[0].astype(F32), axis=0, keepdims=True)
    sums_ref[1:2] = jnp.sum(out_ref[2].astype(F32), axis=0, keepdims=True)
    per_block = blocks_ref.shape[2] // HEAD_DIM
    heads = blocks_ref.shape[0] * per_block // 3
    for step in range(heads // GROUP):

        @pl.when(pl.program_id(0) == step)
        def _(step=step):
            for part in range(3):
                for h in range(GROUP):
                    block, at = divmod(part * heads + step * GROUP + h, per_block)
                    blocks_ref[block, :, at * HEAD_DIM : (at + 1) * HEAD_DIM] = out_ref[
                        part, :, h * HEAD_DIM : (h + 1) * HEAD_DIM
                    ]


def attend_back(grad_branch, w_out, qkv, lse, segment, narrow):
    t, d = grad_branch.shape
    width = GROUP * HEAD_DIM
    return pl.pallas_call(
        attend_back_kernel,
        grid=(d // width,),
        in_specs=[
            pl.BlockSpec((t, d), lambda j: (0, 0)),
            pl.BlockSpec((width, d), lambda j: (j, 0)),
            pl.BlockSpec((3, t, width), lambda j: (0, 0, j)),
            pl.BlockSpec((1, GROUP, t), lambda j: (j, 0, 0)),
            pl.BlockSpec((1, t), lambda j: (0, 0)),
            pl.BlockSpec((t, 1), lambda j: (0, 0)),
        ],
        out_specs=[
            pl.BlockSpec((3, t, width), lambda j: (0, 0, j)),
            pl.BlockSpec((narrow, t, 3 * d // narrow), lambda j: (0, 0, 0)),
            pl.BlockSpec((2, width), lambda j: (0, j)),
        ],
        out_shape=[
            jax.ShapeDtypeStruct((3, t, d), BF),
            jax.ShapeDtypeStruct((narrow, t, 3 * d // narrow), BF),
            jax.ShapeDtypeStruct((2, d), F32),
        ],
        scratch_shapes=[pltpu.VMEM((t, width), BF)],
        compiler_params=pltpu.CompilerParams(vmem_limit_bytes=VMEM),
        cost_estimate=cost(20),
    )(grad_branch, w_out, qkv, lse, segment.reshape(1, t), segment.reshape(t, 1))


def hidden_kernel(x_ref, w_ref, bias_ref, active_ref, slope_ref, pre_ref):
    pre_ref[...] = matmul(x_ref[...], w_ref[0]) + bias_ref[...]

    def body(at, carry):
        pre = pre_ref[at]
        below = 0.5 + 0.5 * lax.erf(pre * 0.5**0.5)
        active_ref[at] = (pre * below).astype(BF)
        density = jnp.exp(-0.5 * pre * pre) * (2.0 * math.pi) ** (-0.5)
        slope_ref[at] = (below + pre * density).astype(BF)
        return carry

    by_rows(pre_ref.shape[0], body)


def hidden_layer(x, w_in, in_bias):
    t, d = x.shape
    parts, _, width = w_in.shape
    block = pl.BlockSpec((t, width), lambda j: (0, j))
    shape = jax.ShapeDtypeStruct((t, parts * width), BF)
    return pl.pallas_call(
        hidden_kernel,
        grid=(parts,),
        in_specs=[
            pl.BlockSpec((t, d), lambda j: (0, 0)),
            pl.BlockSpec((1, d, width), lambda j: (j, 0, 0)),
            pl.BlockSpec((1, width), lambda j: (0, j)),
        ],
        out_specs=[block, block],
        out_shape=[shape, shape],
        scratch_shapes=[pltpu.VMEM((t, width), F32)],
        compiler_params=pltpu.CompilerParams(vmem_limit_bytes=VMEM),
        cost_estimate=cost(8),
    )(x, w_in, in_bias)


def norm_parts(value):
    mean = jnp.mean(value, axis=-1, keepdims=True)
    centered = value - mean
    scale = lax.rsqrt(jnp.mean(centered * centered, axis=-1, keepdims=True) + EPSILON)
    return centered * scale, scale


def norm_back(grad, unit, scale, gain):
    e = grad * gain
    part = jnp.mean(e * unit, axis=-1, keepdims=True)
    return (e - jnp.mean(e, axis=-1, keepdims=True) - unit * part) * scale


def total(value):
    return jnp.sum(jnp.sum(value, axis=0, keepdims=True), axis=1, keepdims=True)


def column_sum(value):
    return jnp.sum(value, axis=0, keepdims=True)


def by_rows(count, body, carry=None):
    if carry is None:
        carry = jnp.zeros((1, 128), F32)
    return lax.fori_loop(
        0, count // STEP, lambda i, c: body(pl.ds(pl.multiple_of(i * STEP, STEP), STEP), c), carry
    )


def store_blocks(ref, at, value):
    count, _, width = ref.shape
    for i in range(count):
        ref[i, at] = value[:, i * width : (i + 1) * width]


def calls(kernel, outs, us, **kwargs):
    return pl.pallas_call(
        kernel,
        out_shape=[jax.ShapeDtypeStruct(shape, dtype) for shape, dtype in outs],
        compiler_params=pltpu.CompilerParams(vmem_limit_bytes=VMEM),
        cost_estimate=cost(us),
        **kwargs,
    )


def branch_kernel(ctx, w, x, rows, valid, normed, low, unit, scale, stats, acc):
    acc[...] = matmul(ctx[...], w[0])
    zero = jnp.zeros((1, acc.shape[1]), F32)

    def body(at, sums):
        branch = acc[at] + rows[2:3]
        residual = x[at].astype(F32) + branch
        unit[at], scale[at] = norm_parts(residual)
        normed[at] = unit[at] * rows[6:7] + rows[3:4]
        low[at] = normed[at].astype(BF)
        return tuple(
            s + column_sum(valid[at] * value * value) for s, value in zip(sums, (residual, branch))
        )

    for i, value in enumerate(by_rows(acc.shape[0], body, (zero, zero))):
        stats[i : i + 1] = jnp.broadcast_to(total(value), (1, 128))


def branch_layer(context, w_out, inputs, rows, valid):
    t, d = inputs.shape
    outs = [((t, d), F32), ((t, d), BF), ((t, d), F32), ((t, 1), F32), ((2, 128), F32)]
    scratch = [pltpu.VMEM((t, d), F32)]
    return calls(branch_kernel, outs, 5, scratch_shapes=scratch)(
        context, w_out, inputs, rows, valid
    )


def output_kernel(plan, level, me_ref, active, normed, rows, valid, hot, *refs):
    pieces = refs[:-8]
    low, unit, scale, pooled, stats, w, acc, sems = refs[-8:]
    step = pl.program_id(0)
    width = active.shape[1]
    block = pieces[0].shape[1]

    @pl.when(step == 0)
    def _():
        copies = []
        if plan is None:
            copies.append(pltpu.make_async_copy(pieces[0], w, sems.at[0]))
        for piece, masks in zip(pieces, plan or []):
            for slot, mask in enumerate(masks):
                at = pl.multiple_of(block_of(me_ref[0], mask, level) * block, block)
                target = w.at[pl.ds(at, block)]
                copies.append(
                    pltpu.make_async_copy(piece.at[slot], target, sems.at[len(copies)])
                )
        for copy in copies:
            copy.start()
        for copy in copies:
            copy.wait()

    product = matmul(active[...], w[pl.ds(pl.multiple_of(step * width, width), width)])

    @pl.when(step == 0)
    def _():
        acc[...] = product

    @pl.when(step > 0)
    def _():
        acc[...] += product

    @pl.when(step == pl.num_programs(0) - 1)
    def _():
        zero = jnp.zeros((1, acc.shape[1]), F32)

        def body(at, sums):
            ffn_out = acc[at] + rows[4:5]
            residual = normed[at] + ffn_out
            unit[at], scale[at] = norm_parts(residual)
            low[at] = (unit[at] * rows[7:8] + rows[5:6]).astype(BF)
            values = (valid[at] * residual * residual, valid[at] * ffn_out * ffn_out)
            return tuple(s + column_sum(value) for s, value in zip(sums, values))

        sums = by_rows(acc.shape[0], body, (zero, zero))
        for i, value in enumerate((*sums, valid[...])):
            stats[i : i + 1] = jnp.broadcast_to(total(value), (1, 128))
        pooled[...] = matmul(hot[...].astype(BF), low[...]).astype(BF)


def all_of(shape):
    return pl.BlockSpec(shape, lambda j: (0,) * len(shape))


def output_layer(place, active, pieces, plan, normed, rows, valid, hot):
    t, ff = active.shape
    d = normed.shape[1]
    outs = [((t, d), BF), ((t, d), F32), ((t, 1), F32), ((hot.shape[0], d), BF), ((3, 128), F32)]
    outs.append(((ff, d), BF))
    return calls(
        functools.partial(output_kernel, plan, place.wide * place.narrow // LEVELS),
        outs,
        9,
        grid=(ff // d,),
        in_specs=[pl.BlockSpec(memory_space=pltpu.SMEM), pl.BlockSpec((t, d), lambda j: (0, j))]
        + [all_of(a.shape) for a in (normed, rows, valid, hot)]
        + [pl.BlockSpec(memory_space=pl.ANY)] * len(pieces),
        out_specs=[all_of(shape) for shape, _ in outs],
        scratch_shapes=[
            pltpu.VMEM((t, d), F32),
            pltpu.SemaphoreType.DMA((place.wide * place.narrow,)),
        ],
    )(place.me.reshape(1), active, normed, rows, valid, hot, *pieces)


def output_back_kernel(cot, valid, hot, pool, unit, scale, rows, grad, low, sums):
    zero = jnp.zeros((1, grad.shape[1]), F32)

    def body(at, totals):
        grad_out = cot[at].astype(F32) * valid[at] + lax.dot_general(
            hot[:, at],
            pool[...],
            (((0,), (0,)), ((), ())),
            precision=lax.Precision.HIGHEST,
            preferred_element_type=F32,
        )
        grad[at] = norm_back(grad_out, unit[at], scale[at], rows[7:8])
        low[at] = grad[at].astype(BF)
        values = (grad_out * unit[at], grad_out, low[at].astype(F32))
        return tuple(t + column_sum(value) for t, value in zip(totals, values))

    for i, value in enumerate(by_rows(grad.shape[0], body, (zero,) * 3)):
        sums[i : i + 1] = value


def output_back(cot, valid, hot, pool, unit, scale, rows):
    t, d = cot.shape
    outs = [((t, d), F32), ((t, d), BF), ((3, d), F32)]
    return calls(output_back_kernel, outs, 6)(cot, valid, hot, pool, unit, scale, rows)


def hidden_back_kernel(
    low, w_back, slope, w_in, grad, unit, scale, rows, hidden, inb, residual, branch, blocks, sums, acc
):
    step = pl.program_id(0)
    product = inner_cols(low[...], w_back[...])
    hidden[...] = (product * slope[...].astype(F32)).astype(BF)
    inb[...] = column_sum(hidden[...].astype(F32))
    product = inner_cols(hidden[...], w_in[0])

    @pl.when(step == 0)
    def _():
        acc[...] = grad[...] + product

    @pl.when(step > 0)
    def _():
        acc[...] += product

    @pl.when(step == pl.num_programs(0) - 1)
    def _():
        zero = jnp.zeros((1, acc.shape[1]), F32)

        def body(at, totals):
            value = acc[at]
            residual[at] = norm_back(value, unit[at], scale[at], rows[6:7])
            branch[at] = residual[at].astype(BF)
            store_blocks(blocks, at, branch[at])
            values = (value * unit[at], value, branch[at].astype(F32))
            return tuple(t + column_sum(value) for t, value in zip(totals, values))

        for i, value in enumerate(by_rows(acc.shape[0], body, (zero,) * 3)):
            sums[i : i + 1] = value


def hidden_back(low, w_back, slope, w_in, grad, unit, scale, rows, narrow):
    t, d = low.shape
    ff = slope.shape[1]
    tile = pl.BlockSpec((t, d), lambda j: (0, j))
    outs = [
        ((t, ff), BF),
        ((1, ff), F32),
        ((t, d), F32),
        ((t, d), BF),
        ((narrow, t, d // narrow), BF),
        ((3, d), F32),
    ]
    return calls(
        hidden_back_kernel,
        outs,
        14,
        grid=(ff // d,),
        in_specs=[
            all_of(low.shape),
            pl.BlockSpec((d, d), lambda j: (j, 0)),
            tile,
            pl.BlockSpec((1, d, d), lambda j: (j, 0, 0)),
        ]
        + [all_of(a.shape) for a in (grad, unit, scale, rows)],
        out_specs=[tile, pl.BlockSpec((1, d), lambda j: (0, j))]
        + [all_of(shape) for shape, _ in outs[2:]],
        scratch_shapes=[pltpu.VMEM((t, d), F32)],
    )(low, w_back, slope, w_in, grad, unit, scale, rows)


def input_back_kernel(grad, w, residual, out, acc):
    step = pl.program_id(0)
    product = inner_cols(grad[0], w[0])

    @pl.when(step == 0)
    def _():
        acc[...] = residual[...] + product

    @pl.when(step == 1)
    def _():
        acc[...] += product

    @pl.when(step == 2)
    def _():
        out[...] = (acc[...] + product).astype(BF)


def input_back(grad_qkv, w_qkv, residual):
    _, t, d = grad_qkv.shape
    return calls(
        input_back_kernel,
        [((t, d), BF)],
        6,
        grid=(3,),
        in_specs=[
            pl.BlockSpec((1, t, d), lambda j: (j, 0, 0)),
            pl.BlockSpec((1, d, d), lambda j: (j, 0, 0)),
            all_of((t, d)),
        ],
        out_specs=[all_of((t, d))],
        scratch_shapes=[pltpu.VMEM((t, d), F32)],
    )(grad_qkv, w_qkv, residual)[0]


def spread_masks(count, width):
    total_cols = count * width
    column = lax.broadcasted_iota(jnp.int32, (count, total_cols), 1)
    first = lax.broadcasted_iota(jnp.int32, (count, total_cols), 0) * width
    own = (column >= first) & (column < first + width)
    owner = jnp.sum(jnp.where(own, first, 0), axis=0, keepdims=True)
    within = lax.broadcasted_iota(jnp.int32, (width, total_cols), 1) - owner
    spread = within == lax.broadcasted_iota(jnp.int32, (width, total_cols), 0)
    return own, spread.astype(F32)


def unpack_kernel(small, rows, inb):
    count = small.shape[0]
    value = small[...].astype(F32)

    def unpack(part, masks):
        own, spread = masks
        placed = matmul(part.astype(BF), spread.astype(BF))
        return column_sum(jnp.where(own, placed, 0.0))

    width = rows.shape[1] // count
    masks = spread_masks(count, width)
    for r in range(8):
        rows[r : r + 1] = unpack(value[:, r, :width], masks)
    width = inb.shape[1] // count
    inb[...] = unpack(value[:, 0, 128 : 128 + width], spread_masks(count, width))


def unpack_params(small, d, ff):
    return calls(unpack_kernel, [((8, d), F32), ((1, ff), F32)], 0.1)(small)


def pack_kernel(attn, out, ffn, inb, stats_a, stats_b, packed, rows, parts):
    count = packed.shape[0]
    vectors = (attn[0:1], attn[1:2], out[2:3], out[1:2], ffn[2:3], ffn[1:2], out[0:1], ffn[0:1])

    def pack(vector, own, spread):
        return lax.dot_general(
            jnp.where(own, vector, 0.0),
            spread,
            (((1,), (1,)), ((), ())),
            precision=lax.Precision.HIGHEST,
            preferred_element_type=F32,
        )

    for i, vector in enumerate(vectors):
        rows[i : i + 1] = vector
    packed[...] = jnp.zeros(packed.shape, F32)
    width = rows.shape[1] // count
    masks = spread_masks(count, width)

    def body(i, carry):
        parts[i] = pack(rows[pl.ds(i, 1)], *masks)
        return carry

    lax.fori_loop(0, len(vectors), body, 0)
    for i in range(len(vectors)):
        packed[:, i * width : (i + 1) * width] = parts[i]
    at = len(vectors) * width
    width = inb.shape[1] // count
    packed[:, at : at + width] = pack(inb[...], *spread_masks(count, width))
    at += width
    for i, row in enumerate((stats_a[0:1], stats_a[1:2], stats_b[0:1], stats_b[1:2], stats_b[2:3])):
        packed[:, at + i : at + i + 1] = jnp.broadcast_to(row[:, :1], (count, 1))


def pack_sums(count, attn, out, ffn, inb, stats_a, stats_b):
    width = attn.shape[1]
    scratch = [pltpu.VMEM((8, width), F32), pltpu.VMEM((8, count, width // count), F32)]
    return calls(pack_kernel, [((count, 384), F32)], 4, scratch_shapes=scratch)(
        attn, out, ffn, inb, stats_a, stats_b
    )[0]


def match_grads(rows, label_rows, label_cols):
    is_query, is_pass = label_rows >= 0, label_cols >= 0
    match = jnp.where(is_pass, inner_cols(rows, rows) / SCORE_DIV, MASKED)
    shifted = jnp.exp(match - jnp.max(match, axis=1, keepdims=True))
    probs = shifted / jnp.sum(shifted, axis=1, keepdims=True)
    hot = (label_rows == label_cols).astype(F32)
    grad = jnp.where(is_query & is_pass, (probs - hot) / SCORE_DIV, 0.0).astype(BF)
    return matmul(grad[:POOL], rows) + inner_rows(grad[:, :POOL], rows)


def match_kernel(rows, label_rows, label_cols, out):
    out[...] = match_grads(rows[...], label_rows[...], label_cols[...])


def row_of(z, y, n, s):
    own = (z * s + y) * 3 + n
    spare = y * 3 + (z - 1)
    return jnp.where(z == 0, n * s + y, jnp.where(n < 3, own, spare))


def body(
    passages,
    queries,
    passage_cot,
    query_cot,
    passage_lengths,
    query_lengths,
    labels,
    w_qkv,
    w_out,
    w_in,
    w_back,
    biases,
    norm_gains,
    in_bias,
):
    place = Place()
    s, narrow, devices = place.stride, place.narrow, place.wide * place.narrow
    model_width = passages.shape[2]
    length = passages.shape[1] * narrow
    segs, qsegs = passage_lengths.shape[1] - 1, query_lengths.shape[1] - 1
    on_query = place.z == 0

    piece = model_width // devices
    whole = jnp.concatenate(
        [passage_lengths.reshape(-1), query_lengths.reshape(-1), labels.reshape(-1)]
    )
    whole = jnp.concatenate([whole // 32, whole % 32]).astype(BF)

    w_rows, in_parts = w_out.shape[1], w_in.shape[2] // w_out.shape[2]
    swapped = swap_in_directly(place, passages, queries)
    if s == 2:
        swapped[0], w_qkv = phase(swapped[0], w_qkv)
        towers = pick_towers(place, w_qkv, biases, norm_gains, in_bias, whole)
        got = {k: flip(towers[k], "wide", k * s) for k in (3, 2, 1)}
        levels_qkv = jnp.stack([towers[0], got[1], got[2], got[3]])
        own = [k * s * narrow for k in range(LEVELS)]
        layout = [(0, part, part * w_rows, 0) for part in range(3)] + [(1, 0, 3 * w_rows, 0)]
        shapes = [(3, w_rows, model_width), (1, 8, model_width)]
    else:
        small = jnp.concatenate(
            [biases.reshape(2, -1), norm_gains.reshape(2, -1), in_bias.reshape(2, -1)], axis=1
        )
        small_count = small.shape[1]
        small = jnp.concatenate([small, jnp.broadcast_to(whole, (2, whole.shape[0]))], axis=1)
        to_query = (jnp.arange(devices) < s * narrow)[:, None]
        small = lax.all_to_all(
            jnp.where(to_query, small[1][None], small[0][None]), BOTH, 0, 0, tiled=True
        )
        levels_qkv, own = gather_levels(place, w_qkv), None
        layout = [(0, part, 0, part * model_width) for part in range(3)]
        shapes = [(3, w_rows, model_width)]
    out_in = jnp.concatenate([w_out, w_in], axis=2)
    levels_qkv, swapped, out_in = phase(levels_qkv, swapped, out_in)

    pieces_qkv, plan = gather_columns(place, levels_qkv, own)
    levels_out_in = gather_levels(place, out_in)
    pieces_qkv, levels_out_in, w_back = phase(pieces_qkv, levels_out_in, w_back)

    cores_qkv, core_plan = gather_cores(pieces_qkv, plan)
    cores_qkv, levels_out_in, swapped = phase(cores_qkv, levels_out_in, swapped)

    pieces_out_in, plan = gather_columns(place, levels_out_in)
    inputs = to_row(place, passages, queries, join_swapped(place, queries, swapped))
    inputs, w_back = phase(inputs, w_back)
    levels_back = gather_levels(place, w_back)
    made = assemble(place, cores_qkv, core_plan, layout, shapes)
    w_qkv_all = made[0]

    n_bias, n_gain = biases.shape[1], norm_gains.shape[1]
    ff = in_bias.shape[1] * devices
    if s == 2:
        small = made[1].reshape(devices, 8, -1)
        rows, inb_row = unpack_params(small, model_width, ff)
        ints = small[:, 0, 256 : 256 + whole.shape[0]].astype(F32)
    else:
        params = small[:, :small_count].astype(F32)
        vectors = params[:, : (n_bias + n_gain) * piece].reshape(devices, n_bias + n_gain, piece)
        rows = vectors.transpose(1, 0, 2).reshape(n_bias + n_gain, -1)
        inb_row = params[:, (n_bias + n_gain) * piece :].reshape(1, -1)
        ints = small[:, small_count : small_count + whole.shape[0]].astype(F32)
    half = ints.shape[1] // 2
    ints = (ints[::narrow, :half] * 32 + ints[::narrow, half:]).astype(jnp.int32)
    n_pass = passage_lengths.size
    n_query = query_lengths.size
    pass_lens = ints[:, :n_pass].reshape(-1, segs + 1)
    query_lens = ints[:, n_pass : n_pass + n_query].reshape(-1, qsegs + 1)
    label_all = ints[:, n_pass + n_query :].reshape(-1, qsegs)
    my_row = row_of(place.z, place.y, place.n, s)
    pass_row = pick(pass_lens, jnp.where(on_query, 0, my_row), 0)
    query_row = pick(query_lens, jnp.where(on_query, my_row, 0), 0)
    ends_p = jnp.cumsum(pass_row)[:-1]
    ends_q = jnp.cumsum(query_row)[:-1]
    starts_p, starts_q = ends_p - pass_row[:-1], ends_q - query_row[:-1]
    ends_p = jnp.concatenate([ends_p, jnp.full((qsegs - segs,), length + 1, jnp.int32)])
    ends = jnp.where(on_query, ends_q, ends_p)
    seg_count = jnp.where(on_query, qsegs, segs)
    position = jnp.arange(length, dtype=jnp.int32)
    segment = jnp.sum((position[:, None] >= ends[None, :]).astype(jnp.int32), axis=1)
    valid = (segment < seg_count).astype(F32)[:, None]
    slot = jnp.arange(POOL)
    starts = jnp.where(on_query, jnp.concatenate([starts_q, jnp.full((qsegs,), -1)]), -1)
    for z in range(1, LEVELS):
        here = (place.z == z) & (slot >= qsegs + segs * (z - 1)) & (slot < qsegs + segs * z)
        starts = jnp.where(here, jnp.tile(starts_p, POOL // segs), starts)
    hot = (starts[:, None] == position[None, :]).astype(F32)
    masks = [0]
    if s == 2:
        masks += [dy * narrow + 2 * dx for dx, dy in OTHERS]
        masks += [m ^ 1 for m in masks]
    else:
        for mask in [b * narrow for b in bits_of(s)] + [b for b in reversed(bits_of(narrow))]:
            masks = masks + [m ^ mask for m in masks]
    there = (place.y * narrow + place.n) ^ jnp.array(masks, jnp.int32)
    their_y, their_n = there // narrow, there % narrow
    label_rows = label_all[row_of(jnp.int32(0), their_y, their_n, s)]
    label_rows = jnp.pad(label_rows, ((0, 0), (0, POOL - qsegs)), constant_values=-1)
    levels = jnp.arange(1, LEVELS)
    pass_rows = row_of(levels[None, :], their_y[:, None], their_n[:, None], s)
    pass_ids = (pass_rows[:, :, None] * segs + jnp.arange(segs)).reshape(len(masks), -1)
    spare = POOL - qsegs - pass_ids.shape[1]
    label_cols = jnp.pad(pass_ids, ((0, 0), (qsegs, spare)), constant_values=-1)
    label_rows, label_cols = label_rows.reshape(-1, 1), label_cols.reshape(1, -1)

    qkv, context, log_sum = attend(inputs, w_qkv_all, rows, segment)
    context, pieces_out_in, levels_back, cots = phase(
        context, pieces_out_in, levels_back, (passage_cot, query_cot)
    )

    cores_out_in, core_plan = gather_cores(pieces_out_in, plan)
    cores_out_in, levels_back, cots = phase(cores_out_in, levels_back, cots)

    pieces_back, plan = gather_columns(place, levels_back)
    swapped = swap_in(place, *cots)
    w_out_all, w_in_all = assemble(
        place,
        cores_out_in,
        core_plan,
        [(0, 0, 0, 0)] + [(1, part, 0, (part + 1) * model_width) for part in range(in_parts)],
        [(1, w_rows, model_width), (in_parts, w_rows, model_width)],
    )
    normed, normed_low, unit_one, scale_one, stats_one = branch_layer(
        context, w_out_all, inputs, rows, valid
    )
    active, slope = hidden_layer(normed_low, w_in_all, inb_row)
    active, pieces_back, swapped = phase(active, pieces_back, swapped)

    cores_back, core_plan = gather_cores(pieces_back, plan)
    cot = to_row(place, passage_cot, query_cot, swapped)
    if s != 2:
        back_shape = [(1, w_back.shape[1], model_width)]
        cores_back = assemble(place, cores_back, core_plan, [(0, 0, 0, 0)], back_shape)
        cores_back, core_plan = [cores_back[0][0]], None
    output_low, unit_two, scale_two, pooled, stats_two, w_back_all = output_layer(
        place, active, cores_back, core_plan, normed, rows, valid, hot
    )
    pooled, cot = phase(pooled, cot)

    column = sum([flip(pooled, "wide", k * s).astype(F32) for k in (3, 2, 1)], pooled.astype(F32))
    seen = column.astype(BF)[None]
    if s == 2:
        seen = jnp.concatenate([seen] + [flip_both(seen, dy, 2 * dx) for dx, dy in OTHERS])
        seen = jnp.concatenate([seen, flip(seen, "narrow", 1)])
    else:
        for axis, step in [("wide", b) for b in bits_of(s)] + [
            ("narrow", b) for b in reversed(bits_of(narrow))
        ]:
            seen = jnp.concatenate([seen, flip(seen, axis, step)])
    seen = seen.reshape(-1, model_width)
    if s == 2:
        (grad_pool,) = calls(match_kernel, [((POOL, model_width), F32)], 3)(
            seen, label_rows, label_cols
        )
    else:
        grad_pool = match_grads(seen, label_rows, label_cols)

    grad_pool, output_low = phase(grad_pool, output_low)
    if s == 2:
        out_four = row_pieces(place, output_low)
    grad_resid_two, grad_ffn, sums_two = output_back(
        cot, valid, hot, grad_pool, unit_two, scale_two, rows
    )
    if s == 2:
        send_c, keep_c = products_back(place, active, grad_ffn)
        send_c, out_four = phase(send_c, out_four)
        got_c = flip(send_c, "narrow", 1)
        shares_c = column_shares(place, keep_c, got_c)
        shares_c, grad_ffn = phase(shares_c, grad_ffn)

        columns_c = send_columns(shares_c)
        swapped = swap_out(place, out_four)
    grad_hidden, inb_sums, grad_residual, grad_branch, blocks_b, sums_one = hidden_back(
        grad_ffn, w_back_all, slope, w_in_all, grad_resid_two, unit_one, scale_one, rows, narrow
    )
    if s == 2:
        send_b, keep_b = products_out_in(place, context, blocks_b, normed_low, grad_hidden)
        send_b, columns_c, swapped = phase(send_b, columns_c, swapped)
        passage_out, query_out = from_row(place, out_four, swapped)

        got_b = flip(send_b, "narrow", 1)
        level_c = level_sums(columns_c)
        shares_b = column_shares(place, keep_b, got_b)
        shares_b, level_c, grad_branch = phase(shares_b, level_c, grad_branch)

        columns_b = send_columns(shares_b)
        levels_c = across_levels(level_c, s)
    grad_qkv, blocks_a, sums_qkv = attend_back(
        grad_branch, w_out_all[0], qkv, log_sum, segment, narrow
    )
    if s == 2:
        send_a, keep_a = products_qkv(place, inputs, blocks_a)
        send_a, grad_qkv, columns_b, levels_c = phase(send_a, grad_qkv, columns_b, levels_c)

        got_a = flip(send_a, "narrow", 1)
    input_grad = input_back(grad_qkv, w_qkv_all, grad_residual)
    if s == 2:
        got_a, input_grad, columns_b = phase(got_a, input_grad, columns_b)

        in_four = row_pieces(place, input_grad)
        levels_b = swap_shares(place, level_shares(place, columns_b))
        shares_a = column_shares(place, keep_a, got_a)
        shares_a, levels_b, in_four, sums_qkv, levels_c = phase(
            shares_a, levels_b, in_four, sums_qkv, levels_c
        )

        columns_a = send_columns(shares_a)
        swapped = swap_out(place, in_four)
        packed = pack_sums(devices, sums_qkv, sums_one, sums_two, inb_sums, stats_one, stats_two)
        grad_w_back = finish_back(levels_c)
        columns_a, swapped, packed = phase(columns_a, swapped, packed)

        packed = lax.all_to_all(packed, BOTH, 0, 0, tiled=True)
        levels_a = swap_shares(place, level_shares(place, columns_a))
        grad_w_out, grad_w_in = finish_out_in(place, levels_b, model_width // place.wide)
        passage_grad, query_grad = from_row(place, in_four, swapped)
        grad_w_qkv = finish_qkv(place, levels_a)
    else:
        packed = pack_sums(devices, sums_qkv, sums_one, sums_two, inb_sums, stats_one, stats_two)
        packed = lax.all_to_all(packed, BOTH, 0, 0, tiled=True)
        grad_w_back = scatter_tower(place, grad_blocks(active, grad_ffn, narrow))
        grad_w_out = scatter_tower(place, grad_blocks(context, grad_branch, narrow))
        grad_w_in = scatter_tower(place, grad_blocks(normed_low, grad_hidden, narrow))
        flat = jnp.moveaxis(grad_qkv, 0, 1).reshape(length, -1)
        grad_w_qkv = scatter_tower(place, grad_blocks(inputs, flat, narrow))
        out_four, in_four = row_pieces(place, output_low), row_pieces(place, input_grad)
        passage_out, query_out = from_row(place, out_four, swap_out(place, out_four))
        passage_grad, query_grad = from_row(place, in_four, swap_out(place, in_four))

    packed = packed.reshape(LEVELS, -1, packed.shape[1]).sum(axis=1)
    packed = jnp.stack([packed[1] + packed[2] + packed[3], packed[0]])
    edges = [n_bias * piece, (n_bias + n_gain) * piece]
    edges.append(edges[1] + in_bias.shape[1])
    grad_biases = packed[:, : edges[0]].reshape(2, n_bias, piece)
    grad_gains = packed[:, edges[0] : edges[1]].reshape(2, n_gain, piece)
    grad_inb = packed[:, edges[1] : edges[2]]
    totals = packed[:, edges[2] : edges[2] + 5]
    rms_stats = jnp.sqrt(totals[:, :4] / (totals[:, 4:] * model_width))
    return (
        passage_out,
        query_out,
        passage_grad,
        query_grad,
        grad_w_qkv,
        grad_w_out,
        grad_w_in,
        grad_w_back,
        grad_biases,
        grad_gains,
        grad_inb,
        rms_stats,
    )


def solution(mesh):
    return jax.shard_map(
        body,
        mesh=mesh,
        in_specs=(
            P("wide", "narrow", None),
            P("wide", "narrow", None),
            P("wide", "narrow", None),
            P("wide", "narrow", None),
            P("wide", None),
            P("wide", None),
            P("wide"),
            P(None, ("wide", "narrow"), None),
            P(None, ("wide", "narrow"), None),
            P(None, ("wide", "narrow"), None),
            P(None, ("wide", "narrow"), None),
            P(None, None, ("wide", "narrow")),
            P(None, None, ("wide", "narrow")),
            P(None, ("wide", "narrow")),
        ),
        out_specs=(
            P("wide", "narrow", None),
            P("wide", "narrow", None),
            P("wide", "narrow", None),
            P("wide", "narrow", None),
            P(None, "wide", "narrow"),
            P(None, "wide", "narrow"),
            P(None, "wide", "narrow"),
            P(None, "wide", "narrow"),
            P(None, None, ("wide", "narrow")),
            P(None, None, ("wide", "narrow")),
            P(None, ("wide", "narrow")),
            P(),
        ),
        check_vma=False,
    )
```

profile of v0, /device:TPU:0, one launch (start us, length us, event | category | flops | bytes accessed | tf_op | source)
XLA Modules:
  0.0 386.5 jit_solution(2992285949543626191)
XLA Ops:
  1.9 4.9 %collective-permute-start = (bf16[128,768]{1,0:T(8,128)(2,1)S(1)}, bf16[128,768]{1,0:T(8,128)(2,1)S(1)}, u32[]{:S(2)}, u32[]{:S(2)}) collective-permute-start(bf16[128,768]{1,0:T(8,128)(2,1)S(1)} %get-tuple-element.403), channel_id=1, source_target_pairs={{0,8},{8,0},{4,12},{12,4},{1,9},{9,1},{5,13},{13,5},{2,10},{10,2},... | collective-permute-start | bytes 589832 | tf_op jit(solution)/shard_map/ppermute | solution.py:68
  17.2 3.8 collective-permute-start.3
  21.6 3.9 %collective-permute-done.3 = bf16[80,768]{1,0:T(8,128)(2,1)S(1)} collective-permute-done((bf16[80,768]{1,0:T(8,128)(2,1)}, bf16[80,768]{1,0:T(8,128)(2,1)S(1)}, u32[]{:S(2)}, u32[]{:S(2)}) %collective-permute-start.3) | collective-permute-done | bytes 122912 | tf_op jit(solution)/shard_map/ppermute | solution.py:46
  25.5 5.3 %collective-permute-done.2 = bf16[80,768]{1,0:T(8,128)(2,1)S(1)} collective-permute-done((bf16[80,768]{1,0:T(8,128)(2,1)}, bf16[80,768]{1,0:T(8,128)(2,1)S(1)}, u32[]{:S(2)}, u32[]{:S(2)}) %collective-permute-start.2) | collective-permute-done | bytes 122912 | tf_op jit(solution)/shard_map/ppermute | solution.py:46
  32.8 4.7 %all-to-all-start = ((bf16[4,24,3840]{2,1,0:T(8,128)(2,1)}), bf16[4,24,3840]{2,1,0:T(8,128)(2,1)S(1)}, u32[]{:S(2)}, u32[]{:S(2)}) async-start(bf16[4,24,3840]{2,1,0:T(8,128)(2,1)} %broadcast_select_fusion.2), calls=%async_computation | async-start | bytes 1474560 | tf_op jit(solution)/shard_map/all_to_all | solution.py:61
  37.6 2.4 collective-permute-start.6
  41.1 11.6 %collective-permute-done.6.refs_1_ = bf16[4,80,768]{2,1,0:T(8,128)(2,1)S(1)} collective-permute-done((bf16[4,80,768]{2,1,0:T(8,128)(2,1)S(1)}, bf16[4,80,768]{2,1,0:T(8,128)(2,1)S(1)}, u32[]{:S(2)}, u32[]{:S(2)}) %collective-permute-start.6) | collective-permute-done | bytes 491552 | tf_op jit(solution)/shard_map/ppermute | solution.py:52
  52.6 9.4 %collective-permute-done.7.refs_2_ = bf16[4,80,768]{2,1,0:T(8,128)(2,1)} collective-permute-done((bf16[4,80,768]{2,1,0:T(8,128)(2,1)S(1)}, bf16[4,80,768]{2,1,0:T(8,128)(2,1)}, u32[]{:S(2)}, u32[]{:S(2)}) %collective-permute-start.7) | collective-permute-done | bytes 491552 | tf_op jit(solution)/shard_map/ppermute | solution.py:52
  68.8 3.5 all-to-all-start.1
  72.3 5.2 %shard_map.239 = (bf16[3,32,24,768]{3,2,1,0:T(8,128)(2,1)}, bf16[1,32,8,768]{3,2,1,0:T(8,128)(2,1)}) custom-call(s32[1]{0:T(128)} %bitcast.21.me_ref, bf16[4,80,768]{2,1,0:T(8,128)(2,1)} %copy-done.5, bf16[4,80,768]{2,1,0:T(8,128)(2,1)} %copy-done.11, bf16[4,80,768]{2,1,0:T(8,128)(2,1)} %collective-permute-done.7.refs_2_, ...), custom_call_target="tpu_custom_call" | custom-call | flops 115000000 | bytes 1024 | tf_op jit(solution)/shard_map/pallas_call | solution.py:157
  78.5 2.7 collective-permute-start.13
  85.4 4.8 %all-to-all-start.2 = ((bf16[4,96,768]{2,1,0:T(8,128)(2,1)}), bf16[4,96,768]{2,1,0:T(8,128)(2,1)}, u32[]{:S(2)}, u32[]{:S(2)}) async-start(bf16[4,96,768]{2,1,0:T(8,128)(2,1)} %broadcast_select_fusion.3), calls=%async_computation.2 | async-start | bytes 1179648 | tf_op jit(solution)/shard_map/all_to_all | solution.py:61
  94.0 15.6 %shard_map.241 = (bf16[3,512,768]{2,1,0:T(8,128)(2,1)}, bf16[512,768]{1,0:T(8,128)(2,1)}, f32[3,4,512]{2,1,0:T(4,128)}) custom-call(bf16[512,768]{1,0:T(8,128)(2,1)} %bitcast.115, bf16[3,768,768]{2,1,0:T(8,128)(2,1)} %bitcast.113, f32[8,768]{1,0:T(8,128)} %get-tuple-element.212.rows_ref.rows, s32[1,512]{1,0:T(1,128)} %bitcast.139, s32[512,1]{1,0:T(8,128)} %copy.58.seg_col_ref), custom_call_target="tpu_custom_call" | custom-call | flops 115000000 | bytes 1024 | tf_op jit(solution)/shard_map/pallas_call | solution.py:555
  109.6 6.1 %collective-permute-done.14.refs_2_ = bf16[4,24,3840]{2,1,0:T(8,128)(2,1)} collective-permute-done((bf16[4,24,3840]{2,1,0:T(8,128)(2,1)S(1)}, bf16[4,24,3840]{2,1,0:T(8,128)(2,1)}, u32[]{:S(2)}, u32[]{:S(2)}) %collective-permute-start.14) | collective-permute-done | bytes 737312 | tf_op jit(solution)/shard_map/ppermute | solution.py:52
  126.0 4.8 %all-to-all-start.3 = ((bf16[4,128,768]{2,1,0:T(8,128)(2,1)}), bf16[4,128,768]{2,1,0:T(8,128)(2,1)S(1)}, u32[]{:S(2)}, u32[]{:S(2)}) async-start(bf16[4,128,768]{2,1,0:T(8,128)(2,1)} %maximum_select_fusion.1), calls=%async_computation.3 | async-start | bytes 1572864 | tf_op jit(solution)/shard_map/all_to_all | solution.py:61
  130.8 6.7 %shard_map.242 = (bf16[1,32,24,768]{3,2,1,0:T(8,128)(2,1)}, bf16[4,32,24,768]{3,2,1,0:T(8,128)(2,1)}) custom-call(s32[1]{0:T(128)} %bitcast.21.me_ref, bf16[4,24,3840]{2,1,0:T(8,128)(2,1)} %copy-done.1, bf16[4,24,3840]{2,1,0:T(8,128)(2,1)} %copy-done.9, bf16[4,24,3840]{2,1,0:T(8,128)(2,1)} %collective-permute-done.14.refs_2_, ...), custom_call_target="tpu_custom_call" | custom-call | flops 115000000 | bytes 1024 | tf_op jit(solution)/shard_map/pallas_call | solution.py:157
  137.5 5.8 %shard_map.243 = (f32[512,768]{1,0:T(8,128)}, bf16[512,768]{1,0:T(8,128)(2,1)}, f32[512,768]{1,0:T(8,128)}, f32[512,1]{1,0:T(8,128)}, f32[2,128]{1,0:T(2,128)}) custom-call(bf16[512,768]{1,0:T(8,128)(2,1)} %get-tuple-element.216.ctx.refs_0_, bf16[1,768,768]{2,1,0:T(8,128)(2,1)} %bitcast.147, bf16[512,768]{1,0:T(8,128)(2,1)} %bitcast.116, ...), custom_call_target="tpu_custom_call" | custom-call | flops 5750000128 | bytes 1024 | tf_op jit(solution)/shard_map/pallas_call | solution.py:759
  143.3 9.2 %shard_map.244 = (bf16[512,3072]{1,0:T(8,128)(2,1)}, bf16[512,3072]{1,0:T(8,128)(2,1)}) custom-call(bf16[512,768]{1,0:T(8,128)(2,1)} %get-tuple-element.233.x_ref.refs_2_, bf16[4,768,768]{2,1,0:T(8,128)(2,1)} %bitcast.145, f32[1,3072]{1,0:T(1,128)} %get-tuple-element.235.bias_ref), custom_call_target="tpu_custom_call" | custom-call | flops 9200000000 | bytes 1024 | tf_op jit(solution)/shard_map/pallas_call | solution.py:676
  155.5 3.7 all-to-all-start.4
  160.2 12.8 %shard_map.245 = (bf16[512,768]{1,0:T(8,128)(2,1)}, f32[512,768]{1,0:T(8,128)}, f32[512,1]{1,0:T(8,128)}, bf16[32,768]{1,0:T(8,128)(2,1)}, f32[3,128]{1,0:T(4,128)}, /*index=5*/bf16[3072,768]{1,0:T(8,128)(2,1)}) custom-call(s32[1]{0:T(128)} %bitcast.21.me_ref, bf16[512,3072]{1,0:T(8,128)(2,1)} %get-tuple-element.240.active.left_ref, ...), custom_call_target="tpu_custom_call" | custom-call | flops 10350000128 | bytes 1024 | tf_op jit(solution)/shard_map/pallas_call | solution.py:825
  177.6 3.7 collective-permute-done.28
  184.4 2.7 collective-permute-start.30
  193.7 2.6 shard_map.246.pool
  196.3 3.5 all-to-all-start.5
  199.8 6.1 %shard_map.247 = (f32[512,768]{1,0:T(8,128)}, bf16[512,768]{1,0:T(8,128)(2,1)}, f32[3,768]{1,0:T(4,128)}) custom-call(bf16[512,768]{1,0:T(8,128)(2,1)} %bitcast.123, f32[512,1]{1,0:T(8,128)} %compare_convert_fusion.valid, f32[32,512]{1,0:T(8,128)} %fusion.14.hot, f32[32,768]{1,0:T(8,128)} %shard_map.246.pool, f32[512,768]{1,0:T(8,128)} %get-tuple-element.252.unit, ...), custom_call_target="tpu_custom_call" | custom-call | flops 6899999744 | bytes 1024 | tf_op jit(solution)/shard_map/pallas_call | solution.py:864
  205.8 9.0 %shard_map.248 = (bf16[2,8,192,384]{3,2,1,0:T(8,128)(2,1)}, bf16[2,8,192,384]{3,2,1,0:T(8,128)(2,1)}) custom-call(s32[1]{0:T(128)} %bitcast.34.core_ref, bf16[512,3072]{1,0:T(8,128)(2,1)} %get-tuple-element.240.active.left_ref, bf16[512,768]{1,0:T(8,128)(2,1)} %get-tuple-element.263.right_ref.low), custom_call_target="tpu_custom_call" | custom-call | flops 8049999872 | bytes 1024 | tf_op jit(solution)/shard_map/pallas_call | solution.py:421
  216.9 3.5 all-to-all-start.6
  220.4 5.1 %shard_map.249 = (f32[4,192,384]{2,1,0:T(8,128)}, bf16[4,192,384]{2,1,0:T(8,128)(2,1)}, bf16[4,192,384]{2,1,0:T(8,128)(2,1)}, bf16[4,192,384]{2,1,0:T(8,128)(2,1)}) custom-call(s32[2]{0:T(128)} %pad_add_fusion.1.at_ref, bf16[2,4,2,192,384]{4,3,2,1,0:T(8,128)(2,1)} %bitcast.119, bf16[2,4,2,192,384]{4,3,2,1,0:T(8,128)(2,1)} %bitcast.46.got_ref), custom_call_target="tpu_custom_call" | custom-call | flops 1150000000 | bytes 1024 | tf_op jit(solution)/shard_map/pallas_call | solution.py:291
  229.0 14.4 %shard_map.250 = (bf16[512,3072]{1,0:T(8,128)(2,1)}, f32[1,3072]{1,0:T(1,128)}, f32[512,768]{1,0:T(8,128)}, bf16[512,768]{1,0:T(8,128)(2,1)}, bf16[4,512,192]{2,1,0:T(8,128)(2,1)}, /*index=5*/f32[3,768]{1,0:T(4,128)}) custom-call(bf16[512,768]{1,0:T(8,128)(2,1)} %get-tuple-element.263.right_ref.low, bf16[3072,768]{1,0:T(8,128)(2,1)} %get-tuple-element.264.w_back, ...), custom_call_target="tpu_custom_call" | custom-call | flops 16099999744 | bytes 1024 | tf_op jit(solution)/shard_map/pallas_call | solution.py:912
  243.4 8.4 %shard_map.251 = (bf16[2,8,120,768]{3,2,1,0:T(8,128)(2,1)}, bf16[2,8,120,768]{3,2,1,0:T(8,128)(2,1)}) custom-call(s32[1]{0:T(128)} %bitcast.me_ref, bf16[512,768]{1,0:T(8,128)(2,1)} %get-tuple-element.216.ctx.refs_0_, bf16[4,512,192]{2,1,0:T(8,128)(2,1)} %get-tuple-element.269.refs_1_, bf16[512,768]{1,0:T(8,128)(2,1)} %get-tuple-element.233.x_ref.refs_2_, ...), custom_call_target="tpu_custom_call" | custom-call | flops 9200000000 | bytes 1024 | tf_op jit(solution)/shard_map/pallas_call | solution.py:380
  255.3 2.8 shard_map.253
  260.3 5.7 %shard_map.252 = (f32[4,120,768]{2,1,0:T(8,128)}, bf16[4,120,768]{2,1,0:T(8,128)(2,1)}, bf16[4,120,768]{2,1,0:T(8,128)(2,1)}, bf16[4,120,768]{2,1,0:T(8,128)(2,1)}) custom-call(s32[2]{0:T(128)} %pad_add_fusion.1.at_ref, bf16[2,4,2,120,768]{4,3,2,1,0:T(8,128)(2,1)} %bitcast.118, bf16[2,4,2,120,768]{4,3,2,1,0:T(8,128)(2,1)} %bitcast.49.got_ref), custom_call_target="tpu_custom_call" | custom-call | flops 1150000000 | bytes 1024 | tf_op jit(solution)/shard_map/pallas_call | solution.py:291
  269.4 4.8 %all-to-all-start.7 = ((bf16[4,192,384]{2,1,0:T(8,128)(2,1)}), bf16[4,192,384]{2,1,0:T(8,128)(2,1)S(1)}, u32[]{:S(2)}, u32[]{:S(2)}) async-start(bf16[4,192,384]{2,1,0:T(8,128)(2,1)} %shard_map.253), calls=%async_computation.7 | async-start | bytes 1179648 | tf_op jit(solution)/shard_map/all_to_all | solution.py:61
  274.2 20.3 %shard_map.254 = (bf16[3,512,768]{2,1,0:T(8,128)(2,1)}, bf16[4,512,576]{2,1,0:T(8,128)(2,1)}, f32[2,768]{1,0:T(2,128)}) custom-call(bf16[512,768]{1,0:T(8,128)(2,1)} %get-tuple-element.289.gb_ref, bf16[768,768]{1,0:T(8,128)(2,1)} %bitcast.148, bf16[3,512,768]{2,1,0:T(8,128)(2,1)} %get-tuple-element.290.qkv_ref, f32[3,4,512]{2,1,0:T(4,128)} %get-tuple-element.291.lse_ref, ...), custom_call_target="tpu_custom_call" | custom-call | flops 23000000512 | bytes 1024 | tf_op jit(solution)/shard_map/pallas_call | solution.py:630
  294.5 6.8 %shard_map.255 = (bf16[2,8,48,1152]{3,2,1,0:T(8,128)(2,1)}, bf16[2,8,48,1152]{3,2,1,0:T(8,128)(2,1)}) custom-call(s32[1]{0:T(128)} %bitcast.me_ref, bf16[512,768]{1,0:T(8,128)(2,1)} %bitcast.117, bf16[4,512,576]{2,1,0:T(8,128)(2,1)} %get-tuple-element.292.refs_1_), custom_call_target="tpu_custom_call" | custom-call | flops 9200000000 | bytes 1024 | tf_op jit(solution)/shard_map/pallas_call | solution.py:380
  301.5 6.3 %shard_map.256 = bf16[512,768]{1,0:T(8,128)(2,1)} custom-call(bf16[3,512,768]{2,1,0:T(8,128)(2,1)} %get-tuple-element.302.grad, bf16[3,768,768]{2,1,0:T(8,128)(2,1)} %bitcast.114, f32[512,768]{1,0:T(8,128)} %get-tuple-element.303.residual), custom_call_target="tpu_custom_call" | custom-call | flops 6899999744 | bytes 1024 | tf_op jit(solution)/shard_map/pallas_call | solution.py:949
  307.8 3.5 all-to-all-start.8
  312.2 3.1 shard_map.258
  317.3 2.4 collective-permute-start.44
  320.5 4.7 %shard_map.257 = (f32[4,48,1152]{2,1,0:T(8,128)}, bf16[4,48,1152]{2,1,0:T(8,128)(2,1)}, bf16[4,48,1152]{2,1,0:T(8,128)(2,1)}, bf16[4,48,1152]{2,1,0:T(8,128)(2,1)}) custom-call(s32[2]{0:T(128)} %pad_add_fusion.1.at_ref, bf16[2,4,2,48,1152]{4,3,2,1,0:T(8,128)(2,1)} %bitcast.150, bf16[2,4,2,48,1152]{4,3,2,1,0:T(8,128)(2,1)} %bitcast.52.got_ref), custom_call_target="tpu_custom_call" | custom-call | flops 1150000000 | bytes 1024 | tf_op jit(solution)/shard_map/pallas_call | solution.py:291
  326.3 7.7 %collective-permute-done.44 = bf16[120,768]{1,0:T(8,128)(2,1)} collective-permute-done((bf16[120,768]{1,0:T(8,128)(2,1)}, bf16[120,768]{1,0:T(8,128)(2,1)}, u32[]{:S(2)}, u32[]{:S(2)}) %collective-permute-start.44) | collective-permute-done | bytes 184352 | tf_op jit(solution)/shard_map/ppermute | solution.py:46
  338.5 5.9 %all-to-all-start.9 = ((bf16[4,128,768]{2,1,0:T(8,128)(2,1)}), bf16[4,128,768]{2,1,0:T(8,128)(2,1)S(1)}, u32[]{:S(2)}, u32[]{:S(2)}) async-start(bf16[4,128,768]{2,1,0:T(8,128)(2,1)} %broadcast_select_fusion), calls=%async_computation.9 | async-start | bytes 1572864 | tf_op jit(solution)/shard_map/all_to_all | solution.py:61
  348.6 4.7 %shard_map.259 = f32[32,384]{1,0:T(8,128)} custom-call(f32[2,768]{1,0:T(2,128)} %get-tuple-element.329.attn, f32[3,768]{1,0:T(4,128)} %get-tuple-element.330.out, f32[3,768]{1,0:T(4,128)} %get-tuple-element.331.ffn, f32[1,3072]{1,0:T(1,128)} %get-tuple-element.332.inb, f32[2,128]{1,0:T(2,128)} %get-tuple-element.333.stats_a, f32[3,128]{1,0:T(4,128)} %get-tuple-element.334.stats_b), custom_call_target="tpu_custom_call" | custom-call | flops 4600000000 | bytes 1024 | tf_op jit(solution)/shard_map/pallas_call | solution.py:1033
  355.4 7.8 %all-to-all-done.9 = bf16[4,128,768]{2,1,0:T(8,128)(2,1)S(1)} async-done(((bf16[4,128,768]{2,1,0:T(8,128)(2,1)}), bf16[4,128,768]{2,1,0:T(8,128)(2,1)S(1)}, u32[]{:S(2)}, u32[]{:S(2)}) %all-to-all-start.9) | async-done | bytes 786464 | tf_op jit(solution)/shard_map/all_to_all | solution.py:61
  365.4 3.0 all-to-all-start.10
  368.4 2.4 shard_map.260
  372.6 2.4 collective-permute-start.50
  378.7 5.7 %collective-permute-done.50 = bf16[48,1152]{1,0:T(8,128)(2,1)S(1)} collective-permute-done((bf16[48,1152]{1,0:T(8,128)(2,1)}, bf16[48,1152]{1,0:T(8,128)(2,1)S(1)}, u32[]{:S(2)}, u32[]{:S(2)}) %collective-permute-start.50) | collective-permute-done | bytes 110624 | tf_op jit(solution)/shard_map/ppermute | solution.py:46
  (265 shorter events, 99.0 us)
Async XLA Ops:
  1.9 13.4 %collective-permute-start = (bf16[128,768]{1,0:T(8,128)(2,1)S(1)}, bf16[128,768]{1,0:T(8,128)(2,1)S(1)}, u32[]{:S(2)}, u32[]{:S(2)}) collective-permute-start(bf16[128,768]{1,0:T(8,128)(2,1)S(1)} %get-tuple-element.403), channel_id=1, source_target_pairs={{0,8},{8,0},{4,12},{12,4},{1,9},{9,1},{5,13},{13,5},{2,10},{10,2},... | collective-permute-start | bytes 589832 | tf_op jit(solution)/shard_map/ppermute | solution.py:68
  6.9 24.9 %collective-permute-start.4 = (bf16[128,768]{1,0:T(8,128)(2,1)S(1)}, bf16[128,768]{1,0:T(8,128)(2,1)S(1)}, u32[]{:S(2)}, u32[]{:S(2)}) collective-permute-start(bf16[128,768]{1,0:T(8,128)(2,1)S(1)} %get-tuple-element.402), channel_id=1, source_target_pairs={{0,16},{16,0},{4,20},{20,4},{1,17},{17,1},{5,21},{21,5},{2,18},{18... | collective-permute-start | bytes 589832 | tf_op jit(solution)/shard_map/ppermute | solution.py:68
  8.8 23.0 %collective-permute-start.5 = (bf16[128,768]{1,0:T(8,128)(2,1)S(1)}, bf16[128,768]{1,0:T(8,128)(2,1)S(1)}, u32[]{:S(2)}, u32[]{:S(2)}) collective-permute-start(bf16[128,768]{1,0:T(8,128)(2,1)S(1)} %get-tuple-element.401), channel_id=1, source_target_pairs={{0,24},{24,0},{4,28},{28,4},{1,25},{25,1},{5,29},{29,5},{2,26},{26... | collective-permute-start | bytes 589832 | tf_op jit(solution)/shard_map/ppermute | solution.py:68
  17.2 8.3 %collective-permute-start.3 = (bf16[80,768]{1,0:T(8,128)(2,1)}, bf16[80,768]{1,0:T(8,128)(2,1)S(1)}, u32[]{:S(2)}, u32[]{:S(2)}) collective-permute-start(bf16[80,768]{1,0:T(8,128)(2,1)} %get-tuple-element.185), channel_id=1, source_target_pairs={{0,24},{4,28},{8,16},{12,20},{16,8},{20,12},{24,0},{28,4},{1,25},{... | collective-permute-start | bytes 368648 | tf_op jit(solution)/shard_map/ppermute | solution.py:46
  21.0 9.8 %collective-permute-start.2 = (bf16[80,768]{1,0:T(8,128)(2,1)}, bf16[80,768]{1,0:T(8,128)(2,1)S(1)}, u32[]{:S(2)}, u32[]{:S(2)}) collective-permute-start(bf16[80,768]{1,0:T(8,128)(2,1)} %get-tuple-element.184), channel_id=1, source_target_pairs={{0,16},{4,20},{8,24},{12,28},{16,0},{20,4},{24,8},{28,12},{1,17},{... | collective-permute-start | bytes 368648 | tf_op jit(solution)/shard_map/ppermute | solution.py:46
  21.0 9.8 %collective-permute-start.1 = (bf16[80,768]{1,0:T(8,128)(2,1)}, bf16[80,768]{1,0:T(8,128)(2,1)S(1)}, u32[]{:S(2)}, u32[]{:S(2)}) collective-permute-start(bf16[80,768]{1,0:T(8,128)(2,1)} %get-tuple-element.183), channel_id=1, source_target_pairs={{0,8},{4,12},{8,0},{12,4},{16,24},{20,28},{24,16},{28,20},{1,9},{5... | collective-permute-start | bytes 368648 | tf_op jit(solution)/shard_map/ppermute | solution.py:46
  32.8 29.3 %all-to-all-start = ((bf16[4,24,3840]{2,1,0:T(8,128)(2,1)}), bf16[4,24,3840]{2,1,0:T(8,128)(2,1)S(1)}, u32[]{:S(2)}, u32[]{:S(2)}) async-start(bf16[4,24,3840]{2,1,0:T(8,128)(2,1)} %broadcast_select_fusion.2), calls=%async_computation | async-start | bytes 1474560 | tf_op jit(solution)/shard_map/all_to_all | solution.py:61
  37.6 15.1 %collective-permute-start.6 = (bf16[4,80,768]{2,1,0:T(8,128)(2,1)S(1)}, bf16[4,80,768]{2,1,0:T(8,128)(2,1)S(1)}, u32[]{:S(2)}, u32[]{:S(2)}) collective-permute-start(bf16[4,80,768]{2,1,0:T(8,128)(2,1)S(1)} %pad_maximum_fusion.2.refs_0_), channel_id=1, source_target_pairs={{0,6},{1,7},{2,4},{3,5},{4,2},{5,3},{6,0},{7,1},{8,14},{9,15},{10,... | collective-permute-start | bytes 1474568 | tf_op jit(solution)/shard_map/ppermute | solution.py:52
  40.0 22.1 %collective-permute-start.7 = (bf16[4,80,768]{2,1,0:T(8,128)(2,1)S(1)}, bf16[4,80,768]{2,1,0:T(8,128)(2,1)}, u32[]{:S(2)}, u32[]{:S(2)}) collective-permute-start(bf16[4,80,768]{2,1,0:T(8,128)(2,1)S(1)} %pad_maximum_fusion.2.refs_0_), channel_id=1, source_target_pairs={{0,2},{1,3},{2,0},{3,1},{4,6},{5,7},{6,4},{7,5},{8,10},{9,11},{10,... | collective-permute-start | bytes 1474568 | tf_op jit(solution)/shard_map/ppermute | solution.py:52
  40.5 21.5 %collective-permute-start.8 = (bf16[4,80,768]{2,1,0:T(8,128)(2,1)S(1)}, bf16[4,80,768]{2,1,0:T(8,128)(2,1)}, u32[]{:S(2)}, u32[]{:S(2)}) collective-permute-start(bf16[4,80,768]{2,1,0:T(8,128)(2,1)S(1)} %pad_maximum_fusion.2.refs_0_), channel_id=1, source_target_pairs={{0,4},{1,5},{2,6},{3,7},{4,0},{5,1},{6,2},{7,3},{8,12},{9,13},{10,... | collective-permute-start | bytes 1474568 | tf_op jit(solution)/shard_map/ppermute | solution.py:52
  68.8 15.6 %all-to-all-start.1 = ((bf16[4,128,768]{2,1,0:T(8,128)(2,1)}), bf16[4,128,768]{2,1,0:T(8,128)(2,1)S(1)}, u32[]{:S(2)}, u32[]{:S(2)}) async-start(bf16[4,128,768]{2,1,0:T(8,128)(2,1)} %maximum_select_fusion), calls=%async_computation.1 | async-start | bytes 1572864 | tf_op jit(solution)/shard_map/all_to_all | solution.py:107
  78.5 31.0 %collective-permute-start.13 = (bf16[4,24,3840]{2,1,0:T(8,128)(2,1)S(1)}, bf16[4,24,3840]{2,1,0:T(8,128)(2,1)S(1)}, u32[]{:S(2)}, u32[]{:S(2)}) collective-permute-start(bf16[4,24,3840]{2,1,0:T(8,128)(2,1)S(1)} %all-to-all-done.refs_0_), channel_id=1, source_target_pairs={{0,6},{1,7},{2,4},{3,5},{4,2},{5,3},{6,0},{7,1},{8,14},{9,15},{10,... | collective-permute-start | bytes 2211848 | tf_op jit(solution)/shard_map/ppermute | solution.py:52
  81.2 34.4 %collective-permute-start.14 = (bf16[4,24,3840]{2,1,0:T(8,128)(2,1)S(1)}, bf16[4,24,3840]{2,1,0:T(8,128)(2,1)}, u32[]{:S(2)}, u32[]{:S(2)}) collective-permute-start(bf16[4,24,3840]{2,1,0:T(8,128)(2,1)S(1)} %all-to-all-done.refs_0_), channel_id=1, source_target_pairs={{0,2},{1,3},{2,0},{3,1},{4,6},{5,7},{6,4},{7,5},{8,10},{9,11},{10,... | collective-permute-start | bytes 2211848 | tf_op jit(solution)/shard_map/ppermute | solution.py:52
  81.4 34.3 %collective-permute-start.15 = (bf16[4,24,3840]{2,1,0:T(8,128)(2,1)S(1)}, bf16[4,24,3840]{2,1,0:T(8,128)(2,1)}, u32[]{:S(2)}, u32[]{:S(2)}) collective-permute-start(bf16[4,24,3840]{2,1,0:T(8,128)(2,1)S(1)} %all-to-all-done.refs_0_), channel_id=1, source_target_pairs={{0,4},{1,5},{2,6},{3,7},{4,0},{5,1},{6,2},{7,3},{8,12},{9,13},{10,... | collective-permute-start | bytes 2211848 | tf_op jit(solution)/shard_map/ppermute | solution.py:52
  85.4 30.2 %all-to-all-start.2 = ((bf16[4,96,768]{2,1,0:T(8,128)(2,1)}), bf16[4,96,768]{2,1,0:T(8,128)(2,1)}, u32[]{:S(2)}, u32[]{:S(2)}) async-start(bf16[4,96,768]{2,1,0:T(8,128)(2,1)} %broadcast_select_fusion.3), calls=%async_computation.2 | async-start | bytes 1179648 | tf_op jit(solution)/shard_map/all_to_all | solution.py:61
  121.4 31.1 %collective-permute-start.20 = (bf16[4,96,768]{2,1,0:T(8,128)(2,1)}, bf16[4,96,768]{2,1,0:T(8,128)(2,1)}, u32[]{:S(2)}, u32[]{:S(2)}) collective-permute-start(bf16[4,96,768]{2,1,0:T(8,128)(2,1)} %all-to-all-done.2.refs_0_), channel_id=1, source_target_pairs={{0,6},{1,7},{2,4},{3,5},{4,2},{5,3},{6,0},{7,1},{8,14},{9,15},{10,... | collective-permute-start | bytes 1769480 | tf_op jit(solution)/shard_map/ppermute | solution.py:52
  122.6 30.0 %collective-permute-start.21 = (bf16[4,96,768]{2,1,0:T(8,128)(2,1)}, bf16[4,96,768]{2,1,0:T(8,128)(2,1)}, u32[]{:S(2)}, u32[]{:S(2)}) collective-permute-start(bf16[4,96,768]{2,1,0:T(8,128)(2,1)} %all-to-all-done.2.refs_0_), channel_id=1, source_target_pairs={{0,2},{1,3},{2,0},{3,1},{4,6},{5,7},{6,4},{7,5},{8,10},{9,11},{10,... | collective-permute-start | bytes 1769480 | tf_op jit(solution)/shard_map/ppermute | solution.py:52
  124.2 28.3 %collective-permute-start.22 = (bf16[4,96,768]{2,1,0:T(8,128)(2,1)}, bf16[4,96,768]{2,1,0:T(8,128)(2,1)}, u32[]{:S(2)}, u32[]{:S(2)}) collective-permute-start(bf16[4,96,768]{2,1,0:T(8,128)(2,1)} %all-to-all-done.2.refs_0_), channel_id=1, source_target_pairs={{0,4},{1,5},{2,6},{3,7},{4,0},{5,1},{6,2},{7,3},{8,12},{9,13},{10,... | collective-permute-start | bytes 1769480 | tf_op jit(solution)/shard_map/ppermute | solution.py:52
  126.0 26.6 %all-to-all-start.3 = ((bf16[4,128,768]{2,1,0:T(8,128)(2,1)}), bf16[4,128,768]{2,1,0:T(8,128)(2,1)S(1)}, u32[]{:S(2)}, u32[]{:S(2)}) async-start(bf16[4,128,768]{2,1,0:T(8,128)(2,1)} %maximum_select_fusion.1), calls=%async_computation.3 | async-start | bytes 1572864 | tf_op jit(solution)/shard_map/all_to_all | solution.py:61
  152.6 6.5 %collective-permute-start.23 = (bf16[4,96,768]{2,1,0:T(8,128)(2,1)}, bf16[4,96,768]{2,1,0:T(8,128)(2,1)S(1)}, u32[]{:S(2)}, u32[]{:S(2)}) collective-permute-start(bf16[4,96,768]{2,1,0:T(8,128)(2,1)} %all-to-all-done.2.refs_0_), channel_id=1, source_target_pairs={{0,1},{1,0},{2,3},{3,2},{4,5},{5,4},{6,7},{7,6},{8,9},{9,8},{10,11... | collective-permute-start | bytes 1769480 | tf_op jit(solution)/shard_map/ppermute | solution.py:46
  152.7 6.5 %collective-permute-start.24 = (bf16[4,96,768]{2,1,0:T(8,128)(2,1)}, bf16[4,96,768]{2,1,0:T(8,128)(2,1)S(1)}, u32[]{:S(2)}, u32[]{:S(2)}) collective-permute-start(bf16[4,96,768]{2,1,0:T(8,128)(2,1)} %collective-permute-done.20.refs_1_), channel_id=1, source_target_pairs={{0,1},{1,0},{2,3},{3,2},{4,5},{5,4},{6,7},{7,6},{8,9},{9,8},{10,11... | collective-permute-start | bytes 1769480 | tf_op jit(solution)/shard_map/ppermute | solution.py:46
  153.2 6.0 %collective-permute-start.25 = (bf16[4,96,768]{2,1,0:T(8,128)(2,1)}, bf16[4,96,768]{2,1,0:T(8,128)(2,1)}, u32[]{:S(2)}, u32[]{:S(2)}) collective-permute-start(bf16[4,96,768]{2,1,0:T(8,128)(2,1)} %collective-permute-done.21.refs_2_), channel_id=1, source_target_pairs={{0,1},{1,0},{2,3},{3,2},{4,5},{5,4},{6,7},{7,6},{8,9},{9,8},{10,11... | collective-permute-start | bytes 1769480 | tf_op jit(solution)/shard_map/ppermute | solution.py:46
  153.3 5.9 %collective-permute-start.26 = (bf16[4,96,768]{2,1,0:T(8,128)(2,1)}, bf16[4,96,768]{2,1,0:T(8,128)(2,1)}, u32[]{:S(2)}, u32[]{:S(2)}) collective-permute-start(bf16[4,96,768]{2,1,0:T(8,128)(2,1)} %collective-permute-done.22.refs_3_), channel_id=1, source_target_pairs={{0,1},{1,0},{2,3},{3,2},{4,5},{5,4},{6,7},{7,6},{8,9},{9,8},{10,11... | collective-permute-start | bytes 1769480 | tf_op jit(solution)/shard_map/ppermute | solution.py:46
  155.5 17.5 %all-to-all-start.4 = ((bf16[4,128,768]{2,1,0:T(8,128)(2,1)}), bf16[4,128,768]{2,1,0:T(8,128)(2,1)S(1)}, u32[]{:S(2)}, u32[]{:S(2)}) async-start(bf16[4,128,768]{2,1,0:T(8,128)(2,1)} %maximum_select_fusion.2), calls=%async_computation.4 | async-start | bytes 1572864 | tf_op jit(solution)/shard_map/all_to_all | solution.py:107
  175.1 6.2 %collective-permute-start.28 = (bf16[32,768]{1,0:T(8,128)(2,1)}, bf16[32,768]{1,0:T(8,128)(2,1)S(1)}, u32[]{:S(2)}, u32[]{:S(2)}) collective-permute-start(bf16[32,768]{1,0:T(8,128)(2,1)} %get-tuple-element.249), channel_id=1, source_target_pairs={{0,16},{4,20},{8,24},{12,28},{16,0},{20,4},{24,8},{28,12},{1,17},{... | collective-permute-start | bytes 147464 | tf_op jit(solution)/shard_map/ppermute | solution.py:46
  177.5 6.1 %collective-permute-start.27 = (bf16[32,768]{1,0:T(8,128)(2,1)}, bf16[32,768]{1,0:T(8,128)(2,1)S(1)}, u32[]{:S(2)}, u32[]{:S(2)}) collective-permute-start(bf16[32,768]{1,0:T(8,128)(2,1)} %get-tuple-element.249), channel_id=1, source_target_pairs={{0,24},{4,28},{8,16},{12,20},{16,8},{20,12},{24,0},{28,4},{1,25},{... | collective-permute-start | bytes 147464 | tf_op jit(solution)/shard_map/ppermute | solution.py:46
  196.3 18.6 %all-to-all-start.5 = ((bf16[4,128,768]{2,1,0:T(8,128)(2,1)}), bf16[4,128,768]{2,1,0:T(8,128)(2,1)S(1)}, u32[]{:S(2)}, u32[]{:S(2)}) async-start(bf16[4,128,768]{2,1,0:T(8,128)(2,1)} %bitcast.45), calls=%async_computation.5 | async-start | bytes 1572864 | tf_op jit(solution)/shard_map/all_to_all | solution.py:112
  216.9 34.9 %all-to-all-start.6 = ((bf16[4,128,768]{2,1,0:T(8,128)(2,1)}), bf16[4,128,768]{2,1,0:T(8,128)(2,1)S(1)}, u32[]{:S(2)}, u32[]{:S(2)}) async-start(bf16[4,128,768]{2,1,0:T(8,128)(2,1)} %broadcast_select_fusion.1), calls=%async_computation.6 | async-start | bytes 1572864 | tf_op jit(solution)/shard_map/all_to_all | solution.py:61
  225.5 26.3 %collective-permute-start.35 = (bf16[4,192,384]{2,1,0:T(8,128)(2,1)}, bf16[4,192,384]{2,1,0:T(8,128)(2,1)S(1)}, u32[]{:S(2)}, u32[]{:S(2)}) collective-permute-start(bf16[4,192,384]{2,1,0:T(8,128)(2,1)} %get-tuple-element.273), channel_id=1, source_target_pairs={{0,6},{1,7},{2,4},{3,5},{4,2},{5,3},{6,0},{7,1},{8,14},{9,15},{10,... | collective-permute-start | bytes 1769480 | tf_op jit(solution)/shard_map/ppermute | solution.py:52
  227.3 26.6 %collective-permute-start.36 = (bf16[4,192,384]{2,1,0:T(8,128)(2,1)}, bf16[4,192,384]{2,1,0:T(8,128)(2,1)S(1)}, u32[]{:S(2)}, u32[]{:S(2)}) collective-permute-start(bf16[4,192,384]{2,1,0:T(8,128)(2,1)} %get-tuple-element.274), channel_id=1, source_target_pairs={{0,2},{1,3},{2,0},{3,1},{4,6},{5,7},{6,4},{7,5},{8,10},{9,11},{10,... | collective-permute-start | bytes 1769480 | tf_op jit(solution)/shard_map/ppermute | solution.py:52
  227.6 26.9 %collective-permute-start.37 = (bf16[4,192,384]{2,1,0:T(8,128)(2,1)}, bf16[4,192,384]{2,1,0:T(8,128)(2,1)S(1)}, u32[]{:S(2)}, u32[]{:S(2)}) collective-permute-start(bf16[4,192,384]{2,1,0:T(8,128)(2,1)} %get-tuple-element.275), channel_id=1, source_target_pairs={{0,4},{1,5},{2,6},{3,7},{4,0},{5,1},{6,2},{7,3},{8,12},{9,13},{10,... | collective-permute-start | bytes 1769480 | tf_op jit(solution)/shard_map/ppermute | solution.py:52
  266.0 35.3 %collective-permute-start.39 = (bf16[4,120,768]{2,1,0:T(8,128)(2,1)}, bf16[4,120,768]{2,1,0:T(8,128)(2,1)S(1)}, u32[]{:S(2)}, u32[]{:S(2)}) collective-permute-start(bf16[4,120,768]{2,1,0:T(8,128)(2,1)} %get-tuple-element.297), channel_id=1, source_target_pairs={{0,6},{1,7},{2,4},{3,5},{4,2},{5,3},{6,0},{7,1},{8,14},{9,15},{10,... | collective-permute-start | bytes 2211848 | tf_op jit(solution)/shard_map/ppermute | solution.py:52
  268.1 33.2 %collective-permute-start.40 = (bf16[4,120,768]{2,1,0:T(8,128)(2,1)}, bf16[4,120,768]{2,1,0:T(8,128)(2,1)}, u32[]{:S(2)}, u32[]{:S(2)}) collective-permute-start(bf16[4,120,768]{2,1,0:T(8,128)(2,1)} %get-tuple-element.298), channel_id=1, source_target_pairs={{0,2},{1,3},{2,0},{3,1},{4,6},{5,7},{6,4},{7,5},{8,10},{9,11},{10,... | collective-permute-start | bytes 2211848 | tf_op jit(solution)/shard_map/ppermute | solution.py:52
  268.2 33.3 %collective-permute-start.41 = (bf16[4,120,768]{2,1,0:T(8,128)(2,1)}, bf16[4,120,768]{2,1,0:T(8,128)(2,1)}, u32[]{:S(2)}, u32[]{:S(2)}) collective-permute-start(bf16[4,120,768]{2,1,0:T(8,128)(2,1)} %get-tuple-element.299), channel_id=1, source_target_pairs={{0,4},{1,5},{2,6},{3,7},{4,0},{5,1},{6,2},{7,3},{8,12},{9,13},{10,... | collective-permute-start | bytes 2211848 | tf_op jit(solution)/shard_map/ppermute | solution.py:52
  269.4 32.1 %all-to-all-start.7 = ((bf16[4,192,384]{2,1,0:T(8,128)(2,1)}), bf16[4,192,384]{2,1,0:T(8,128)(2,1)S(1)}, u32[]{:S(2)}, u32[]{:S(2)}) async-start(bf16[4,192,384]{2,1,0:T(8,128)(2,1)} %shard_map.253), calls=%async_computation.7 | async-start | bytes 1179648 | tf_op jit(solution)/shard_map/all_to_all | solution.py:61
  301.5 6.3 %collective-permute-start.42 = (bf16[2,8,48,1152]{3,2,1,0:T(8,128)(2,1)}, bf16[2,8,48,1152]{3,2,1,0:T(8,128)(2,1)}, u32[]{:S(2)}, u32[]{:S(2)}) collective-permute-start(bf16[2,8,48,1152]{3,2,1,0:T(8,128)(2,1)} %get-tuple-element.301), channel_id=1, source_target_pairs={{0,1},{1,0},{2,3},{3,2},{4,5},{5,4},{6,7},{7,6},{8,9},{9,8},{10,11... | collective-permute-start | bytes 5308424 | tf_op jit(solution)/shard_map/ppermute | solution.py:46
  307.8 26.1 %all-to-all-start.8 = ((bf16[4,128,768]{2,1,0:T(8,128)(2,1)}), bf16[4,128,768]{2,1,0:T(8,128)(2,1)S(1)}, u32[]{:S(2)}, u32[]{:S(2)}) async-start(bf16[4,128,768]{2,1,0:T(8,128)(2,1)} %bitcast.124), calls=%async_computation.8 | async-start | bytes 1572864 | tf_op jit(solution)/shard_map/all_to_all | solution.py:112
  315.4 10.9 %collective-permute-start.43 = (bf16[120,768]{1,0:T(8,128)(2,1)}, bf16[120,768]{1,0:T(8,128)(2,1)S(1)}, u32[]{:S(2)}, u32[]{:S(2)}) collective-permute-start(bf16[120,768]{1,0:T(8,128)(2,1)} %get-tuple-element.318), channel_id=1, source_target_pairs={{0,8},{4,12},{8,0},{12,4},{16,24},{20,28},{24,16},{28,20},{1,9},{5... | collective-permute-start | bytes 552968 | tf_op jit(solution)/shard_map/ppermute | solution.py:46
  317.3 16.6 %collective-permute-start.44 = (bf16[120,768]{1,0:T(8,128)(2,1)}, bf16[120,768]{1,0:T(8,128)(2,1)}, u32[]{:S(2)}, u32[]{:S(2)}) collective-permute-start(bf16[120,768]{1,0:T(8,128)(2,1)} %get-tuple-element.319), channel_id=1, source_target_pairs={{0,16},{4,20},{8,24},{12,28},{16,0},{20,4},{24,8},{28,12},{1,17},{... | collective-permute-start | bytes 552968 | tf_op jit(solution)/shard_map/ppermute | solution.py:46
  319.7 14.3 %collective-permute-start.45 = (bf16[120,768]{1,0:T(8,128)(2,1)}, bf16[120,768]{1,0:T(8,128)(2,1)}, u32[]{:S(2)}, u32[]{:S(2)}) collective-permute-start(bf16[120,768]{1,0:T(8,128)(2,1)} %get-tuple-element.320), channel_id=1, source_target_pairs={{0,24},{4,28},{8,16},{12,20},{16,8},{20,12},{24,0},{28,4},{1,25},{... | collective-permute-start | bytes 552968 | tf_op jit(solution)/shard_map/ppermute | solution.py:46
  334.0 19.3 %collective-permute-start.46 = (bf16[4,48,1152]{2,1,0:T(8,128)(2,1)}, bf16[4,48,1152]{2,1,0:T(8,128)(2,1)}, u32[]{:S(2)}, u32[]{:S(2)}) collective-permute-start(bf16[4,48,1152]{2,1,0:T(8,128)(2,1)} %get-tuple-element.325), channel_id=1, source_target_pairs={{0,6},{1,7},{2,4},{3,5},{4,2},{5,3},{6,0},{7,1},{8,14},{9,15},{10,... | collective-permute-start | bytes 1327112 | tf_op jit(solution)/shard_map/ppermute | solution.py:52
  336.2 18.6 %collective-permute-start.47 = (bf16[4,48,1152]{2,1,0:T(8,128)(2,1)}, bf16[4,48,1152]{2,1,0:T(8,128)(2,1)}, u32[]{:S(2)}, u32[]{:S(2)}) collective-permute-start(bf16[4,48,1152]{2,1,0:T(8,128)(2,1)} %get-tuple-element.326), channel_id=1, source_target_pairs={{0,2},{1,3},{2,0},{3,1},{4,6},{5,7},{6,4},{7,5},{8,10},{9,11},{10,... | collective-permute-start | bytes 1327112 | tf_op jit(solution)/shard_map/ppermute | solution.py:52
  336.3 19.2 %collective-permute-start.48 = (bf16[4,48,1152]{2,1,0:T(8,128)(2,1)}, bf16[4,48,1152]{2,1,0:T(8,128)(2,1)}, u32[]{:S(2)}, u32[]{:S(2)}) collective-permute-start(bf16[4,48,1152]{2,1,0:T(8,128)(2,1)} %get-tuple-element.327), channel_id=1, source_target_pairs={{0,4},{1,5},{2,6},{3,7},{4,0},{5,1},{6,2},{7,3},{8,12},{9,13},{10,... | collective-permute-start | bytes 1327112 | tf_op jit(solution)/shard_map/ppermute | solution.py:52
  338.5 24.7 %all-to-all-start.9 = ((bf16[4,128,768]{2,1,0:T(8,128)(2,1)}), bf16[4,128,768]{2,1,0:T(8,128)(2,1)S(1)}, u32[]{:S(2)}, u32[]{:S(2)}) async-start(bf16[4,128,768]{2,1,0:T(8,128)(2,1)} %broadcast_select_fusion), calls=%async_computation.9 | async-start | bytes 1572864 | tf_op jit(solution)/shard_map/all_to_all | solution.py:61
  365.4 10.3 %all-to-all-start.10 = ((f32[32,1,384]{2,1,0:T(1,128)}), f32[32,1,384]{2,1,0:T(1,128)S(1)}, u32[]{:S(2)}, u32[]{:S(2)}) async-start(f32[32,1,384]{2,1,0:T(1,128)} %copy.65), calls=%async_computation.10 | async-start | bytes 98304 | tf_op jit(solution)/shard_map/all_to_all | solution.py:1289
  370.8 7.9 %collective-permute-start.49 = (bf16[48,1152]{1,0:T(8,128)(2,1)}, bf16[48,1152]{1,0:T(8,128)(2,1)S(1)}, u32[]{:S(2)}, u32[]{:S(2)}) collective-permute-start(bf16[48,1152]{1,0:T(8,128)(2,1)} %get-tuple-element.341), channel_id=1, source_target_pairs={{0,8},{4,12},{8,0},{12,4},{16,24},{20,28},{24,16},{28,20},{1,9},{5... | collective-permute-start | bytes 331784 | tf_op jit(solution)/shard_map/ppermute | solution.py:46
  372.6 11.8 %collective-permute-start.50 = (bf16[48,1152]{1,0:T(8,128)(2,1)}, bf16[48,1152]{1,0:T(8,128)(2,1)S(1)}, u32[]{:S(2)}, u32[]{:S(2)}) collective-permute-start(bf16[48,1152]{1,0:T(8,128)(2,1)} %get-tuple-element.342), channel_id=1, source_target_pairs={{0,16},{4,20},{8,24},{12,28},{16,0},{20,4},{24,8},{28,12},{1,17},{... | collective-permute-start | bytes 331784 | tf_op jit(solution)/shard_map/ppermute | solution.py:46
  375.0 9.4 %collective-permute-start.51 = (bf16[48,1152]{1,0:T(8,128)(2,1)}, bf16[48,1152]{1,0:T(8,128)(2,1)S(1)}, u32[]{:S(2)}, u32[]{:S(2)}) collective-permute-start(bf16[48,1152]{1,0:T(8,128)(2,1)} %get-tuple-element.343), channel_id=1, source_target_pairs={{0,24},{4,28},{8,16},{12,20},{16,8},{20,12},{24,0},{28,4},{1,25},{... | collective-permute-start | bytes 331784 | tf_op jit(solution)/shard_map/ppermute | solution.py:46
  (44 other events, 498.7 us)
where the time goes:
time: 389 us; the launch traced here: 386 us
  Pallas kernels  162 us (42%)
  starting transfers between devices  100 us (26%)
  waiting for transfers between devices  83.7 us (22%)
  other arithmetic  25.3 us (7%)
  local copies, waits for them, and re-layouts  13.6 us (3%)
    ppermute x28, waiting for transfers between devices, flip(): return lax.ppermute(x, axis, [(i, i ^ mask) for i in range(size)])  39.9 us
    ppermute x21, waiting for transfers between devices, flip_both(): return lax.ppermute(x, BOTH, [(i, i ^ mask) for i in range(wide * narrow)])  33.3 us
    all_to_all x6, starting transfers between devices, across_levels(): return lax.all_to_all(x, 'wide', 0, 0, axis_index_groups=groups, tiled=True)  28.6 us
    ppermute x21, starting transfers between devices, flip_both(): return lax.ppermute(x, BOTH, [(i, i ^ mask) for i in range(wide * narrow)])  24.5 us
    ppermute x28, starting transfers between devices, flip(): return lax.ppermute(x, axis, [(i, i ^ mask) for i in range(size)])  21.5 us
    pallas_call x1, Pallas kernels, attend_back(): pl.pallas_call(attend_back_kernel, grid=(d // width,), in_specs=[pl.Block...  20.3 us
    pallas_call x1, Pallas kernels, attend(): pl.pallas_call(attend_kernel, grid=(steps,), in_specs=[pl.BlockSpec((t, d...  15.6 us
    pallas_call x3, Pallas kernels, column_shares(): pl.pallas_call(share_kernel, grid_spec=pltpu.PrefetchScalarGridSpec(num_s...  15.5 us
  transfers between devices with their start and end apart: 63, of which 29 were waited for; matrix products, arithmetic and copies ran while one was open for 7% of the time, Pallas kernels for 40%

commit v1 on v0

--- a/solution.py
+++ b/solution.py
@@ -448,16 +448,22 @@
 
     def step(refs, store):
         context_ref, branch_ref, normed_ref, hidden_ref = refs
-        value = inner_rows(normed_ref[...], hidden_ref[...])
-        for w in range(place.wide):
-            store((w, slice(0, rows)), value[w * rows : (w + 1) * rows])
-        value = inner_rows(context_ref[...], branch_ref[0])
-        for w in range(place.wide):
-            for g in range(fold):
-                store(
-                    (w, slice(rows, rows + low), slice(g * cols_out, (g + 1) * cols_out)),
-                    value[w * rows + g * low : w * rows + (g + 1) * low],
-                )
+
+        def body(i, carry):
+            at = pl.ds(pl.multiple_of(i * 4 * rows, 4 * rows), 4 * rows)
+            value = inner_rows(normed_ref[:, at], hidden_ref[...])
+            for w in range(4):
+                store((4 * i + w, slice(0, rows)), value[w * rows : (w + 1) * rows])
+            value = inner_rows(context_ref[:, at], branch_ref[0])
+            for w in range(4):
+                for g in range(fold):
+                    store(
+                        (4 * i + w, slice(rows, rows + low), slice(g * cols_out, (g + 1) * cols_out)),
+                        value[w * rows + g * low : w * rows + (g + 1) * low],
+                    )
+            return carry
+
+        lax.fori_loop(0, place.wide // 4, body, 0)
 
     return products(
         place,
@@ -491,13 +497,19 @@
 
     def step(refs, store):
         left, right = refs
-        value = inner_rows(left[...], right[0])
-        for w in range(place.wide):
-            for g in range(2):
-                store(
-                    (w, slice(None), slice(g * cols, (g + 1) * cols)),
-                    value[w * rows + g * half : w * rows + (g + 1) * half],
-                )
+
+        def body(i, carry):
+            at = pl.ds(pl.multiple_of(i * 4 * rows, 4 * rows), 4 * rows)
+            value = inner_rows(left[:, at], right[0])
+            for w in range(4):
+                for g in range(2):
+                    store(
+                        (4 * i + w, slice(None), slice(g * cols, (g + 1) * cols)),
+                        value[w * rows + g * half : w * rows + (g + 1) * half],
+                    )
+            return carry
+
+        lax.fori_loop(0, place.wide // 4, body, 0)
 
     return products(
         place,
@@ -527,25 +539,16 @@
         return carry
 
     lax.fori_loop(0, 3, project, 0)
-
-    def pair(p, carry):
-        at = pl.ds(pl.multiple_of(p * 2 * HEAD_DIM, 2 * HEAD_DIM), 2 * HEAD_DIM)
-        queries, keys, values = qkv_ref[0, :, at], qkv_ref[1, :, at], qkv_ref[2, :, at]
-        contexts = []
-        for h in range(2):
-            lanes = slice(h * HEAD_DIM, (h + 1) * HEAD_DIM)
-            q, k, v = queries[:, lanes], keys[:, lanes], values[:, lanes]
-            scores = jnp.where(same, inner_cols(k, q) * HEAD_DIM ** (-0.5), MASKED)
-            top = jnp.max(scores, axis=0, keepdims=True)
-            shifted = jnp.exp(scores - top)
-            total = jnp.sum(shifted, axis=0, keepdims=True)
-            probs = (shifted * (1.0 / total)).astype(BF)
-            contexts.append(inner_rows(probs, v).astype(BF))
-            lse_ref[0, pl.ds(2 * p + h, 1), :] = top + jnp.log(total)
-        ctx_ref[:, at] = jnp.concatenate(contexts, axis=1)
-        return carry
-
-    lax.fori_loop(0, GROUP // 2, pair, 0)
+    for h in range(GROUP):
+        lanes = slice(h * HEAD_DIM, (h + 1) * HEAD_DIM)
+        q, k, v = qkv_ref[0, :, lanes], qkv_ref[1, :, lanes], qkv_ref[2, :, lanes]
+        scores = jnp.where(same, inner_cols(k, q) * HEAD_DIM ** (-0.5), MASKED)
+        top = jnp.max(scores, axis=0, keepdims=True)
+        shifted = jnp.exp(scores - top)
+        total = jnp.sum(shifted, axis=0, keepdims=True)
+        probs = (shifted * (1.0 / total)).astype(BF)
+        ctx_ref[:, lanes] = inner_rows(probs, v).astype(BF)
+        lse_ref[0, h : h + 1, :] = top + jnp.log(total)
 
 
 def attend(x, w_qkv, rows, segment):
@@ -1085,9 +1088,7 @@
     whole = jnp.concatenate([whole // 32, whole % 32]).astype(BF)
 
     w_rows, in_parts = w_out.shape[1], w_in.shape[2] // w_out.shape[2]
-    swapped = swap_in_directly(place, passages, queries)
     if s == 2:
-        swapped[0], w_qkv = phase(swapped[0], w_qkv)
         towers = pick_towers(place, w_qkv, biases, norm_gains, in_bias, whole)
         got = {k: flip(towers[k], "wide", k * s) for k in (3, 2, 1)}
         levels_qkv = jnp.stack([towers[0], got[1], got[2], got[3]])
@@ -1108,18 +1109,21 @@
         layout = [(0, part, 0, part * model_width) for part in range(3)]
         shapes = [(3, w_rows, model_width)]
     out_in = jnp.concatenate([w_out, w_in], axis=2)
-    levels_qkv, swapped, out_in = phase(levels_qkv, swapped, out_in)
+    levels_qkv, out_in, parts = phase(levels_qkv, out_in, (passages, queries))
 
     pieces_qkv, plan = gather_columns(place, levels_qkv, own)
     levels_out_in = gather_levels(place, out_in)
-    pieces_qkv, levels_out_in, w_back = phase(pieces_qkv, levels_out_in, w_back)
+    swapped = swap_in_directly(place, *parts)
+    pieces_qkv, levels_out_in, w_back, swapped = phase(
+        pieces_qkv, levels_out_in, w_back, swapped
+    )
 
     cores_qkv, core_plan = gather_cores(pieces_qkv, plan)
     cores_qkv, levels_out_in, swapped = phase(cores_qkv, levels_out_in, swapped)
 
     pieces_out_in, plan = gather_columns(place, levels_out_in)
     inputs = to_row(place, passages, queries, join_swapped(place, queries, swapped))
-    inputs, w_back = phase(inputs, w_back)
+    inputs, w_back, cores_qkv = phase(inputs, w_back, cores_qkv)
     levels_back = gather_levels(place, w_back)
     made = assemble(place, cores_qkv, core_plan, layout, shapes)
     w_qkv_all = made[0]

time: 389 us -> 380 us (0.977)
    ppermute x21, waiting for transfers between devices: 33.3 us -> 8.7 us  [flip_both(): return lax.ppermute(x, BOTH, [(i, i ^ mask) for i in range(wide * narrow)])]
    ppermute x3, waiting for transfers between devices: 0.01 us -> 15.5 us  [swap_levels(): return lax.ppermute(x, 'wide', pairs)]
    all_to_all x2, waiting for transfers between devices: 2.17 us -> 8.4 us  [to_row(): mine = lax.all_to_all(four, 'narrow', 0, 0, tiled=True)]
    all_to_all x6, starting transfers between devices: 28.6 us -> 24.4 us  [across_levels(): return lax.all_to_all(x, 'wide', 0, 0, axis_index_groups=groups, tiled=True)]
  transfers between devices with their start and end apart: 63 -> 63, of which waited for: 29 -> 30; matrix products, arithmetic and copies ran while one was open for 7% -> 6% of each run, Pallas kernels for 40% -> 40%
where the time goes in v1:
time: 380 us; the launch traced here: 378 us
  Pallas kernels  162 us (43%)
  starting transfers between devices  96.5 us (25%)
  waiting for transfers between devices  81.7 us (22%)
  other arithmetic  24.1 us (6%)
  local copies, waits for them, and re-layouts  12.7 us (3%)
    ppermute x28, waiting for transfers between devices, flip(): return lax.ppermute(x, axis, [(i, i ^ mask) for i in range(size)])  40.8 us
    ppermute x21, starting transfers between devices, flip_both(): return lax.ppermute(x, BOTH, [(i, i ^ mask) for i in range(wide * narrow)])  24.6 us
    all_to_all x6, starting transfers between devices, across_levels(): return lax.all_to_all(x, 'wide', 0, 0, axis_index_groups=groups, tiled=True)  24.4 us
    ppermute x28, starting transfers between devices, flip(): return lax.ppermute(x, axis, [(i, i ^ mask) for i in range(size)])  22.7 us
    pallas_call x1, Pallas kernels, attend_back(): pl.pallas_call(attend_back_kernel, grid=(d // width,), in_specs=[pl.Block...  20.3 us
    pallas_call x2, Pallas kernels, products(): pl.pallas_call(functools.partial(product_kernel, step), grid_spec=grid_sp...  16.9 us
    pallas_call x3, Pallas kernels, column_shares(): pl.pallas_call(share_kernel, grid_spec=pltpu.PrefetchScalarGridSpec(num_s...  15.5 us
    ppermute x3, waiting for transfers between devices, swap_levels(): return lax.ppermute(x, 'wide', pairs)  15.5 us
  transfers between devices with their start and end apart: 63, of which 30 were waited for; matrix products, arithmetic and copies ran while one was open for 6% of the time, Pallas kernels for 40%

profile of v1, /device:TPU:0, one launch (start us, length us, event | category | flops | bytes accessed | tf_op | source)
XLA Modules:
  0.0 378.2 jit_solution(17278222284391184619)
XLA Ops:
  7.1 5.0 %collective-permute-start.2 = (bf16[80,768]{1,0:T(8,128)(2,1)}, bf16[80,768]{1,0:T(8,128)(2,1)S(1)}, u32[]{:S(2)}, u32[]{:S(2)}) collective-permute-start(bf16[80,768]{1,0:T(8,128)(2,1)} %get-tuple-element.192), channel_id=1, source_target_pairs={{0,24},{4,28},{8,16},{12,20},{16,8},{20,12},{24,0},{28,4},{1,25},{... | collective-permute-start | bytes 368648 | tf_op jit(solution)/shard_map/ppermute | solution.py:46
  12.8 3.8 %collective-permute-done.2 = bf16[80,768]{1,0:T(8,128)(2,1)S(1)} collective-permute-done((bf16[80,768]{1,0:T(8,128)(2,1)}, bf16[80,768]{1,0:T(8,128)(2,1)S(1)}, u32[]{:S(2)}, u32[]{:S(2)}) %collective-permute-start.2) | collective-permute-done | bytes 122912 | tf_op jit(solution)/shard_map/ppermute | solution.py:46
  16.6 6.1 %collective-permute-done.1 = bf16[80,768]{1,0:T(8,128)(2,1)S(1)} collective-permute-done((bf16[80,768]{1,0:T(8,128)(2,1)}, bf16[80,768]{1,0:T(8,128)(2,1)S(1)}, u32[]{:S(2)}, u32[]{:S(2)}) %collective-permute-start.1) | collective-permute-done | bytes 122912 | tf_op jit(solution)/shard_map/ppermute | solution.py:46
  24.8 3.7 all-to-all-start
  28.5 2.4 collective-permute-start.3
  32.1 3.9 %collective-permute-start.6 = (bf16[128,768]{1,0:T(8,128)(2,1)S(1)}, bf16[128,768]{1,0:T(8,128)(2,1)S(1)}, u32[]{:S(2)}, u32[]{:S(2)}) collective-permute-start(bf16[128,768]{1,0:T(8,128)(2,1)S(1)} %get-tuple-element.419), channel_id=1, source_target_pairs={{0,8},{8,0},{4,12},{12,4},{1,9},{9,1},{5,13},{13,5},{2,10},{10,2},... | collective-permute-start | bytes 589832 | tf_op jit(solution)/shard_map/ppermute | solution.py:68
  38.0 8.0 %collective-permute-done.6 = bf16[128,768]{1,0:T(8,128)(2,1)S(1)} collective-permute-done((bf16[128,768]{1,0:T(8,128)(2,1)S(1)}, bf16[128,768]{1,0:T(8,128)(2,1)S(1)}, u32[]{:S(2)}, u32[]{:S(2)}) %collective-permute-start.6) | collective-permute-done | bytes 196640 | tf_op jit(solution)/shard_map/ppermute | solution.py:68
  47.9 5.3 %collective-permute-done.7 = bf16[128,768]{1,0:T(8,128)(2,1)S(1)} collective-permute-done((bf16[128,768]{1,0:T(8,128)(2,1)S(1)}, bf16[128,768]{1,0:T(8,128)(2,1)S(1)}, u32[]{:S(2)}, u32[]{:S(2)}) %collective-permute-start.7) | collective-permute-done | bytes 196640 | tf_op jit(solution)/shard_map/ppermute | solution.py:68
  61.6 3.5 all-to-all-start.1
  65.2 2.9 collective-permute-start.13
  68.8 8.4 %all-to-all-done.1 = bf16[4,128,768]{2,1,0:T(8,128)(2,1)S(1)} async-done(((bf16[4,128,768]{2,1,0:T(8,128)(2,1)}), bf16[4,128,768]{2,1,0:T(8,128)(2,1)S(1)}, u32[]{:S(2)}, u32[]{:S(2)}) %all-to-all-start.1) | async-done | bytes 786464 | tf_op jit(solution)/shard_map/all_to_all | solution.py:107
  77.2 5.4 %shard_map.239 = (bf16[3,32,24,768]{3,2,1,0:T(8,128)(2,1)}, bf16[1,32,8,768]{3,2,1,0:T(8,128)(2,1)}) custom-call(s32[1]{0:T(128)} %bitcast.21.me_ref, bf16[4,80,768]{2,1,0:T(8,128)(2,1)} %copy-done.5, bf16[4,80,768]{2,1,0:T(8,128)(2,1)} %copy-done.11, bf16[4,80,768]{2,1,0:T(8,128)(2,1)} %copy-done.12, bf16[4,80,768]{2,1,0:T(8,128)(2,1)} %collective-permute-done.5.refs_3_, ...), custom_call_target="tpu_custom_call" | custom-call | flops 115000000 | bytes 1024 | tf_op jit(solution)/shard_map/pallas_call | solution.py:157
  84.7 3.5 all-to-all-start.2
  91.9 13.3 %shard_map.241 = (bf16[3,512,768]{2,1,0:T(8,128)(2,1)}, bf16[512,768]{1,0:T(8,128)(2,1)}, f32[3,4,512]{2,1,0:T(4,128)}) custom-call(bf16[512,768]{1,0:T(8,128)(2,1)} %bitcast.112, bf16[3,768,768]{2,1,0:T(8,128)(2,1)} %bitcast.110, f32[8,768]{1,0:T(8,128)} %get-tuple-element.228.rows_ref.rows, s32[1,512]{1,0:T(1,128)} %bitcast.136, s32[512,1]{1,0:T(8,128)} %copy.58.seg_col_ref), custom_call_target="tpu_custom_call" | custom-call | flops 115000000 | bytes 1024 | tf_op jit(solution)/shard_map/pallas_call | solution.py:558
  105.2 3.3 collective-permute-done.14.refs_2_
  118.9 3.5 all-to-all-start.3
  122.4 6.7 %shard_map.242 = (bf16[1,32,24,768]{3,2,1,0:T(8,128)(2,1)}, bf16[4,32,24,768]{3,2,1,0:T(8,128)(2,1)}) custom-call(s32[1]{0:T(128)} %bitcast.21.me_ref, bf16[4,24,3840]{2,1,0:T(8,128)(2,1)} %copy-done.1, bf16[4,24,3840]{2,1,0:T(8,128)(2,1)} %copy-done.9, bf16[4,24,3840]{2,1,0:T(8,128)(2,1)} %collective-permute-done.14.refs_2_, ...), custom_call_target="tpu_custom_call" | custom-call | flops 115000000 | bytes 1024 | tf_op jit(solution)/shard_map/pallas_call | solution.py:157
  129.1 5.8 %shard_map.243 = (f32[512,768]{1,0:T(8,128)}, bf16[512,768]{1,0:T(8,128)(2,1)}, f32[512,768]{1,0:T(8,128)}, f32[512,1]{1,0:T(8,128)}, f32[2,128]{1,0:T(2,128)}) custom-call(bf16[512,768]{1,0:T(8,128)(2,1)} %get-tuple-element.232.ctx.refs_0_, bf16[1,768,768]{2,1,0:T(8,128)(2,1)} %bitcast.144, bf16[512,768]{1,0:T(8,128)(2,1)} %bitcast.113, ...), custom_call_target="tpu_custom_call" | custom-call | flops 5750000128 | bytes 1024 | tf_op jit(solution)/shard_map/pallas_call | solution.py:762
  134.9 9.2 %shard_map.244 = (bf16[512,3072]{1,0:T(8,128)(2,1)}, bf16[512,3072]{1,0:T(8,128)(2,1)}) custom-call(bf16[512,768]{1,0:T(8,128)(2,1)} %get-tuple-element.249.x_ref.refs_2_, bf16[4,768,768]{2,1,0:T(8,128)(2,1)} %bitcast.142, f32[1,3072]{1,0:T(1,128)} %get-tuple-element.251.bias_ref), custom_call_target="tpu_custom_call" | custom-call | flops 9200000000 | bytes 1024 | tf_op jit(solution)/shard_map/pallas_call | solution.py:679
  147.0 3.7 all-to-all-start.4
  150.7 12.9 %shard_map.245 = (bf16[512,768]{1,0:T(8,128)(2,1)}, f32[512,768]{1,0:T(8,128)}, f32[512,1]{1,0:T(8,128)}, bf16[32,768]{1,0:T(8,128)(2,1)}, f32[3,128]{1,0:T(4,128)}, /*index=5*/bf16[3072,768]{1,0:T(8,128)(2,1)}) custom-call(s32[1]{0:T(128)} %bitcast.21.me_ref, bf16[512,3072]{1,0:T(8,128)(2,1)} %get-tuple-element.256.active.left_ref, ...), custom_call_target="tpu_custom_call" | custom-call | flops 10350000128 | bytes 1024 | tf_op jit(solution)/shard_map/pallas_call | solution.py:828
  168.2 3.7 collective-permute-done.28
  175.0 2.8 collective-permute-start.30
  184.4 2.6 shard_map.246.pool
  187.0 3.5 all-to-all-start.5
  190.5 6.1 %shard_map.247 = (f32[512,768]{1,0:T(8,128)}, bf16[512,768]{1,0:T(8,128)(2,1)}, f32[3,768]{1,0:T(4,128)}) custom-call(bf16[512,768]{1,0:T(8,128)(2,1)} %bitcast.120, f32[512,1]{1,0:T(8,128)} %compare_convert_fusion.valid, f32[32,512]{1,0:T(8,128)} %fusion.14.hot, f32[32,768]{1,0:T(8,128)} %shard_map.246.pool, f32[512,768]{1,0:T(8,128)} %get-tuple-element.268.unit, ...), custom_call_target="tpu_custom_call" | custom-call | flops 6899999744 | bytes 1024 | tf_op jit(solution)/shard_map/pallas_call | solution.py:867
  196.6 9.0 %shard_map.248 = (bf16[2,8,192,384]{3,2,1,0:T(8,128)(2,1)}, bf16[2,8,192,384]{3,2,1,0:T(8,128)(2,1)}) custom-call(s32[1]{0:T(128)} %bitcast.34.core_ref, bf16[512,3072]{1,0:T(8,128)(2,1)} %get-tuple-element.256.active.left_ref, bf16[512,768]{1,0:T(8,128)(2,1)} %get-tuple-element.279.right_ref.low), custom_call_target="tpu_custom_call" | custom-call | flops 8049999872 | bytes 1024 | tf_op jit(solution)/shard_map/pallas_call | solution.py:421
  207.6 3.5 all-to-all-start.6
  211.2 5.1 %shard_map.249 = (f32[4,192,384]{2,1,0:T(8,128)}, bf16[4,192,384]{2,1,0:T(8,128)(2,1)}, bf16[4,192,384]{2,1,0:T(8,128)(2,1)}, bf16[4,192,384]{2,1,0:T(8,128)(2,1)}) custom-call(s32[2]{0:T(128)} %pad_add_fusion.1.at_ref, bf16[2,4,2,192,384]{4,3,2,1,0:T(8,128)(2,1)} %bitcast.116, bf16[2,4,2,192,384]{4,3,2,1,0:T(8,128)(2,1)} %bitcast.46.got_ref), custom_call_target="tpu_custom_call" | custom-call | flops 1150000000 | bytes 1024 | tf_op jit(solution)/shard_map/pallas_call | solution.py:291
  219.8 14.4 %shard_map.250 = (bf16[512,3072]{1,0:T(8,128)(2,1)}, f32[1,3072]{1,0:T(1,128)}, f32[512,768]{1,0:T(8,128)}, bf16[512,768]{1,0:T(8,128)(2,1)}, bf16[4,512,192]{2,1,0:T(8,128)(2,1)}, /*index=5*/f32[3,768]{1,0:T(4,128)}) custom-call(bf16[512,768]{1,0:T(8,128)(2,1)} %get-tuple-element.279.right_ref.low, bf16[3072,768]{1,0:T(8,128)(2,1)} %get-tuple-element.280.w_back, ...), custom_call_target="tpu_custom_call" | custom-call | flops 16099999744 | bytes 1024 | tf_op jit(solution)/shard_map/pallas_call | solution.py:915
  234.1 9.3 %shard_map.251 = (bf16[2,8,120,768]{3,2,1,0:T(8,128)(2,1)}, bf16[2,8,120,768]{3,2,1,0:T(8,128)(2,1)}) custom-call(s32[1]{0:T(128)} %bitcast.me_ref, bf16[512,768]{1,0:T(8,128)(2,1)} %get-tuple-element.232.ctx.refs_0_, bf16[4,512,192]{2,1,0:T(8,128)(2,1)} %get-tuple-element.285.refs_1_, bf16[512,768]{1,0:T(8,128)(2,1)} %get-tuple-element.249.x_ref.refs_2_, ...), custom_call_target="tpu_custom_call" | custom-call | flops 9200000000 | bytes 1024 | tf_op jit(solution)/shard_map/pallas_call | solution.py:380
  246.1 2.8 shard_map.253
  251.0 5.7 %shard_map.252 = (f32[4,120,768]{2,1,0:T(8,128)}, bf16[4,120,768]{2,1,0:T(8,128)(2,1)}, bf16[4,120,768]{2,1,0:T(8,128)(2,1)}, bf16[4,120,768]{2,1,0:T(8,128)(2,1)}) custom-call(s32[2]{0:T(128)} %pad_add_fusion.1.at_ref, bf16[2,4,2,120,768]{4,3,2,1,0:T(8,128)(2,1)} %bitcast.115, bf16[2,4,2,120,768]{4,3,2,1,0:T(8,128)(2,1)} %bitcast.49.got_ref), custom_call_target="tpu_custom_call" | custom-call | flops 1150000000 | bytes 1024 | tf_op jit(solution)/shard_map/pallas_call | solution.py:291
  260.2 4.8 %all-to-all-start.7 = ((bf16[4,192,384]{2,1,0:T(8,128)(2,1)}), bf16[4,192,384]{2,1,0:T(8,128)(2,1)S(1)}, u32[]{:S(2)}, u32[]{:S(2)}) async-start(bf16[4,192,384]{2,1,0:T(8,128)(2,1)} %shard_map.253), calls=%async_computation.7 | async-start | bytes 1179648 | tf_op jit(solution)/shard_map/all_to_all | solution.py:61
  265.0 20.3 %shard_map.254 = (bf16[3,512,768]{2,1,0:T(8,128)(2,1)}, bf16[4,512,576]{2,1,0:T(8,128)(2,1)}, f32[2,768]{1,0:T(2,128)}) custom-call(bf16[512,768]{1,0:T(8,128)(2,1)} %get-tuple-element.305.gb_ref, bf16[768,768]{1,0:T(8,128)(2,1)} %bitcast.145, bf16[3,512,768]{2,1,0:T(8,128)(2,1)} %get-tuple-element.306.qkv_ref, f32[3,4,512]{2,1,0:T(4,128)} %get-tuple-element.307.lse_ref, ...), custom_call_target="tpu_custom_call" | custom-call | flops 23000000512 | bytes 1024 | tf_op jit(solution)/shard_map/pallas_call | solution.py:633
  285.3 7.6 %shard_map.255 = (bf16[2,8,48,1152]{3,2,1,0:T(8,128)(2,1)}, bf16[2,8,48,1152]{3,2,1,0:T(8,128)(2,1)}) custom-call(s32[1]{0:T(128)} %bitcast.me_ref, bf16[512,768]{1,0:T(8,128)(2,1)} %bitcast.114, bf16[4,512,576]{2,1,0:T(8,128)(2,1)} %get-tuple-element.308.refs_1_), custom_call_target="tpu_custom_call" | custom-call | flops 9200000000 | bytes 1024 | tf_op jit(solution)/shard_map/pallas_call | solution.py:380
  293.1 6.5 %shard_map.256 = bf16[512,768]{1,0:T(8,128)(2,1)} custom-call(bf16[3,512,768]{2,1,0:T(8,128)(2,1)} %get-tuple-element.318.grad, bf16[3,768,768]{2,1,0:T(8,128)(2,1)} %bitcast.111, f32[512,768]{1,0:T(8,128)} %get-tuple-element.319.residual), custom_call_target="tpu_custom_call" | custom-call | flops 6899999744 | bytes 1024 | tf_op jit(solution)/shard_map/pallas_call | solution.py:952
  299.5 3.5 all-to-all-start.8
  303.9 3.1 shard_map.258
  312.2 4.7 %shard_map.257 = (f32[4,48,1152]{2,1,0:T(8,128)}, bf16[4,48,1152]{2,1,0:T(8,128)(2,1)}, bf16[4,48,1152]{2,1,0:T(8,128)(2,1)}, bf16[4,48,1152]{2,1,0:T(8,128)(2,1)}) custom-call(s32[2]{0:T(128)} %pad_add_fusion.1.at_ref, bf16[2,4,2,48,1152]{4,3,2,1,0:T(8,128)(2,1)} %bitcast.147, bf16[2,4,2,48,1152]{4,3,2,1,0:T(8,128)(2,1)} %bitcast.52.got_ref), custom_call_target="tpu_custom_call" | custom-call | flops 1150000000 | bytes 1024 | tf_op jit(solution)/shard_map/pallas_call | solution.py:291
  318.0 7.6 %collective-permute-done.44 = bf16[120,768]{1,0:T(8,128)(2,1)S(1)} collective-permute-done((bf16[120,768]{1,0:T(8,128)(2,1)}, bf16[120,768]{1,0:T(8,128)(2,1)S(1)}, u32[]{:S(2)}, u32[]{:S(2)}) %collective-permute-start.44) | collective-permute-done | bytes 184352 | tf_op jit(solution)/shard_map/ppermute | solution.py:46
  330.7 5.4 %all-to-all-start.9 = ((bf16[4,128,768]{2,1,0:T(8,128)(2,1)}), bf16[4,128,768]{2,1,0:T(8,128)(2,1)S(1)}, u32[]{:S(2)}, u32[]{:S(2)}) async-start(bf16[4,128,768]{2,1,0:T(8,128)(2,1)} %broadcast_select_fusion), calls=%async_computation.9 | async-start | bytes 1572864 | tf_op jit(solution)/shard_map/all_to_all | solution.py:61
  340.3 4.7 %shard_map.259 = f32[32,384]{1,0:T(8,128)} custom-call(f32[2,768]{1,0:T(2,128)} %get-tuple-element.345.attn, f32[3,768]{1,0:T(4,128)} %get-tuple-element.346.out, f32[3,768]{1,0:T(4,128)} %get-tuple-element.347.ffn, f32[1,3072]{1,0:T(1,128)} %get-tuple-element.348.inb, f32[2,128]{1,0:T(2,128)} %get-tuple-element.349.stats_a, f32[3,128]{1,0:T(4,128)} %get-tuple-element.350.stats_b), custom_call_target="tpu_custom_call" | custom-call | flops 4600000000 | bytes 1024 | tf_op jit(solution)/shard_map/pallas_call | solution.py:1036
  347.1 7.8 %all-to-all-done.9 = bf16[4,128,768]{2,1,0:T(8,128)(2,1)S(1)} async-done(((bf16[4,128,768]{2,1,0:T(8,128)(2,1)}), bf16[4,128,768]{2,1,0:T(8,128)(2,1)S(1)}, u32[]{:S(2)}, u32[]{:S(2)}) %all-to-all-start.9) | async-done | bytes 786464 | tf_op jit(solution)/shard_map/all_to_all | solution.py:61
  357.2 3.0 all-to-all-start.10
  360.1 2.4 shard_map.260
  364.3 2.4 collective-permute-start.50
  370.4 5.7 %collective-permute-done.50 = bf16[48,1152]{1,0:T(8,128)(2,1)S(1)} collective-permute-done((bf16[48,1152]{1,0:T(8,128)(2,1)}, bf16[48,1152]{1,0:T(8,128)(2,1)S(1)}, u32[]{:S(2)}, u32[]{:S(2)}) %collective-permute-start.50) | collective-permute-done | bytes 110624 | tf_op jit(solution)/shard_map/ppermute | solution.py:46
  (261 shorter events, 98.2 us)
Async XLA Ops:
  7.1 9.5 %collective-permute-start.2 = (bf16[80,768]{1,0:T(8,128)(2,1)}, bf16[80,768]{1,0:T(8,128)(2,1)S(1)}, u32[]{:S(2)}, u32[]{:S(2)}) collective-permute-start(bf16[80,768]{1,0:T(8,128)(2,1)} %get-tuple-element.192), channel_id=1, source_target_pairs={{0,24},{4,28},{8,16},{12,20},{16,8},{20,12},{24,0},{28,4},{1,25},{... | collective-permute-start | bytes 368648 | tf_op jit(solution)/shard_map/ppermute | solution.py:46
  12.2 10.6 %collective-permute-start.1 = (bf16[80,768]{1,0:T(8,128)(2,1)}, bf16[80,768]{1,0:T(8,128)(2,1)S(1)}, u32[]{:S(2)}, u32[]{:S(2)}) collective-permute-start(bf16[80,768]{1,0:T(8,128)(2,1)} %get-tuple-element.191), channel_id=1, source_target_pairs={{0,16},{4,20},{8,24},{12,28},{16,0},{20,4},{24,8},{28,12},{1,17},{... | collective-permute-start | bytes 368648 | tf_op jit(solution)/shard_map/ppermute | solution.py:46
  12.2 10.6 %collective-permute-start = (bf16[80,768]{1,0:T(8,128)(2,1)}, bf16[80,768]{1,0:T(8,128)(2,1)S(1)}, u32[]{:S(2)}, u32[]{:S(2)}) collective-permute-start(bf16[80,768]{1,0:T(8,128)(2,1)} %get-tuple-element.190), channel_id=1, source_target_pairs={{0,8},{4,12},{8,0},{12,4},{16,24},{20,28},{24,16},{28,20},{1,9},{5... | collective-permute-start | bytes 368648 | tf_op jit(solution)/shard_map/ppermute | solution.py:46
  24.8 31.4 %all-to-all-start = ((bf16[4,24,3840]{2,1,0:T(8,128)(2,1)}), bf16[4,24,3840]{2,1,0:T(8,128)(2,1)S(1)}, u32[]{:S(2)}, u32[]{:S(2)}) async-start(bf16[4,24,3840]{2,1,0:T(8,128)(2,1)} %broadcast_select_fusion.2), calls=%async_computation | async-start | bytes 1474560 | tf_op jit(solution)/shard_map/all_to_all | solution.py:61
  28.5 26.8 %collective-permute-start.3 = (bf16[4,80,768]{2,1,0:T(8,128)(2,1)S(1)}, bf16[4,80,768]{2,1,0:T(8,128)(2,1)S(1)}, u32[]{:S(2)}, u32[]{:S(2)}) collective-permute-start(bf16[4,80,768]{2,1,0:T(8,128)(2,1)S(1)} %pad_maximum_fusion.2.refs_0_), channel_id=1, source_target_pairs={{0,6},{1,7},{2,4},{3,5},{4,2},{5,3},{6,0},{7,1},{8,14},{9,15},{10,... | collective-permute-start | bytes 1474568 | tf_op jit(solution)/shard_map/ppermute | solution.py:52
  31.0 24.4 %collective-permute-start.4 = (bf16[4,80,768]{2,1,0:T(8,128)(2,1)S(1)}, bf16[4,80,768]{2,1,0:T(8,128)(2,1)S(1)}, u32[]{:S(2)}, u32[]{:S(2)}) collective-permute-start(bf16[4,80,768]{2,1,0:T(8,128)(2,1)S(1)} %pad_maximum_fusion.2.refs_0_), channel_id=1, source_target_pairs={{0,2},{1,3},{2,0},{3,1},{4,6},{5,7},{6,4},{7,5},{8,10},{9,11},{10,... | collective-permute-start | bytes 1474568 | tf_op jit(solution)/shard_map/ppermute | solution.py:52
  31.5 24.6 %collective-permute-start.5 = (bf16[4,80,768]{2,1,0:T(8,128)(2,1)S(1)}, bf16[4,80,768]{2,1,0:T(8,128)(2,1)}, u32[]{:S(2)}, u32[]{:S(2)}) collective-permute-start(bf16[4,80,768]{2,1,0:T(8,128)(2,1)S(1)} %pad_maximum_fusion.2.refs_0_), channel_id=1, source_target_pairs={{0,4},{1,5},{2,6},{3,7},{4,0},{5,1},{6,2},{7,3},{8,12},{9,13},{10,... | collective-permute-start | bytes 1474568 | tf_op jit(solution)/shard_map/ppermute | solution.py:52
  32.1 13.9 %collective-permute-start.6 = (bf16[128,768]{1,0:T(8,128)(2,1)S(1)}, bf16[128,768]{1,0:T(8,128)(2,1)S(1)}, u32[]{:S(2)}, u32[]{:S(2)}) collective-permute-start(bf16[128,768]{1,0:T(8,128)(2,1)S(1)} %get-tuple-element.419), channel_id=1, source_target_pairs={{0,8},{8,0},{4,12},{12,4},{1,9},{9,1},{5,13},{13,5},{2,10},{10,2},... | collective-permute-start | bytes 589832 | tf_op jit(solution)/shard_map/ppermute | solution.py:68
  36.0 17.2 %collective-permute-start.7 = (bf16[128,768]{1,0:T(8,128)(2,1)S(1)}, bf16[128,768]{1,0:T(8,128)(2,1)S(1)}, u32[]{:S(2)}, u32[]{:S(2)}) collective-permute-start(bf16[128,768]{1,0:T(8,128)(2,1)S(1)} %get-tuple-element.418), channel_id=1, source_target_pairs={{0,16},{16,0},{4,20},{20,4},{1,17},{17,1},{5,21},{21,5},{2,18},{18... | collective-permute-start | bytes 589832 | tf_op jit(solution)/shard_map/ppermute | solution.py:68
  46.0 9.3 %collective-permute-start.8 = (bf16[128,768]{1,0:T(8,128)(2,1)S(1)}, bf16[128,768]{1,0:T(8,128)(2,1)S(1)}, u32[]{:S(2)}, u32[]{:S(2)}) collective-permute-start(bf16[128,768]{1,0:T(8,128)(2,1)S(1)} %get-tuple-element.417), channel_id=1, source_target_pairs={{0,24},{24,0},{4,28},{28,4},{1,25},{25,1},{5,29},{29,5},{2,26},{26... | collective-permute-start | bytes 589832 | tf_op jit(solution)/shard_map/ppermute | solution.py:68
  61.6 15.6 %all-to-all-start.1 = ((bf16[4,128,768]{2,1,0:T(8,128)(2,1)}), bf16[4,128,768]{2,1,0:T(8,128)(2,1)S(1)}, u32[]{:S(2)}, u32[]{:S(2)}) async-start(bf16[4,128,768]{2,1,0:T(8,128)(2,1)} %maximum_select_fusion), calls=%async_computation.1 | async-start | bytes 1572864 | tf_op jit(solution)/shard_map/all_to_all | solution.py:107
  65.2 39.9 %collective-permute-start.13 = (bf16[4,24,3840]{2,1,0:T(8,128)(2,1)S(1)}, bf16[4,24,3840]{2,1,0:T(8,128)(2,1)S(1)}, u32[]{:S(2)}, u32[]{:S(2)}) collective-permute-start(bf16[4,24,3840]{2,1,0:T(8,128)(2,1)S(1)} %all-to-all-done.refs_0_), channel_id=1, source_target_pairs={{0,6},{1,7},{2,4},{3,5},{4,2},{5,3},{6,0},{7,1},{8,14},{9,15},{10,... | collective-permute-start | bytes 2211848 | tf_op jit(solution)/shard_map/ppermute | solution.py:52
  68.2 40.3 %collective-permute-start.14 = (bf16[4,24,3840]{2,1,0:T(8,128)(2,1)S(1)}, bf16[4,24,3840]{2,1,0:T(8,128)(2,1)}, u32[]{:S(2)}, u32[]{:S(2)}) collective-permute-start(bf16[4,24,3840]{2,1,0:T(8,128)(2,1)S(1)} %all-to-all-done.refs_0_), channel_id=1, source_target_pairs={{0,2},{1,3},{2,0},{3,1},{4,6},{5,7},{6,4},{7,5},{8,10},{9,11},{10,... | collective-permute-start | bytes 2211848 | tf_op jit(solution)/shard_map/ppermute | solution.py:52
  68.3 40.2 %collective-permute-start.15 = (bf16[4,24,3840]{2,1,0:T(8,128)(2,1)S(1)}, bf16[4,24,3840]{2,1,0:T(8,128)(2,1)}, u32[]{:S(2)}, u32[]{:S(2)}) collective-permute-start(bf16[4,24,3840]{2,1,0:T(8,128)(2,1)S(1)} %all-to-all-done.refs_0_), channel_id=1, source_target_pairs={{0,4},{1,5},{2,6},{3,7},{4,0},{5,1},{6,2},{7,3},{8,12},{9,13},{10,... | collective-permute-start | bytes 2211848 | tf_op jit(solution)/shard_map/ppermute | solution.py:52
  84.7 23.8 %all-to-all-start.2 = ((bf16[4,96,768]{2,1,0:T(8,128)(2,1)}), bf16[4,96,768]{2,1,0:T(8,128)(2,1)S(1)}, u32[]{:S(2)}, u32[]{:S(2)}) async-start(bf16[4,96,768]{2,1,0:T(8,128)(2,1)} %broadcast_select_fusion.3), calls=%async_computation.2 | async-start | bytes 1179648 | tf_op jit(solution)/shard_map/all_to_all | solution.py:61
  114.3 29.8 %collective-permute-start.20 = (bf16[4,96,768]{2,1,0:T(8,128)(2,1)S(1)}, bf16[4,96,768]{2,1,0:T(8,128)(2,1)S(1)}, u32[]{:S(2)}, u32[]{:S(2)}) collective-permute-start(bf16[4,96,768]{2,1,0:T(8,128)(2,1)S(1)} %all-to-all-done.2.refs_0_), channel_id=1, source_target_pairs={{0,6},{1,7},{2,4},{3,5},{4,2},{5,3},{6,0},{7,1},{8,14},{9,15},{10,... | collective-permute-start | bytes 1769480 | tf_op jit(solution)/shard_map/ppermute | solution.py:52
  115.6 28.5 %collective-permute-start.21 = (bf16[4,96,768]{2,1,0:T(8,128)(2,1)S(1)}, bf16[4,96,768]{2,1,0:T(8,128)(2,1)}, u32[]{:S(2)}, u32[]{:S(2)}) collective-permute-start(bf16[4,96,768]{2,1,0:T(8,128)(2,1)S(1)} %all-to-all-done.2.refs_0_), channel_id=1, source_target_pairs={{0,2},{1,3},{2,0},{3,1},{4,6},{5,7},{6,4},{7,5},{8,10},{9,11},{10,... | collective-permute-start | bytes 1769480 | tf_op jit(solution)/shard_map/ppermute | solution.py:52
  117.3 26.8 %collective-permute-start.22 = (bf16[4,96,768]{2,1,0:T(8,128)(2,1)S(1)}, bf16[4,96,768]{2,1,0:T(8,128)(2,1)}, u32[]{:S(2)}, u32[]{:S(2)}) collective-permute-start(bf16[4,96,768]{2,1,0:T(8,128)(2,1)S(1)} %all-to-all-done.2.refs_0_), channel_id=1, source_target_pairs={{0,4},{1,5},{2,6},{3,7},{4,0},{5,1},{6,2},{7,3},{8,12},{9,13},{10,... | collective-permute-start | bytes 1769480 | tf_op jit(solution)/shard_map/ppermute | solution.py:52
  118.9 25.3 %all-to-all-start.3 = ((bf16[4,128,768]{2,1,0:T(8,128)(2,1)}), bf16[4,128,768]{2,1,0:T(8,128)(2,1)S(1)}, u32[]{:S(2)}, u32[]{:S(2)}) async-start(bf16[4,128,768]{2,1,0:T(8,128)(2,1)} %maximum_select_fusion.1), calls=%async_computation.3 | async-start | bytes 1572864 | tf_op jit(solution)/shard_map/all_to_all | solution.py:61
  144.2 6.5 %collective-permute-start.23 = (bf16[4,96,768]{2,1,0:T(8,128)(2,1)S(1)}, bf16[4,96,768]{2,1,0:T(8,128)(2,1)}, u32[]{:S(2)}, u32[]{:S(2)}) collective-permute-start(bf16[4,96,768]{2,1,0:T(8,128)(2,1)S(1)} %all-to-all-done.2.refs_0_), channel_id=1, source_target_pairs={{0,1},{1,0},{2,3},{3,2},{4,5},{5,4},{6,7},{7,6},{8,9},{9,8},{10,11... | collective-permute-start | bytes 1769480 | tf_op jit(solution)/shard_map/ppermute | solution.py:46
  144.2 6.5 %collective-permute-start.24 = (bf16[4,96,768]{2,1,0:T(8,128)(2,1)S(1)}, bf16[4,96,768]{2,1,0:T(8,128)(2,1)}, u32[]{:S(2)}, u32[]{:S(2)}) collective-permute-start(bf16[4,96,768]{2,1,0:T(8,128)(2,1)S(1)} %collective-permute-done.20.refs_1_), channel_id=1, source_target_pairs={{0,1},{1,0},{2,3},{3,2},{4,5},{5,4},{6,7},{7,6},{8,9},{9,8},{10,11... | collective-permute-start | bytes 1769480 | tf_op jit(solution)/shard_map/ppermute | solution.py:46
  144.7 6.0 %collective-permute-start.25 = (bf16[4,96,768]{2,1,0:T(8,128)(2,1)}, bf16[4,96,768]{2,1,0:T(8,128)(2,1)}, u32[]{:S(2)}, u32[]{:S(2)}) collective-permute-start(bf16[4,96,768]{2,1,0:T(8,128)(2,1)} %collective-permute-done.21.refs_2_), channel_id=1, source_target_pairs={{0,1},{1,0},{2,3},{3,2},{4,5},{5,4},{6,7},{7,6},{8,9},{9,8},{10,11... | collective-permute-start | bytes 1769480 | tf_op jit(solution)/shard_map/ppermute | solution.py:46
  144.8 5.9 %collective-permute-start.26 = (bf16[4,96,768]{2,1,0:T(8,128)(2,1)}, bf16[4,96,768]{2,1,0:T(8,128)(2,1)}, u32[]{:S(2)}, u32[]{:S(2)}) collective-permute-start(bf16[4,96,768]{2,1,0:T(8,128)(2,1)} %collective-permute-done.22.refs_3_), channel_id=1, source_target_pairs={{0,1},{1,0},{2,3},{3,2},{4,5},{5,4},{6,7},{7,6},{8,9},{9,8},{10,11... | collective-permute-start | bytes 1769480 | tf_op jit(solution)/shard_map/ppermute | solution.py:46
  147.0 16.6 %all-to-all-start.4 = ((bf16[4,128,768]{2,1,0:T(8,128)(2,1)}), bf16[4,128,768]{2,1,0:T(8,128)(2,1)S(1)}, u32[]{:S(2)}, u32[]{:S(2)}) async-start(bf16[4,128,768]{2,1,0:T(8,128)(2,1)} %maximum_select_fusion.2), calls=%async_computation.4 | async-start | bytes 1572864 | tf_op jit(solution)/shard_map/all_to_all | solution.py:107
  165.7 6.2 %collective-permute-start.28 = (bf16[32,768]{1,0:T(8,128)(2,1)}, bf16[32,768]{1,0:T(8,128)(2,1)S(1)}, u32[]{:S(2)}, u32[]{:S(2)}) collective-permute-start(bf16[32,768]{1,0:T(8,128)(2,1)} %get-tuple-element.265), channel_id=1, source_target_pairs={{0,16},{4,20},{8,24},{12,28},{16,0},{20,4},{24,8},{28,12},{1,17},{... | collective-permute-start | bytes 147464 | tf_op jit(solution)/shard_map/ppermute | solution.py:46
  168.0 6.1 %collective-permute-start.27 = (bf16[32,768]{1,0:T(8,128)(2,1)}, bf16[32,768]{1,0:T(8,128)(2,1)S(1)}, u32[]{:S(2)}, u32[]{:S(2)}) collective-permute-start(bf16[32,768]{1,0:T(8,128)(2,1)} %get-tuple-element.265), channel_id=1, source_target_pairs={{0,24},{4,28},{8,16},{12,20},{16,8},{20,12},{24,0},{28,4},{1,25},{... | collective-permute-start | bytes 147464 | tf_op jit(solution)/shard_map/ppermute | solution.py:46
  187.0 18.6 %all-to-all-start.5 = ((bf16[4,128,768]{2,1,0:T(8,128)(2,1)}), bf16[4,128,768]{2,1,0:T(8,128)(2,1)S(1)}, u32[]{:S(2)}, u32[]{:S(2)}) async-start(bf16[4,128,768]{2,1,0:T(8,128)(2,1)} %bitcast.45), calls=%async_computation.5 | async-start | bytes 1572864 | tf_op jit(solution)/shard_map/all_to_all | solution.py:112
  207.6 35.7 %all-to-all-start.6 = ((bf16[4,128,768]{2,1,0:T(8,128)(2,1)}), bf16[4,128,768]{2,1,0:T(8,128)(2,1)S(1)}, u32[]{:S(2)}, u32[]{:S(2)}) async-start(bf16[4,128,768]{2,1,0:T(8,128)(2,1)} %broadcast_select_fusion.1), calls=%async_computation.6 | async-start | bytes 1572864 | tf_op jit(solution)/shard_map/all_to_all | solution.py:61
  216.3 27.1 %collective-permute-start.35 = (bf16[4,192,384]{2,1,0:T(8,128)(2,1)}, bf16[4,192,384]{2,1,0:T(8,128)(2,1)S(1)}, u32[]{:S(2)}, u32[]{:S(2)}) collective-permute-start(bf16[4,192,384]{2,1,0:T(8,128)(2,1)} %get-tuple-element.289), channel_id=1, source_target_pairs={{0,6},{1,7},{2,4},{3,5},{4,2},{5,3},{6,0},{7,1},{8,14},{9,15},{10,... | collective-permute-start | bytes 1769480 | tf_op jit(solution)/shard_map/ppermute | solution.py:52
  217.9 26.8 %collective-permute-start.36 = (bf16[4,192,384]{2,1,0:T(8,128)(2,1)}, bf16[4,192,384]{2,1,0:T(8,128)(2,1)S(1)}, u32[]{:S(2)}, u32[]{:S(2)}) collective-permute-start(bf16[4,192,384]{2,1,0:T(8,128)(2,1)} %get-tuple-element.290), channel_id=1, source_target_pairs={{0,2},{1,3},{2,0},{3,1},{4,6},{5,7},{6,4},{7,5},{8,10},{9,11},{10,... | collective-permute-start | bytes 1769480 | tf_op jit(solution)/shard_map/ppermute | solution.py:52
  218.2 27.1 %collective-permute-start.37 = (bf16[4,192,384]{2,1,0:T(8,128)(2,1)}, bf16[4,192,384]{2,1,0:T(8,128)(2,1)S(1)}, u32[]{:S(2)}, u32[]{:S(2)}) collective-permute-start(bf16[4,192,384]{2,1,0:T(8,128)(2,1)} %get-tuple-element.291), channel_id=1, source_target_pairs={{0,4},{1,5},{2,6},{3,7},{4,0},{5,1},{6,2},{7,3},{8,12},{9,13},{10,... | collective-permute-start | bytes 1769480 | tf_op jit(solution)/shard_map/ppermute | solution.py:52
  256.7 36.2 %collective-permute-start.39 = (bf16[4,120,768]{2,1,0:T(8,128)(2,1)}, bf16[4,120,768]{2,1,0:T(8,128)(2,1)S(1)}, u32[]{:S(2)}, u32[]{:S(2)}) collective-permute-start(bf16[4,120,768]{2,1,0:T(8,128)(2,1)} %get-tuple-element.313), channel_id=1, source_target_pairs={{0,6},{1,7},{2,4},{3,5},{4,2},{5,3},{6,0},{7,1},{8,14},{9,15},{10,... | collective-permute-start | bytes 2211848 | tf_op jit(solution)/shard_map/ppermute | solution.py:52
  258.8 34.1 %collective-permute-start.40 = (bf16[4,120,768]{2,1,0:T(8,128)(2,1)}, bf16[4,120,768]{2,1,0:T(8,128)(2,1)}, u32[]{:S(2)}, u32[]{:S(2)}) collective-permute-start(bf16[4,120,768]{2,1,0:T(8,128)(2,1)} %get-tuple-element.314), channel_id=1, source_target_pairs={{0,2},{1,3},{2,0},{3,1},{4,6},{5,7},{6,4},{7,5},{8,10},{9,11},{10,... | collective-permute-start | bytes 2211848 | tf_op jit(solution)/shard_map/ppermute | solution.py:52
  259.0 34.0 %collective-permute-start.41 = (bf16[4,120,768]{2,1,0:T(8,128)(2,1)}, bf16[4,120,768]{2,1,0:T(8,128)(2,1)}, u32[]{:S(2)}, u32[]{:S(2)}) collective-permute-start(bf16[4,120,768]{2,1,0:T(8,128)(2,1)} %get-tuple-element.315), channel_id=1, source_target_pairs={{0,4},{1,5},{2,6},{3,7},{4,0},{5,1},{6,2},{7,3},{8,12},{9,13},{10,... | collective-permute-start | bytes 2211848 | tf_op jit(solution)/shard_map/ppermute | solution.py:52
  260.2 32.7 %all-to-all-start.7 = ((bf16[4,192,384]{2,1,0:T(8,128)(2,1)}), bf16[4,192,384]{2,1,0:T(8,128)(2,1)S(1)}, u32[]{:S(2)}, u32[]{:S(2)}) async-start(bf16[4,192,384]{2,1,0:T(8,128)(2,1)} %shard_map.253), calls=%async_computation.7 | async-start | bytes 1179648 | tf_op jit(solution)/shard_map/all_to_all | solution.py:61
  293.0 6.6 %collective-permute-start.42 = (bf16[2,8,48,1152]{3,2,1,0:T(8,128)(2,1)}, bf16[2,8,48,1152]{3,2,1,0:T(8,128)(2,1)}, u32[]{:S(2)}, u32[]{:S(2)}) collective-permute-start(bf16[2,8,48,1152]{3,2,1,0:T(8,128)(2,1)} %get-tuple-element.317), channel_id=1, source_target_pairs={{0,1},{1,0},{2,3},{3,2},{4,5},{5,4},{6,7},{7,6},{8,9},{9,8},{10,11... | collective-permute-start | bytes 5308424 | tf_op jit(solution)/shard_map/ppermute | solution.py:46
  299.5 26.7 %all-to-all-start.8 = ((bf16[4,128,768]{2,1,0:T(8,128)(2,1)}), bf16[4,128,768]{2,1,0:T(8,128)(2,1)S(1)}, u32[]{:S(2)}, u32[]{:S(2)}) async-start(bf16[4,128,768]{2,1,0:T(8,128)(2,1)} %bitcast.121), calls=%async_computation.8 | async-start | bytes 1572864 | tf_op jit(solution)/shard_map/all_to_all | solution.py:112
  307.1 10.9 %collective-permute-start.43 = (bf16[120,768]{1,0:T(8,128)(2,1)}, bf16[120,768]{1,0:T(8,128)(2,1)S(1)}, u32[]{:S(2)}, u32[]{:S(2)}) collective-permute-start(bf16[120,768]{1,0:T(8,128)(2,1)} %get-tuple-element.334), channel_id=1, source_target_pairs={{0,8},{4,12},{8,0},{12,4},{16,24},{20,28},{24,16},{28,20},{1,9},{5... | collective-permute-start | bytes 552968 | tf_op jit(solution)/shard_map/ppermute | solution.py:46
  309.1 16.5 %collective-permute-start.44 = (bf16[120,768]{1,0:T(8,128)(2,1)}, bf16[120,768]{1,0:T(8,128)(2,1)S(1)}, u32[]{:S(2)}, u32[]{:S(2)}) collective-permute-start(bf16[120,768]{1,0:T(8,128)(2,1)} %get-tuple-element.335), channel_id=1, source_target_pairs={{0,16},{4,20},{8,24},{12,28},{16,0},{20,4},{24,8},{28,12},{1,17},{... | collective-permute-start | bytes 552968 | tf_op jit(solution)/shard_map/ppermute | solution.py:46
  311.4 14.8 %collective-permute-start.45 = (bf16[120,768]{1,0:T(8,128)(2,1)}, bf16[120,768]{1,0:T(8,128)(2,1)}, u32[]{:S(2)}, u32[]{:S(2)}) collective-permute-start(bf16[120,768]{1,0:T(8,128)(2,1)} %get-tuple-element.336), channel_id=1, source_target_pairs={{0,24},{4,28},{8,16},{12,20},{16,8},{20,12},{24,0},{28,4},{1,25},{... | collective-permute-start | bytes 552968 | tf_op jit(solution)/shard_map/ppermute | solution.py:46
  326.3 18.7 %collective-permute-start.46 = (bf16[4,48,1152]{2,1,0:T(8,128)(2,1)}, bf16[4,48,1152]{2,1,0:T(8,128)(2,1)}, u32[]{:S(2)}, u32[]{:S(2)}) collective-permute-start(bf16[4,48,1152]{2,1,0:T(8,128)(2,1)} %get-tuple-element.341), channel_id=1, source_target_pairs={{0,6},{1,7},{2,4},{3,5},{4,2},{5,3},{6,0},{7,1},{8,14},{9,15},{10,... | collective-permute-start | bytes 1327112 | tf_op jit(solution)/shard_map/ppermute | solution.py:52
  328.5 18.0 %collective-permute-start.47 = (bf16[4,48,1152]{2,1,0:T(8,128)(2,1)}, bf16[4,48,1152]{2,1,0:T(8,128)(2,1)}, u32[]{:S(2)}, u32[]{:S(2)}) collective-permute-start(bf16[4,48,1152]{2,1,0:T(8,128)(2,1)} %get-tuple-element.342), channel_id=1, source_target_pairs={{0,2},{1,3},{2,0},{3,1},{4,6},{5,7},{6,4},{7,5},{8,10},{9,11},{10,... | collective-permute-start | bytes 1327112 | tf_op jit(solution)/shard_map/ppermute | solution.py:52
  328.5 18.6 %collective-permute-start.48 = (bf16[4,48,1152]{2,1,0:T(8,128)(2,1)}, bf16[4,48,1152]{2,1,0:T(8,128)(2,1)}, u32[]{:S(2)}, u32[]{:S(2)}) collective-permute-start(bf16[4,48,1152]{2,1,0:T(8,128)(2,1)} %get-tuple-element.343), channel_id=1, source_target_pairs={{0,4},{1,5},{2,6},{3,7},{4,0},{5,1},{6,2},{7,3},{8,12},{9,13},{10,... | collective-permute-start | bytes 1327112 | tf_op jit(solution)/shard_map/ppermute | solution.py:52
  330.7 24.2 %all-to-all-start.9 = ((bf16[4,128,768]{2,1,0:T(8,128)(2,1)}), bf16[4,128,768]{2,1,0:T(8,128)(2,1)S(1)}, u32[]{:S(2)}, u32[]{:S(2)}) async-start(bf16[4,128,768]{2,1,0:T(8,128)(2,1)} %broadcast_select_fusion), calls=%async_computation.9 | async-start | bytes 1572864 | tf_op jit(solution)/shard_map/all_to_all | solution.py:61
  357.2 10.3 %all-to-all-start.10 = ((f32[32,1,384]{2,1,0:T(1,128)}), f32[32,1,384]{2,1,0:T(1,128)S(1)}, u32[]{:S(2)}, u32[]{:S(2)}) async-start(f32[32,1,384]{2,1,0:T(1,128)} %copy.65), calls=%async_computation.10 | async-start | bytes 98304 | tf_op jit(solution)/shard_map/all_to_all | solution.py:1293
  362.6 7.9 %collective-permute-start.49 = (bf16[48,1152]{1,0:T(8,128)(2,1)}, bf16[48,1152]{1,0:T(8,128)(2,1)S(1)}, u32[]{:S(2)}, u32[]{:S(2)}) collective-permute-start(bf16[48,1152]{1,0:T(8,128)(2,1)} %get-tuple-element.357), channel_id=1, source_target_pairs={{0,8},{4,12},{8,0},{12,4},{16,24},{20,28},{24,16},{28,20},{1,9},{5... | collective-permute-start | bytes 331784 | tf_op jit(solution)/shard_map/ppermute | solution.py:46
  364.3 11.8 %collective-permute-start.50 = (bf16[48,1152]{1,0:T(8,128)(2,1)}, bf16[48,1152]{1,0:T(8,128)(2,1)S(1)}, u32[]{:S(2)}, u32[]{:S(2)}) collective-permute-start(bf16[48,1152]{1,0:T(8,128)(2,1)} %get-tuple-element.358), channel_id=1, source_target_pairs={{0,16},{4,20},{8,24},{12,28},{16,0},{20,4},{24,8},{28,12},{1,17},{... | collective-permute-start | bytes 331784 | tf_op jit(solution)/shard_map/ppermute | solution.py:46
  366.8 9.4 %collective-permute-start.51 = (bf16[48,1152]{1,0:T(8,128)(2,1)}, bf16[48,1152]{1,0:T(8,128)(2,1)S(1)}, u32[]{:S(2)}, u32[]{:S(2)}) collective-permute-start(bf16[48,1152]{1,0:T(8,128)(2,1)} %get-tuple-element.359), channel_id=1, source_target_pairs={{0,24},{4,28},{8,16},{12,20},{16,8},{20,12},{24,0},{28,4},{1,25},{... | collective-permute-start | bytes 331784 | tf_op jit(solution)/shard_map/ppermute | solution.py:46
  (42 other events, 465.0 us)

commit v2 on v1

--- a/solution.py
+++ b/solution.py
@@ -271,30 +271,30 @@
     return tower0, tower1
 
 
-def share_kernel(at_ref, keep_ref, got_ref, own_ref, *sent_refs):
+def share_kernel(at_ref, keep_ref, got_ref, *out_refs):
     x, y = at_ref[0], at_ref[1]
 
-    def share(dx, dy):
-        at = (x ^ dx, 0, y ^ dy)
-        return keep_ref[at].astype(F32) + got_ref[at].astype(F32)
-
-    own_ref[0] = share(0, 0)
-    for ref, (dx, dy) in zip(sent_refs, OTHERS):
-        ref[0] = share(dx, dy).astype(BF)
+    def body(level, carry):
+        for ref, (dx, dy) in zip(out_refs, ((0, 0), *OTHERS)):
+            at = (x ^ dx, level, y ^ dy)
+            ref[level] = (keep_ref[at].astype(F32) + got_ref[at].astype(F32)).astype(BF)
+        return carry
+
+    lax.fori_loop(0, keep_ref.shape[1], body, 0)
 
 
 def column_shares(place, keep, got):
     r, c = got.shape[2:]
-    block = pl.BlockSpec((2, 1, place.stride, r, c), lambda i, at: (0, i, 0, 0, 0))
-    out = pl.BlockSpec((1, r, c), lambda i, at: (i, 0, 0))
+    half = LEVELS // 2
+    block = pl.BlockSpec((2, half, place.stride, r, c), lambda i, at: (0, i, 0, 0, 0))
+    out = pl.BlockSpec((half, r, c), lambda i, at: (i, 0, 0))
     shape = (2, LEVELS, place.stride, r, c)
     return pl.pallas_call(
         share_kernel,
         grid_spec=pltpu.PrefetchScalarGridSpec(
-            num_scalar_prefetch=1, grid=(LEVELS,), in_specs=[block] * 2, out_specs=[out] * 4
+            num_scalar_prefetch=1, grid=(2,), in_specs=[block] * 2, out_specs=[out] * 4
         ),
-        out_shape=[jax.ShapeDtypeStruct((LEVELS, r, c), F32)]
-        + [jax.ShapeDtypeStruct((LEVELS, r, c), BF)] * 3,
+        out_shape=[jax.ShapeDtypeStruct((LEVELS, r, c), BF)] * 4,
         compiler_params=pltpu.CompilerParams(vmem_limit_bytes=VMEM),
         cost_estimate=cost(1),
     )(jnp.stack([place.n // 2, place.y]), keep.reshape(shape), got.reshape(shape))
@@ -307,16 +307,20 @@
 
 
 def level_kernel(z_ref, own_ref, *refs):
-    got_refs, (sum_ref, *sent_refs) = refs[:3], refs[3:]
-    for k in range(LEVELS):
-        at = z_ref[0] ^ k
-        total = own_ref[at]
-        for ref in got_refs:
-            total = total + ref[at].astype(F32)
-        if k == 0:
-            sum_ref[...] = total
-        else:
-            sent_refs[k - 1][...] = total.astype(BF)
+    got_refs, out_refs = refs[:3], refs[3:]
+    step = 24
+
+    def body(i, carry):
+        rows = pl.ds(pl.multiple_of(i * step, step), step)
+        for k, out_ref in enumerate(out_refs):
+            at = (z_ref[0] ^ k, rows)
+            total = own_ref[at].astype(F32)
+            for ref in got_refs:
+                total = total + ref[at].astype(F32)
+            out_ref[rows] = total.astype(out_ref.dtype)
+        return carry
+
+    lax.fori_loop(0, own_ref.shape[1] // step, body, 0)
 
 
 def level_shares(place, columns):
@@ -333,8 +337,11 @@
 
 
 def level_sums_kernel(*refs):
-    for at in range(LEVELS):
+    def body(at, carry):
         refs[-1][at] = sum(ref[at].astype(F32) for ref in refs[:-1]).astype(BF)
+        return carry
+
+    lax.fori_loop(0, LEVELS, body, 0)
 
 
 def level_sums(columns):
@@ -403,27 +410,33 @@
     def _():
         turned_ref[...] = right_ref[...].T
 
-    value = matmul(turned_ref[...], left_ref[...]).astype(BF)
-    cols = send_ref.shape[2]
+    cols, rows = send_ref.shape[2:]
     first = core_ref[0] == 0
-    for x in range(2):
-        even = value[2 * x * cols : (2 * x + 1) * cols]
-        odd = value[(2 * x + 1) * cols : (2 * x + 2) * cols]
-        keep_ref[x, 0] = jnp.where(first, even, odd)
-        send_ref[x, 0] = jnp.where(first, odd, even)
+
+    def body(x, carry):
+        at = pl.ds(pl.multiple_of(x * 2 * cols, 2 * cols), 2 * cols)
+        value = matmul(turned_ref[at], left_ref[...]).astype(BF)
+        for w in range(2):
+            columns = slice(w * rows, (w + 1) * rows)
+            even, odd = value[:cols, columns], value[cols:, columns]
+            keep_ref[x, w] = jnp.where(first, even, odd)
+            send_ref[x, w] = jnp.where(first, odd, even)
+        return carry
+
+    lax.fori_loop(0, 2, body, 0)
 
 
 def products_back(place, active, grad_ffn):
     t, ff = active.shape
     d = grad_ffn.shape[1]
     cols, rows = d // place.narrow, ff // place.wide
-    out = pl.BlockSpec((2, 1, cols, rows), lambda j, core: (0, j, 0, 0))
+    out = pl.BlockSpec((2, 2, cols, rows), lambda j, core: (0, j, 0, 0))
     return pl.pallas_call(
         products_back_kernel,
         grid_spec=pltpu.PrefetchScalarGridSpec(
             num_scalar_prefetch=1,
-            grid=(place.wide,),
-            in_specs=[pl.BlockSpec((t, rows), lambda j, core: (0, j)), whole((t, d))],
+            grid=(place.wide // 2,),
+            in_specs=[pl.BlockSpec((t, 2 * rows), lambda j, core: (0, j)), whole((t, d))],
             out_specs=[out, out],
             scratch_shapes=[pltpu.VMEM((d, t), BF)],
         ),
@@ -497,19 +510,13 @@
 
     def step(refs, store):
         left, right = refs
-
-        def body(i, carry):
-            at = pl.ds(pl.multiple_of(i * 4 * rows, 4 * rows), 4 * rows)
-            value = inner_rows(left[:, at], right[0])
-            for w in range(4):
-                for g in range(2):
-                    store(
-                        (4 * i + w, slice(None), slice(g * cols, (g + 1) * cols)),
-                        value[w * rows + g * half : w * rows + (g + 1) * half],
-                    )
-            return carry
-
-        lax.fori_loop(0, place.wide // 4, body, 0)
+        value = inner_rows(left[...], right[0])
+        for w in range(place.wide):
+            for g in range(2):
+                store(
+                    (w, slice(None), slice(g * cols, (g + 1) * cols)),
+                    value[w * rows + g * half : w * rows + (g + 1) * half],
+                )
 
     return products(
         place,
@@ -868,7 +875,7 @@
 
 
 def hidden_back_kernel(
-    low, w_back, slope, w_in, grad, unit, scale, rows, hidden, inb, residual, branch, blocks, sums, acc
+    low, w_back, slope, w_in, grad, unit, scale, rows, hidden, inb, branch, blocks, sums, acc
 ):
     step = pl.program_id(0)
     product = inner_cols(low[...], w_back[...])
@@ -890,8 +897,7 @@
 
         def body(at, totals):
             value = acc[at]
-            residual[at] = norm_back(value, unit[at], scale[at], rows[6:7])
-            branch[at] = residual[at].astype(BF)
+            branch[at] = norm_back(value, unit[at], scale[at], rows[6:7]).astype(BF)
             store_blocks(blocks, at, branch[at])
             values = (value * unit[at], value, branch[at].astype(F32))
             return tuple(t + column_sum(value) for t, value in zip(totals, values))
@@ -907,7 +913,6 @@
     outs = [
         ((t, ff), BF),
         ((1, ff), F32),
-        ((t, d), F32),
         ((t, d), BF),
         ((narrow, t, d // narrow), BF),
         ((3, d), F32),
@@ -936,7 +941,7 @@
 
     @pl.when(step == 0)
     def _():
-        acc[...] = residual[...] + product
+        acc[...] = residual[...].astype(F32) + product
 
     @pl.when(step == 1)
     def _():
@@ -1250,7 +1255,7 @@
 
         columns_c = send_columns(shares_c)
         swapped = swap_out(place, out_four)
-    grad_hidden, inb_sums, grad_residual, grad_branch, blocks_b, sums_one = hidden_back(
+    grad_hidden, inb_sums, grad_branch, blocks_b, sums_one = hidden_back(
         grad_ffn, w_back_all, slope, w_in_all, grad_resid_two, unit_one, scale_one, rows, narrow
     )
     if s == 2:
@@ -1273,22 +1278,24 @@
         send_a, grad_qkv, columns_b, levels_c = phase(send_a, grad_qkv, columns_b, levels_c)
 
         got_a = flip(send_a, "narrow", 1)
-    input_grad = input_back(grad_qkv, w_qkv_all, grad_residual)
+    input_grad = input_back(grad_qkv, w_qkv_all, grad_branch)
     if s == 2:
         got_a, input_grad, columns_b = phase(got_a, input_grad, columns_b)
 
         in_four = row_pieces(place, input_grad)
         levels_b = swap_shares(place, level_shares(place, columns_b))
         shares_a = column_shares(place, keep_a, got_a)
+        late = levels_b.pop(3)
         shares_a, levels_b, in_four, sums_qkv, levels_c = phase(
             shares_a, levels_b, in_four, sums_qkv, levels_c
         )
+        levels_b.insert(3, late)
 
         columns_a = send_columns(shares_a)
         swapped = swap_out(place, in_four)
         packed = pack_sums(devices, sums_qkv, sums_one, sums_two, inb_sums, stats_one, stats_two)
         grad_w_back = finish_back(levels_c)
-        columns_a, swapped, packed = phase(columns_a, swapped, packed)
+        columns_a, swapped, packed, levels_b = phase(columns_a, swapped, packed, levels_b)
 
         packed = lax.all_to_all(packed, BOTH, 0, 0, tiled=True)
         levels_a = swap_shares(place, level_shares(place, columns_a))

time: 380 us -> 374 us (0.984)
  Pallas kernels: 162 us -> 156 us
    all_to_all x6, waiting for transfers between devices: 7.79 us -> 0.02 us  [across_levels(): return lax.all_to_all(x, 'wide', 0, 0, axis_index_groups=groups, tiled=True)]
    ppermute x21, waiting for transfers between devices: 8.7 us -> 12.7 us  [flip_both(): return lax.ppermute(x, BOTH, [(i, i ^ mask) for i in range(wide * narrow)])]
  transfers between devices with their start and end apart: 63 -> 63, of which waited for: 30 -> 28; matrix products, arithmetic and copies ran while one was open for 6% -> 5% of each run, Pallas kernels for 40% -> 39%
where the time goes in v2:
time: 374 us; the launch traced here: 372 us
  Pallas kernels  156 us (42%)
  starting transfers between devices  100 us (27%)
  waiting for transfers between devices  77.9 us (21%)
  other arithmetic  23.1 us (6%)
  local copies, waits for them, and re-layouts  14 us (4%)
    ppermute x28, waiting for transfers between devices, flip(): return lax.ppermute(x, axis, [(i, i ^ mask) for i in range(size)])  41 us
    ppermute x28, starting transfers between devices, flip(): return lax.ppermute(x, axis, [(i, i ^ mask) for i in range(size)])  26.5 us
    ppermute x21, starting transfers between devices, flip_both(): return lax.ppermute(x, BOTH, [(i, i ^ mask) for i in range(wide * narrow)])  24.6 us
    all_to_all x6, starting transfers between devices, across_levels(): return lax.all_to_all(x, 'wide', 0, 0, axis_index_groups=groups, tiled=True)  22.6 us
    pallas_call x1, Pallas kernels, attend_back(): pl.pallas_call(attend_back_kernel, grid=(d // width,), in_specs=[pl.Block...  20.3 us
    pallas_call x2, Pallas kernels, products(): pl.pallas_call(functools.partial(product_kernel, step), grid_spec=grid_sp...  16 us
    ppermute x3, waiting for transfers between devices, swap_levels(): return lax.ppermute(x, 'wide', pairs)  15.8 us
    pallas_call x1, Pallas kernels, hidden_back(): calls(hidden_back_kernel, outs, 14, grid=(ff // d,), in_specs=[all_of(low...  13.9 us
  transfers between devices with their start and end apart: 63, of which 28 were waited for; matrix products, arithmetic and copies ran while one was open for 5% of the time, Pallas kernels for 39%

profile of v2, /device:TPU:0, one launch (start us, length us, event | category | flops | bytes accessed | tf_op | source)
XLA Modules:
  0.0 372.3 jit_solution(798151409932366577)
XLA Ops:
  7.1 5.0 %collective-permute-start.2 = (bf16[80,768]{1,0:T(8,128)(2,1)}, bf16[80,768]{1,0:T(8,128)(2,1)S(1)}, u32[]{:S(2)}, u32[]{:S(2)}) collective-permute-start(bf16[80,768]{1,0:T(8,128)(2,1)} %get-tuple-element.194), channel_id=1, source_target_pairs={{0,24},{4,28},{8,16},{12,20},{16,8},{20,12},{24,0},{28,4},{1,25},{... | collective-permute-start | bytes 368648 | tf_op jit(solution)/shard_map/ppermute | solution.py:46
  12.8 3.8 %collective-permute-done.2 = bf16[80,768]{1,0:T(8,128)(2,1)S(1)} collective-permute-done((bf16[80,768]{1,0:T(8,128)(2,1)}, bf16[80,768]{1,0:T(8,128)(2,1)S(1)}, u32[]{:S(2)}, u32[]{:S(2)}) %collective-permute-start.2) | collective-permute-done | bytes 122912 | tf_op jit(solution)/shard_map/ppermute | solution.py:46
  16.6 2.8 collective-permute-done
  19.4 3.3 collective-permute-done.1
  24.8 3.7 %all-to-all-start = ((bf16[4,24,3840]{2,1,0:T(8,128)(2,1)}), bf16[4,24,3840]{2,1,0:T(8,128)(2,1)S(1)}, u32[]{:S(2)}, u32[]{:S(2)}) async-start(bf16[4,24,3840]{2,1,0:T(8,128)(2,1)} %broadcast_select_fusion.2), calls=%async_computation | async-start | bytes 1474560 | tf_op jit(solution)/shard_map/all_to_all | solution.py:61
  32.1 3.9 %collective-permute-start.6 = (bf16[128,768]{1,0:T(8,128)(2,1)S(1)}, bf16[128,768]{1,0:T(8,128)(2,1)S(1)}, u32[]{:S(2)}, u32[]{:S(2)}) collective-permute-start(bf16[128,768]{1,0:T(8,128)(2,1)S(1)} %get-tuple-element.423), channel_id=1, source_target_pairs={{0,8},{8,0},{4,12},{12,4},{1,9},{9,1},{5,13},{13,5},{2,10},{10,2},... | collective-permute-start | bytes 589832 | tf_op jit(solution)/shard_map/ppermute | solution.py:68
  37.9 8.0 %collective-permute-done.6 = bf16[128,768]{1,0:T(8,128)(2,1)S(1)} collective-permute-done((bf16[128,768]{1,0:T(8,128)(2,1)S(1)}, bf16[128,768]{1,0:T(8,128)(2,1)S(1)}, u32[]{:S(2)}, u32[]{:S(2)}) %collective-permute-start.6) | collective-permute-done | bytes 196640 | tf_op jit(solution)/shard_map/ppermute | solution.py:68
  47.9 7.8 %collective-permute-done.7 = bf16[128,768]{1,0:T(8,128)(2,1)S(1)} collective-permute-done((bf16[128,768]{1,0:T(8,128)(2,1)S(1)}, bf16[128,768]{1,0:T(8,128)(2,1)S(1)}, u32[]{:S(2)}, u32[]{:S(2)}) %collective-permute-start.7) | collective-permute-done | bytes 196640 | tf_op jit(solution)/shard_map/ppermute | solution.py:68
  62.0 3.5 all-to-all-start.1
  65.6 2.9 collective-permute-start.13
  69.2 8.4 %all-to-all-done.1 = bf16[4,128,768]{2,1,0:T(8,128)(2,1)S(1)} async-done(((bf16[4,128,768]{2,1,0:T(8,128)(2,1)}), bf16[4,128,768]{2,1,0:T(8,128)(2,1)S(1)}, u32[]{:S(2)}, u32[]{:S(2)}) %all-to-all-start.1) | async-done | bytes 786464 | tf_op jit(solution)/shard_map/all_to_all | solution.py:107
  77.6 5.4 %shard_map.239 = (bf16[3,32,24,768]{3,2,1,0:T(8,128)(2,1)}, bf16[1,32,8,768]{3,2,1,0:T(8,128)(2,1)}) custom-call(s32[1]{0:T(128)} %bitcast.21.me_ref, bf16[4,80,768]{2,1,0:T(8,128)(2,1)} %copy-done.7, bf16[4,80,768]{2,1,0:T(8,128)(2,1)} %copy-done.13, bf16[4,80,768]{2,1,0:T(8,128)(2,1)} %copy-done.14, bf16[4,80,768]{2,1,0:T(8,128)(2,1)} %collective-permute-done.5.refs_3_, ...), custom_call_target="tpu_custom_call" | custom-call | flops 115000000 | bytes 1024 | tf_op jit(solution)/shard_map/pallas_call | solution.py:157
  84.9 3.5 all-to-all-start.2
  92.3 13.3 %shard_map.241 = (bf16[3,512,768]{2,1,0:T(8,128)(2,1)}, bf16[512,768]{1,0:T(8,128)(2,1)}, f32[3,4,512]{2,1,0:T(4,128)}) custom-call(bf16[512,768]{1,0:T(8,128)(2,1)} %bitcast.112, bf16[3,768,768]{2,1,0:T(8,128)(2,1)} %bitcast.110, f32[8,768]{1,0:T(8,128)} %get-tuple-element.230.rows_ref.rows, s32[1,512]{1,0:T(1,128)} %bitcast.136, s32[512,1]{1,0:T(8,128)} %copy.58.seg_col_ref), custom_call_target="tpu_custom_call" | custom-call | flops 115000000 | bytes 1024 | tf_op jit(solution)/shard_map/pallas_call | solution.py:565
  105.6 3.3 collective-permute-done.14.refs_2_
  119.2 3.5 all-to-all-start.3
  122.7 6.7 %shard_map.242 = (bf16[1,32,24,768]{3,2,1,0:T(8,128)(2,1)}, bf16[4,32,24,768]{3,2,1,0:T(8,128)(2,1)}) custom-call(s32[1]{0:T(128)} %bitcast.21.me_ref, bf16[4,24,3840]{2,1,0:T(8,128)(2,1)} %copy-done.1, bf16[4,24,3840]{2,1,0:T(8,128)(2,1)} %copy-done.11, bf16[4,24,3840]{2,1,0:T(8,128)(2,1)} %collective-permute-done.14.refs_2_, ...), custom_call_target="tpu_custom_call" | custom-call | flops 115000000 | bytes 1024 | tf_op jit(solution)/shard_map/pallas_call | solution.py:157
  129.4 5.8 %shard_map.243 = (f32[512,768]{1,0:T(8,128)}, bf16[512,768]{1,0:T(8,128)(2,1)}, f32[512,768]{1,0:T(8,128)}, f32[512,1]{1,0:T(8,128)}, f32[2,128]{1,0:T(2,128)}) custom-call(bf16[512,768]{1,0:T(8,128)(2,1)} %get-tuple-element.234.ctx.refs_0_, bf16[1,768,768]{2,1,0:T(8,128)(2,1)} %bitcast.145, bf16[512,768]{1,0:T(8,128)(2,1)} %bitcast.113, ...), custom_call_target="tpu_custom_call" | custom-call | flops 5750000128 | bytes 1024 | tf_op jit(solution)/shard_map/pallas_call | solution.py:769
  135.2 9.2 %shard_map.244 = (bf16[512,3072]{1,0:T(8,128)(2,1)}, bf16[512,3072]{1,0:T(8,128)(2,1)}) custom-call(bf16[512,768]{1,0:T(8,128)(2,1)} %get-tuple-element.251.x_ref.refs_2_, bf16[4,768,768]{2,1,0:T(8,128)(2,1)} %bitcast.142, f32[1,3072]{1,0:T(1,128)} %get-tuple-element.253.bias_ref), custom_call_target="tpu_custom_call" | custom-call | flops 9200000000 | bytes 1024 | tf_op jit(solution)/shard_map/pallas_call | solution.py:686
  147.3 3.7 all-to-all-start.4
  151.1 12.9 %shard_map.245 = (bf16[512,768]{1,0:T(8,128)(2,1)}, f32[512,768]{1,0:T(8,128)}, f32[512,1]{1,0:T(8,128)}, bf16[32,768]{1,0:T(8,128)(2,1)}, f32[3,128]{1,0:T(4,128)}, /*index=5*/bf16[3072,768]{1,0:T(8,128)(2,1)}) custom-call(s32[1]{0:T(128)} %bitcast.21.me_ref, bf16[512,3072]{1,0:T(8,128)(2,1)} %get-tuple-element.258.active.left_ref, ...), custom_call_target="tpu_custom_call" | custom-call | flops 10350000128 | bytes 1024 | tf_op jit(solution)/shard_map/pallas_call | solution.py:835
  164.0 3.8 %collective-permute-start.27 = (bf16[32,768]{1,0:T(8,128)(2,1)}, bf16[32,768]{1,0:T(8,128)(2,1)S(1)}, u32[]{:S(2)}, u32[]{:S(2)}) collective-permute-start(bf16[32,768]{1,0:T(8,128)(2,1)} %get-tuple-element.267), channel_id=1, source_target_pairs={{0,24},{4,28},{8,16},{12,20},{16,8},{20,12},{24,0},{28,4},{1,25},{... | collective-permute-start | bytes 147464 | tf_op jit(solution)/shard_map/ppermute | solution.py:46
  170.3 2.8 collective-permute-done.28
  173.9 2.7 collective-permute-start.30
  186.0 3.5 all-to-all-start.5
  189.5 6.1 %shard_map.247 = (f32[512,768]{1,0:T(8,128)}, bf16[512,768]{1,0:T(8,128)(2,1)}, f32[3,768]{1,0:T(4,128)}) custom-call(bf16[512,768]{1,0:T(8,128)(2,1)} %bitcast.120, f32[512,1]{1,0:T(8,128)} %compare_convert_fusion.valid, f32[32,512]{1,0:T(8,128)} %fusion.14.hot, f32[32,768]{1,0:T(8,128)} %shard_map.246.pool, f32[512,768]{1,0:T(8,128)} %get-tuple-element.270.unit, ...), custom_call_target="tpu_custom_call" | custom-call | flops 6899999744 | bytes 1024 | tf_op jit(solution)/shard_map/pallas_call | solution.py:874
  195.5 7.2 %shard_map.248 = (bf16[2,8,192,384]{3,2,1,0:T(8,128)(2,1)}, bf16[2,8,192,384]{3,2,1,0:T(8,128)(2,1)}) custom-call(s32[1]{0:T(128)} %bitcast.34.core_ref, bf16[512,3072]{1,0:T(8,128)(2,1)} %get-tuple-element.258.active.left_ref, bf16[512,768]{1,0:T(8,128)(2,1)} %get-tuple-element.281.right_ref.low), custom_call_target="tpu_custom_call" | custom-call | flops 8049999872 | bytes 1024 | tf_op jit(solution)/shard_map/pallas_call | solution.py:434
  204.8 3.5 all-to-all-start.6
  208.3 4.3 %shard_map.249 = (bf16[4,192,384]{2,1,0:T(8,128)(2,1)}, bf16[4,192,384]{2,1,0:T(8,128)(2,1)}, bf16[4,192,384]{2,1,0:T(8,128)(2,1)}, bf16[4,192,384]{2,1,0:T(8,128)(2,1)}) custom-call(s32[2]{0:T(128)} %pad_add_fusion.1.at_ref, bf16[2,4,2,192,384]{4,3,2,1,0:T(8,128)(2,1)} %bitcast.116, bf16[2,4,2,192,384]{4,3,2,1,0:T(8,128)(2,1)} %bitcast.46.got_ref), custom_call_target="tpu_custom_call" | custom-call | flops 1150000000 | bytes 1024 | tf_op jit(solution)/shard_map/pallas_call | solution.py:292
  216.1 13.9 %shard_map.250 = (bf16[512,3072]{1,0:T(8,128)(2,1)}, f32[1,3072]{1,0:T(1,128)}, bf16[512,768]{1,0:T(8,128)(2,1)}, bf16[4,512,192]{2,1,0:T(8,128)(2,1)}, f32[3,768]{1,0:T(4,128)}) custom-call(bf16[512,768]{1,0:T(8,128)(2,1)} %get-tuple-element.281.right_ref.low, bf16[3072,768]{1,0:T(8,128)(2,1)} %get-tuple-element.282.w_back, ...), custom_call_target="tpu_custom_call" | custom-call | flops 16099999744 | bytes 1024 | tf_op jit(solution)/shard_map/pallas_call | solution.py:920
  230.0 9.2 %shard_map.251 = (bf16[2,8,120,768]{3,2,1,0:T(8,128)(2,1)}, bf16[2,8,120,768]{3,2,1,0:T(8,128)(2,1)}) custom-call(s32[1]{0:T(128)} %bitcast.me_ref, bf16[512,768]{1,0:T(8,128)(2,1)} %get-tuple-element.234.ctx.refs_0_, bf16[4,512,192]{2,1,0:T(8,128)(2,1)} %get-tuple-element.287.refs_1_, bf16[512,768]{1,0:T(8,128)(2,1)} %get-tuple-element.251.x_ref.refs_2_, ...), custom_call_target="tpu_custom_call" | custom-call | flops 9200000000 | bytes 1024 | tf_op jit(solution)/shard_map/pallas_call | solution.py:387
  242.4 2.7 shard_map.253
  247.3 4.9 %shard_map.252 = (bf16[4,120,768]{2,1,0:T(8,128)(2,1)}, bf16[4,120,768]{2,1,0:T(8,128)(2,1)}, bf16[4,120,768]{2,1,0:T(8,128)(2,1)}, bf16[4,120,768]{2,1,0:T(8,128)(2,1)}) custom-call(s32[2]{0:T(128)} %pad_add_fusion.1.at_ref, bf16[2,4,2,120,768]{4,3,2,1,0:T(8,128)(2,1)} %bitcast.115, bf16[2,4,2,120,768]{4,3,2,1,0:T(8,128)(2,1)} %bitcast.49.got_ref), custom_call_target="tpu_custom_call" | custom-call | flops 1150000000 | bytes 1024 | tf_op jit(solution)/shard_map/pallas_call | solution.py:292
  255.7 4.8 %all-to-all-start.7 = ((bf16[4,192,384]{2,1,0:T(8,128)(2,1)}), bf16[4,192,384]{2,1,0:T(8,128)(2,1)S(1)}, u32[]{:S(2)}, u32[]{:S(2)}) async-start(bf16[4,192,384]{2,1,0:T(8,128)(2,1)} %shard_map.253), calls=%async_computation.7 | async-start | bytes 1179648 | tf_op jit(solution)/shard_map/all_to_all | solution.py:61
  260.5 20.3 %shard_map.254 = (bf16[3,512,768]{2,1,0:T(8,128)(2,1)}, bf16[4,512,576]{2,1,0:T(8,128)(2,1)}, f32[2,768]{1,0:T(2,128)}) custom-call(bf16[512,768]{1,0:T(8,128)(2,1)} %get-tuple-element.307.gb_ref.residual, bf16[768,768]{1,0:T(8,128)(2,1)} %bitcast.146, bf16[3,512,768]{2,1,0:T(8,128)(2,1)} %get-tuple-element.308.qkv_ref, ...), custom_call_target="tpu_custom_call" | custom-call | flops 23000000512 | bytes 1024 | tf_op jit(solution)/shard_map/pallas_call | solution.py:640
  280.7 6.8 %shard_map.255 = (bf16[2,8,48,1152]{3,2,1,0:T(8,128)(2,1)}, bf16[2,8,48,1152]{3,2,1,0:T(8,128)(2,1)}) custom-call(s32[1]{0:T(128)} %bitcast.me_ref, bf16[512,768]{1,0:T(8,128)(2,1)} %bitcast.114, bf16[4,512,576]{2,1,0:T(8,128)(2,1)} %get-tuple-element.310.refs_1_), custom_call_target="tpu_custom_call" | custom-call | flops 9200000000 | bytes 1024 | tf_op jit(solution)/shard_map/pallas_call | solution.py:387
  287.8 6.2 %shard_map.256 = bf16[512,768]{1,0:T(8,128)(2,1)} custom-call(bf16[3,512,768]{2,1,0:T(8,128)(2,1)} %get-tuple-element.320.grad, bf16[3,768,768]{2,1,0:T(8,128)(2,1)} %bitcast.111, bf16[512,768]{1,0:T(8,128)(2,1)} %get-tuple-element.307.gb_ref.residual), custom_call_target="tpu_custom_call" | custom-call | flops 6899999744 | bytes 1024 | tf_op jit(solution)/shard_map/pallas_call | solution.py:957
  295.2 3.5 all-to-all-start.8
  298.7 3.1 shard_map.258
  306.2 3.8 %shard_map.257 = (bf16[4,48,1152]{2,1,0:T(8,128)(2,1)}, bf16[4,48,1152]{2,1,0:T(8,128)(2,1)}, bf16[4,48,1152]{2,1,0:T(8,128)(2,1)}, bf16[4,48,1152]{2,1,0:T(8,128)(2,1)}) custom-call(s32[2]{0:T(128)} %pad_add_fusion.1.at_ref, bf16[2,4,2,48,1152]{4,3,2,1,0:T(8,128)(2,1)} %bitcast.148, bf16[2,4,2,48,1152]{4,3,2,1,0:T(8,128)(2,1)} %bitcast.144), custom_call_target="tpu_custom_call" | custom-call | flops 1150000000 | bytes 1024 | tf_op jit(solution)/shard_map/pallas_call | solution.py:292
  310.0 3.0 collective-permute-done.43
  316.7 3.6 all-to-all-start.9
  321.9 3.8 %collective-permute-start.48 = (bf16[120,768]{1,0:T(8,128)(2,1)S(1)}, bf16[120,768]{1,0:T(8,128)(2,1)S(1)}, u32[]{:S(2)}, u32[]{:S(2)}) collective-permute-start(bf16[120,768]{1,0:T(8,128)(2,1)S(1)} %copy-done.34), channel_id=1, source_target_pairs={{0,24},{4,28},{8,16},{12,20},{16,8},{20,12},{24,0},{28,4},{1,25},{... | collective-permute-start | bytes 552968 | tf_op jit(solution)/shard_map/ppermute | solution.py:46
  329.2 4.8 %shard_map.259 = f32[32,384]{1,0:T(8,128)} custom-call(f32[2,768]{1,0:T(2,128)} %get-tuple-element.345.attn, f32[3,768]{1,0:T(4,128)} %get-tuple-element.346.out, f32[3,768]{1,0:T(4,128)} %get-tuple-element.347.ffn, f32[1,3072]{1,0:T(1,128)} %get-tuple-element.348.inb, f32[2,128]{1,0:T(2,128)} %get-tuple-element.349.stats_a, f32[3,128]{1,0:T(4,128)} %get-tuple-element.350.stats_b), custom_call_target="tpu_custom_call" | custom-call | flops 4600000000 | bytes 1024 | tf_op jit(solution)/shard_map/pallas_call | solution.py:1041
  335.1 5.5 %collective-permute-done.48 = bf16[120,768]{1,0:T(8,128)(2,1)S(1)} collective-permute-done((bf16[120,768]{1,0:T(8,128)(2,1)S(1)}, bf16[120,768]{1,0:T(8,128)(2,1)S(1)}, u32[]{:S(2)}, u32[]{:S(2)}) %collective-permute-start.48) | collective-permute-done | bytes 184352 | tf_op jit(solution)/shard_map/ppermute | solution.py:46
  340.6 5.5 %collective-permute-done.46.refs_1_ = bf16[4,48,1152]{2,1,0:T(8,128)(2,1)S(1)} collective-permute-done((bf16[4,48,1152]{2,1,0:T(8,128)(2,1)S(1)}, bf16[4,48,1152]{2,1,0:T(8,128)(2,1)S(1)}, u32[]{:S(2)}, u32[]{:S(2)}) %collective-permute-start.46) | collective-permute-done | bytes 442400 | tf_op jit(solution)/shard_map/ppermute | solution.py:52
  349.4 4.5 %all-to-all-start.10 = ((f32[32,1,384]{2,1,0:T(1,128)}), f32[32,1,384]{2,1,0:T(1,128)S(1)}, u32[]{:S(2)}, u32[]{:S(2)}) async-start(f32[32,1,384]{2,1,0:T(1,128)} %copy.65), calls=%async_computation.10 | async-start | bytes 98304 | tf_op jit(solution)/shard_map/all_to_all | solution.py:1300
  365.5 4.7 %collective-permute-done.50 = bf16[48,1152]{1,0:T(8,128)(2,1)S(1)} collective-permute-done((bf16[48,1152]{1,0:T(8,128)(2,1)}, bf16[48,1152]{1,0:T(8,128)(2,1)S(1)}, u32[]{:S(2)}, u32[]{:S(2)}) %collective-permute-start.50) | collective-permute-done | bytes 110624 | tf_op jit(solution)/shard_map/ppermute | solution.py:46
  (277 shorter events, 101.7 us)
Async XLA Ops:
  7.1 9.5 %collective-permute-start.2 = (bf16[80,768]{1,0:T(8,128)(2,1)}, bf16[80,768]{1,0:T(8,128)(2,1)S(1)}, u32[]{:S(2)}, u32[]{:S(2)}) collective-permute-start(bf16[80,768]{1,0:T(8,128)(2,1)} %get-tuple-element.194), channel_id=1, source_target_pairs={{0,24},{4,28},{8,16},{12,20},{16,8},{20,12},{24,0},{28,4},{1,25},{... | collective-permute-start | bytes 368648 | tf_op jit(solution)/shard_map/ppermute | solution.py:46
  12.2 7.2 %collective-permute-start = (bf16[80,768]{1,0:T(8,128)(2,1)}, bf16[80,768]{1,0:T(8,128)(2,1)S(1)}, u32[]{:S(2)}, u32[]{:S(2)}) collective-permute-start(bf16[80,768]{1,0:T(8,128)(2,1)} %get-tuple-element.192), channel_id=1, source_target_pairs={{0,8},{4,12},{8,0},{12,4},{16,24},{20,28},{24,16},{28,20},{1,9},{5... | collective-permute-start | bytes 368648 | tf_op jit(solution)/shard_map/ppermute | solution.py:46
  12.2 10.6 %collective-permute-start.1 = (bf16[80,768]{1,0:T(8,128)(2,1)}, bf16[80,768]{1,0:T(8,128)(2,1)S(1)}, u32[]{:S(2)}, u32[]{:S(2)}) collective-permute-start(bf16[80,768]{1,0:T(8,128)(2,1)} %get-tuple-element.193), channel_id=1, source_target_pairs={{0,16},{4,20},{8,24},{12,28},{16,0},{20,4},{24,8},{28,12},{1,17},{... | collective-permute-start | bytes 368648 | tf_op jit(solution)/shard_map/ppermute | solution.py:46
  24.8 31.7 %all-to-all-start = ((bf16[4,24,3840]{2,1,0:T(8,128)(2,1)}), bf16[4,24,3840]{2,1,0:T(8,128)(2,1)S(1)}, u32[]{:S(2)}, u32[]{:S(2)}) async-start(bf16[4,24,3840]{2,1,0:T(8,128)(2,1)} %broadcast_select_fusion.2), calls=%async_computation | async-start | bytes 1474560 | tf_op jit(solution)/shard_map/all_to_all | solution.py:61
  28.5 27.1 %collective-permute-start.3 = (bf16[4,80,768]{2,1,0:T(8,128)(2,1)S(1)}, bf16[4,80,768]{2,1,0:T(8,128)(2,1)S(1)}, u32[]{:S(2)}, u32[]{:S(2)}) collective-permute-start(bf16[4,80,768]{2,1,0:T(8,128)(2,1)S(1)} %pad_maximum_fusion.2.refs_0_), channel_id=1, source_target_pairs={{0,6},{1,7},{2,4},{3,5},{4,2},{5,3},{6,0},{7,1},{8,14},{9,15},{10,... | collective-permute-start | bytes 1474568 | tf_op jit(solution)/shard_map/ppermute | solution.py:52
  31.0 24.7 %collective-permute-start.4 = (bf16[4,80,768]{2,1,0:T(8,128)(2,1)S(1)}, bf16[4,80,768]{2,1,0:T(8,128)(2,1)S(1)}, u32[]{:S(2)}, u32[]{:S(2)}) collective-permute-start(bf16[4,80,768]{2,1,0:T(8,128)(2,1)S(1)} %pad_maximum_fusion.2.refs_0_), channel_id=1, source_target_pairs={{0,2},{1,3},{2,0},{3,1},{4,6},{5,7},{6,4},{7,5},{8,10},{9,11},{10,... | collective-permute-start | bytes 1474568 | tf_op jit(solution)/shard_map/ppermute | solution.py:52
  31.5 25.0 %collective-permute-start.5 = (bf16[4,80,768]{2,1,0:T(8,128)(2,1)S(1)}, bf16[4,80,768]{2,1,0:T(8,128)(2,1)}, u32[]{:S(2)}, u32[]{:S(2)}) collective-permute-start(bf16[4,80,768]{2,1,0:T(8,128)(2,1)S(1)} %pad_maximum_fusion.2.refs_0_), channel_id=1, source_target_pairs={{0,4},{1,5},{2,6},{3,7},{4,0},{5,1},{6,2},{7,3},{8,12},{9,13},{10,... | collective-permute-start | bytes 1474568 | tf_op jit(solution)/shard_map/ppermute | solution.py:52
  32.1 13.9 %collective-permute-start.6 = (bf16[128,768]{1,0:T(8,128)(2,1)S(1)}, bf16[128,768]{1,0:T(8,128)(2,1)S(1)}, u32[]{:S(2)}, u32[]{:S(2)}) collective-permute-start(bf16[128,768]{1,0:T(8,128)(2,1)S(1)} %get-tuple-element.423), channel_id=1, source_target_pairs={{0,8},{8,0},{4,12},{12,4},{1,9},{9,1},{5,13},{13,5},{2,10},{10,2},... | collective-permute-start | bytes 589832 | tf_op jit(solution)/shard_map/ppermute | solution.py:68
  36.0 19.7 %collective-permute-start.7 = (bf16[128,768]{1,0:T(8,128)(2,1)S(1)}, bf16[128,768]{1,0:T(8,128)(2,1)S(1)}, u32[]{:S(2)}, u32[]{:S(2)}) collective-permute-start(bf16[128,768]{1,0:T(8,128)(2,1)S(1)} %get-tuple-element.422), channel_id=1, source_target_pairs={{0,16},{16,0},{4,20},{20,4},{1,17},{17,1},{5,21},{21,5},{2,18},{18... | collective-permute-start | bytes 589832 | tf_op jit(solution)/shard_map/ppermute | solution.py:68
  46.0 9.7 %collective-permute-start.8 = (bf16[128,768]{1,0:T(8,128)(2,1)S(1)}, bf16[128,768]{1,0:T(8,128)(2,1)S(1)}, u32[]{:S(2)}, u32[]{:S(2)}) collective-permute-start(bf16[128,768]{1,0:T(8,128)(2,1)S(1)} %get-tuple-element.421), channel_id=1, source_target_pairs={{0,24},{24,0},{4,28},{28,4},{1,25},{25,1},{5,29},{29,5},{2,26},{26... | collective-permute-start | bytes 589832 | tf_op jit(solution)/shard_map/ppermute | solution.py:68
  62.0 15.6 %all-to-all-start.1 = ((bf16[4,128,768]{2,1,0:T(8,128)(2,1)}), bf16[4,128,768]{2,1,0:T(8,128)(2,1)S(1)}, u32[]{:S(2)}, u32[]{:S(2)}) async-start(bf16[4,128,768]{2,1,0:T(8,128)(2,1)} %maximum_select_fusion), calls=%async_computation.1 | async-start | bytes 1572864 | tf_op jit(solution)/shard_map/all_to_all | solution.py:107
  65.6 39.9 %collective-permute-start.13 = (bf16[4,24,3840]{2,1,0:T(8,128)(2,1)S(1)}, bf16[4,24,3840]{2,1,0:T(8,128)(2,1)S(1)}, u32[]{:S(2)}, u32[]{:S(2)}) collective-permute-start(bf16[4,24,3840]{2,1,0:T(8,128)(2,1)S(1)} %all-to-all-done.refs_0_), channel_id=1, source_target_pairs={{0,6},{1,7},{2,4},{3,5},{4,2},{5,3},{6,0},{7,1},{8,14},{9,15},{10,... | collective-permute-start | bytes 2211848 | tf_op jit(solution)/shard_map/ppermute | solution.py:52
  68.6 40.3 %collective-permute-start.14 = (bf16[4,24,3840]{2,1,0:T(8,128)(2,1)S(1)}, bf16[4,24,3840]{2,1,0:T(8,128)(2,1)}, u32[]{:S(2)}, u32[]{:S(2)}) collective-permute-start(bf16[4,24,3840]{2,1,0:T(8,128)(2,1)S(1)} %all-to-all-done.refs_0_), channel_id=1, source_target_pairs={{0,2},{1,3},{2,0},{3,1},{4,6},{5,7},{6,4},{7,5},{8,10},{9,11},{10,... | collective-permute-start | bytes 2211848 | tf_op jit(solution)/shard_map/ppermute | solution.py:52
  68.7 40.2 %collective-permute-start.15 = (bf16[4,24,3840]{2,1,0:T(8,128)(2,1)S(1)}, bf16[4,24,3840]{2,1,0:T(8,128)(2,1)}, u32[]{:S(2)}, u32[]{:S(2)}) collective-permute-start(bf16[4,24,3840]{2,1,0:T(8,128)(2,1)S(1)} %all-to-all-done.refs_0_), channel_id=1, source_target_pairs={{0,4},{1,5},{2,6},{3,7},{4,0},{5,1},{6,2},{7,3},{8,12},{9,13},{10,... | collective-permute-start | bytes 2211848 | tf_op jit(solution)/shard_map/ppermute | solution.py:52
  84.9 24.0 %all-to-all-start.2 = ((bf16[4,96,768]{2,1,0:T(8,128)(2,1)}), bf16[4,96,768]{2,1,0:T(8,128)(2,1)S(1)}, u32[]{:S(2)}, u32[]{:S(2)}) async-start(bf16[4,96,768]{2,1,0:T(8,128)(2,1)} %broadcast_select_fusion.3), calls=%async_computation.2 | async-start | bytes 1179648 | tf_op jit(solution)/shard_map/all_to_all | solution.py:61
  114.7 29.8 %collective-permute-start.20 = (bf16[4,96,768]{2,1,0:T(8,128)(2,1)S(1)}, bf16[4,96,768]{2,1,0:T(8,128)(2,1)S(1)}, u32[]{:S(2)}, u32[]{:S(2)}) collective-permute-start(bf16[4,96,768]{2,1,0:T(8,128)(2,1)S(1)} %all-to-all-done.2.refs_0_), channel_id=1, source_target_pairs={{0,6},{1,7},{2,4},{3,5},{4,2},{5,3},{6,0},{7,1},{8,14},{9,15},{10,... | collective-permute-start | bytes 1769480 | tf_op jit(solution)/shard_map/ppermute | solution.py:52
  116.0 28.5 %collective-permute-start.21 = (bf16[4,96,768]{2,1,0:T(8,128)(2,1)S(1)}, bf16[4,96,768]{2,1,0:T(8,128)(2,1)}, u32[]{:S(2)}, u32[]{:S(2)}) collective-permute-start(bf16[4,96,768]{2,1,0:T(8,128)(2,1)S(1)} %all-to-all-done.2.refs_0_), channel_id=1, source_target_pairs={{0,2},{1,3},{2,0},{3,1},{4,6},{5,7},{6,4},{7,5},{8,10},{9,11},{10,... | collective-permute-start | bytes 1769480 | tf_op jit(solution)/shard_map/ppermute | solution.py:52
  117.7 26.8 %collective-permute-start.22 = (bf16[4,96,768]{2,1,0:T(8,128)(2,1)S(1)}, bf16[4,96,768]{2,1,0:T(8,128)(2,1)}, u32[]{:S(2)}, u32[]{:S(2)}) collective-permute-start(bf16[4,96,768]{2,1,0:T(8,128)(2,1)S(1)} %all-to-all-done.2.refs_0_), channel_id=1, source_target_pairs={{0,4},{1,5},{2,6},{3,7},{4,0},{5,1},{6,2},{7,3},{8,12},{9,13},{10,... | collective-permute-start | bytes 1769480 | tf_op jit(solution)/shard_map/ppermute | solution.py:52
  119.2 25.3 %all-to-all-start.3 = ((bf16[4,128,768]{2,1,0:T(8,128)(2,1)}), bf16[4,128,768]{2,1,0:T(8,128)(2,1)S(1)}, u32[]{:S(2)}, u32[]{:S(2)}) async-start(bf16[4,128,768]{2,1,0:T(8,128)(2,1)} %maximum_select_fusion.1), calls=%async_computation.3 | async-start | bytes 1572864 | tf_op jit(solution)/shard_map/all_to_all | solution.py:61
  144.5 6.5 %collective-permute-start.23 = (bf16[4,96,768]{2,1,0:T(8,128)(2,1)S(1)}, bf16[4,96,768]{2,1,0:T(8,128)(2,1)}, u32[]{:S(2)}, u32[]{:S(2)}) collective-permute-start(bf16[4,96,768]{2,1,0:T(8,128)(2,1)S(1)} %all-to-all-done.2.refs_0_), channel_id=1, source_target_pairs={{0,1},{1,0},{2,3},{3,2},{4,5},{5,4},{6,7},{7,6},{8,9},{9,8},{10,11... | collective-permute-start | bytes 1769480 | tf_op jit(solution)/shard_map/ppermute | solution.py:46
  144.6 6.5 %collective-permute-start.24 = (bf16[4,96,768]{2,1,0:T(8,128)(2,1)S(1)}, bf16[4,96,768]{2,1,0:T(8,128)(2,1)}, u32[]{:S(2)}, u32[]{:S(2)}) collective-permute-start(bf16[4,96,768]{2,1,0:T(8,128)(2,1)S(1)} %collective-permute-done.20.refs_1_), channel_id=1, source_target_pairs={{0,1},{1,0},{2,3},{3,2},{4,5},{5,4},{6,7},{7,6},{8,9},{9,8},{10,11... | collective-permute-start | bytes 1769480 | tf_op jit(solution)/shard_map/ppermute | solution.py:46
  145.1 6.0 %collective-permute-start.25 = (bf16[4,96,768]{2,1,0:T(8,128)(2,1)}, bf16[4,96,768]{2,1,0:T(8,128)(2,1)}, u32[]{:S(2)}, u32[]{:S(2)}) collective-permute-start(bf16[4,96,768]{2,1,0:T(8,128)(2,1)} %collective-permute-done.21.refs_2_), channel_id=1, source_target_pairs={{0,1},{1,0},{2,3},{3,2},{4,5},{5,4},{6,7},{7,6},{8,9},{9,8},{10,11... | collective-permute-start | bytes 1769480 | tf_op jit(solution)/shard_map/ppermute | solution.py:46
  145.2 5.9 %collective-permute-start.26 = (bf16[4,96,768]{2,1,0:T(8,128)(2,1)}, bf16[4,96,768]{2,1,0:T(8,128)(2,1)}, u32[]{:S(2)}, u32[]{:S(2)}) collective-permute-start(bf16[4,96,768]{2,1,0:T(8,128)(2,1)} %collective-permute-done.22.refs_3_), channel_id=1, source_target_pairs={{0,1},{1,0},{2,3},{3,2},{4,5},{5,4},{6,7},{7,6},{8,9},{9,8},{10,11... | collective-permute-start | bytes 1769480 | tf_op jit(solution)/shard_map/ppermute | solution.py:46
  147.3 16.6 %all-to-all-start.4 = ((bf16[4,128,768]{2,1,0:T(8,128)(2,1)}), bf16[4,128,768]{2,1,0:T(8,128)(2,1)S(1)}, u32[]{:S(2)}, u32[]{:S(2)}) async-start(bf16[4,128,768]{2,1,0:T(8,128)(2,1)} %maximum_select_fusion.2), calls=%async_computation.4 | async-start | bytes 1572864 | tf_op jit(solution)/shard_map/all_to_all | solution.py:107
  164.0 6.3 %collective-permute-start.27 = (bf16[32,768]{1,0:T(8,128)(2,1)}, bf16[32,768]{1,0:T(8,128)(2,1)S(1)}, u32[]{:S(2)}, u32[]{:S(2)}) collective-permute-start(bf16[32,768]{1,0:T(8,128)(2,1)} %get-tuple-element.267), channel_id=1, source_target_pairs={{0,24},{4,28},{8,16},{12,20},{16,8},{20,12},{24,0},{28,4},{1,25},{... | collective-permute-start | bytes 147464 | tf_op jit(solution)/shard_map/ppermute | solution.py:46
  173.9 5.8 %collective-permute-start.30 = (bf16[1,32,768]{2,1,0:T(8,128)(2,1)S(1)}, bf16[1,32,768]{2,1,0:T(8,128)(2,1)S(1)}, u32[]{:S(2)}, u32[]{:S(2)}) collective-permute-start(bf16[1,32,768]{2,1,0:T(8,128)(2,1)S(1)} %get-tuple-element.414), channel_id=1, source_target_pairs={{0,6},{1,7},{2,4},{3,5},{4,2},{5,3},{6,0},{7,1},{8,14},{9,15},{10,... | collective-permute-start | bytes 147464 | tf_op jit(solution)/shard_map/ppermute | solution.py:52
  186.0 16.8 %all-to-all-start.5 = ((bf16[4,128,768]{2,1,0:T(8,128)(2,1)}), bf16[4,128,768]{2,1,0:T(8,128)(2,1)S(1)}, u32[]{:S(2)}, u32[]{:S(2)}) async-start(bf16[4,128,768]{2,1,0:T(8,128)(2,1)} %bitcast.45), calls=%async_computation.5 | async-start | bytes 1572864 | tf_op jit(solution)/shard_map/all_to_all | solution.py:112
  204.8 34.5 %all-to-all-start.6 = ((bf16[4,128,768]{2,1,0:T(8,128)(2,1)}), bf16[4,128,768]{2,1,0:T(8,128)(2,1)S(1)}, u32[]{:S(2)}, u32[]{:S(2)}) async-start(bf16[4,128,768]{2,1,0:T(8,128)(2,1)} %broadcast_select_fusion.1), calls=%async_computation.6 | async-start | bytes 1572864 | tf_op jit(solution)/shard_map/all_to_all | solution.py:61
  212.6 26.7 %collective-permute-start.35 = (bf16[4,192,384]{2,1,0:T(8,128)(2,1)}, bf16[4,192,384]{2,1,0:T(8,128)(2,1)S(1)}, u32[]{:S(2)}, u32[]{:S(2)}) collective-permute-start(bf16[4,192,384]{2,1,0:T(8,128)(2,1)} %get-tuple-element.291), channel_id=1, source_target_pairs={{0,6},{1,7},{2,4},{3,5},{4,2},{5,3},{6,0},{7,1},{8,14},{9,15},{10,... | collective-permute-start | bytes 1769480 | tf_op jit(solution)/shard_map/ppermute | solution.py:52
  214.2 26.8 %collective-permute-start.36 = (bf16[4,192,384]{2,1,0:T(8,128)(2,1)}, bf16[4,192,384]{2,1,0:T(8,128)(2,1)S(1)}, u32[]{:S(2)}, u32[]{:S(2)}) collective-permute-start(bf16[4,192,384]{2,1,0:T(8,128)(2,1)} %get-tuple-element.292), channel_id=1, source_target_pairs={{0,2},{1,3},{2,0},{3,1},{4,6},{5,7},{6,4},{7,5},{8,10},{9,11},{10,... | collective-permute-start | bytes 1769480 | tf_op jit(solution)/shard_map/ppermute | solution.py:52
  214.6 27.1 %collective-permute-start.37 = (bf16[4,192,384]{2,1,0:T(8,128)(2,1)}, bf16[4,192,384]{2,1,0:T(8,128)(2,1)S(1)}, u32[]{:S(2)}, u32[]{:S(2)}) collective-permute-start(bf16[4,192,384]{2,1,0:T(8,128)(2,1)} %get-tuple-element.293), channel_id=1, source_target_pairs={{0,4},{1,5},{2,6},{3,7},{4,0},{5,1},{6,2},{7,3},{8,12},{9,13},{10,... | collective-permute-start | bytes 1769480 | tf_op jit(solution)/shard_map/ppermute | solution.py:52
  252.2 35.3 %collective-permute-start.39 = (bf16[4,120,768]{2,1,0:T(8,128)(2,1)}, bf16[4,120,768]{2,1,0:T(8,128)(2,1)S(1)}, u32[]{:S(2)}, u32[]{:S(2)}) collective-permute-start(bf16[4,120,768]{2,1,0:T(8,128)(2,1)} %get-tuple-element.315), channel_id=1, source_target_pairs={{0,6},{1,7},{2,4},{3,5},{4,2},{5,3},{6,0},{7,1},{8,14},{9,15},{10,... | collective-permute-start | bytes 2211848 | tf_op jit(solution)/shard_map/ppermute | solution.py:52
  254.3 33.2 %collective-permute-start.40 = (bf16[4,120,768]{2,1,0:T(8,128)(2,1)}, bf16[4,120,768]{2,1,0:T(8,128)(2,1)}, u32[]{:S(2)}, u32[]{:S(2)}) collective-permute-start(bf16[4,120,768]{2,1,0:T(8,128)(2,1)} %get-tuple-element.316), channel_id=1, source_target_pairs={{0,2},{1,3},{2,0},{3,1},{4,6},{5,7},{6,4},{7,5},{8,10},{9,11},{10,... | collective-permute-start | bytes 2211848 | tf_op jit(solution)/shard_map/ppermute | solution.py:52
  254.5 33.3 %collective-permute-start.41 = (bf16[4,120,768]{2,1,0:T(8,128)(2,1)}, bf16[4,120,768]{2,1,0:T(8,128)(2,1)}, u32[]{:S(2)}, u32[]{:S(2)}) collective-permute-start(bf16[4,120,768]{2,1,0:T(8,128)(2,1)} %get-tuple-element.317), channel_id=1, source_target_pairs={{0,4},{1,5},{2,6},{3,7},{4,0},{5,1},{6,2},{7,3},{8,12},{9,13},{10,... | collective-permute-start | bytes 2211848 | tf_op jit(solution)/shard_map/ppermute | solution.py:52
  255.7 32.1 %all-to-all-start.7 = ((bf16[4,192,384]{2,1,0:T(8,128)(2,1)}), bf16[4,192,384]{2,1,0:T(8,128)(2,1)S(1)}, u32[]{:S(2)}, u32[]{:S(2)}) async-start(bf16[4,192,384]{2,1,0:T(8,128)(2,1)} %shard_map.253), calls=%async_computation.7 | async-start | bytes 1179648 | tf_op jit(solution)/shard_map/all_to_all | solution.py:61
  287.8 6.3 %collective-permute-start.42 = (bf16[2,8,48,1152]{3,2,1,0:T(8,128)(2,1)}, bf16[2,8,48,1152]{3,2,1,0:T(8,128)(2,1)S(1)}, u32[]{:S(2)}, u32[]{:S(2)}) collective-permute-start(bf16[2,8,48,1152]{3,2,1,0:T(8,128)(2,1)} %get-tuple-element.319), channel_id=1, source_target_pairs={{0,1},{1,0},{2,3},{3,2},{4,5},{5,4},{6,7},{7,6},{8,9},{9,8},{10,11... | collective-permute-start | bytes 5308424 | tf_op jit(solution)/shard_map/ppermute | solution.py:46
  295.2 20.5 %all-to-all-start.8 = ((bf16[4,128,768]{2,1,0:T(8,128)(2,1)}), bf16[4,128,768]{2,1,0:T(8,128)(2,1)S(1)}, u32[]{:S(2)}, u32[]{:S(2)}) async-start(bf16[4,128,768]{2,1,0:T(8,128)(2,1)} %bitcast.121), calls=%async_computation.8 | async-start | bytes 1572864 | tf_op jit(solution)/shard_map/all_to_all | solution.py:112
  301.8 11.2 %collective-permute-start.43 = (bf16[120,768]{1,0:T(8,128)(2,1)}, bf16[120,768]{1,0:T(8,128)(2,1)S(1)}, u32[]{:S(2)}, u32[]{:S(2)}) collective-permute-start(bf16[120,768]{1,0:T(8,128)(2,1)} %get-tuple-element.335), channel_id=1, source_target_pairs={{0,8},{4,12},{8,0},{12,4},{16,24},{20,28},{24,16},{28,20},{1,9},{5... | collective-permute-start | bytes 552968 | tf_op jit(solution)/shard_map/ppermute | solution.py:46
  303.9 11.8 %collective-permute-start.44 = (bf16[120,768]{1,0:T(8,128)(2,1)}, bf16[120,768]{1,0:T(8,128)(2,1)S(1)}, u32[]{:S(2)}, u32[]{:S(2)}) collective-permute-start(bf16[120,768]{1,0:T(8,128)(2,1)} %get-tuple-element.336), channel_id=1, source_target_pairs={{0,16},{4,20},{8,24},{12,28},{16,0},{20,4},{24,8},{28,12},{1,17},{... | collective-permute-start | bytes 552968 | tf_op jit(solution)/shard_map/ppermute | solution.py:46
  316.7 30.2 %all-to-all-start.9 = ((bf16[4,128,768]{2,1,0:T(8,128)(2,1)}), bf16[4,128,768]{2,1,0:T(8,128)(2,1)S(1)}, u32[]{:S(2)}, u32[]{:S(2)}) async-start(bf16[4,128,768]{2,1,0:T(8,128)(2,1)} %broadcast_select_fusion), calls=%async_computation.9 | async-start | bytes 1572864 | tf_op jit(solution)/shard_map/all_to_all | solution.py:61
  321.9 18.7 %collective-permute-start.48 = (bf16[120,768]{1,0:T(8,128)(2,1)S(1)}, bf16[120,768]{1,0:T(8,128)(2,1)S(1)}, u32[]{:S(2)}, u32[]{:S(2)}) collective-permute-start(bf16[120,768]{1,0:T(8,128)(2,1)S(1)} %copy-done.34), channel_id=1, source_target_pairs={{0,24},{4,28},{8,16},{12,20},{16,8},{20,12},{24,0},{28,4},{1,25},{... | collective-permute-start | bytes 552968 | tf_op jit(solution)/shard_map/ppermute | solution.py:46
  325.7 14.9 %collective-permute-start.45 = (bf16[4,48,1152]{2,1,0:T(8,128)(2,1)S(1)}, bf16[4,48,1152]{2,1,0:T(8,128)(2,1)S(1)}, u32[]{:S(2)}, u32[]{:S(2)}) collective-permute-start(bf16[4,48,1152]{2,1,0:T(8,128)(2,1)S(1)} %copy-done.33), channel_id=1, source_target_pairs={{0,6},{1,7},{2,4},{3,5},{4,2},{5,3},{6,0},{7,1},{8,14},{9,15},{10,... | collective-permute-start | bytes 1327112 | tf_op jit(solution)/shard_map/ppermute | solution.py:52
  327.6 18.4 %collective-permute-start.46 = (bf16[4,48,1152]{2,1,0:T(8,128)(2,1)S(1)}, bf16[4,48,1152]{2,1,0:T(8,128)(2,1)S(1)}, u32[]{:S(2)}, u32[]{:S(2)}) collective-permute-start(bf16[4,48,1152]{2,1,0:T(8,128)(2,1)S(1)} %copy-done.32), channel_id=1, source_target_pairs={{0,2},{1,3},{2,0},{3,1},{4,6},{5,7},{6,4},{7,5},{8,10},{9,11},{10,... | collective-permute-start | bytes 1327112 | tf_op jit(solution)/shard_map/ppermute | solution.py:52
  328.0 18.9 %collective-permute-start.47 = (bf16[4,48,1152]{2,1,0:T(8,128)(2,1)S(1)}, bf16[4,48,1152]{2,1,0:T(8,128)(2,1)}, u32[]{:S(2)}, u32[]{:S(2)}) collective-permute-start(bf16[4,48,1152]{2,1,0:T(8,128)(2,1)S(1)} %copy-done.31), channel_id=1, source_target_pairs={{0,4},{1,5},{2,6},{3,7},{4,0},{5,1},{6,2},{7,3},{8,12},{9,13},{10,... | collective-permute-start | bytes 1327112 | tf_op jit(solution)/shard_map/ppermute | solution.py:52
  349.4 13.2 %all-to-all-start.10 = ((f32[32,1,384]{2,1,0:T(1,128)}), f32[32,1,384]{2,1,0:T(1,128)S(1)}, u32[]{:S(2)}, u32[]{:S(2)}) async-start(f32[32,1,384]{2,1,0:T(1,128)} %copy.65), calls=%async_computation.10 | async-start | bytes 98304 | tf_op jit(solution)/shard_map/all_to_all | solution.py:1300
  356.6 8.9 %collective-permute-start.49 = (bf16[48,1152]{1,0:T(8,128)(2,1)}, bf16[48,1152]{1,0:T(8,128)(2,1)S(1)}, u32[]{:S(2)}, u32[]{:S(2)}) collective-permute-start(bf16[48,1152]{1,0:T(8,128)(2,1)} %get-tuple-element.361), channel_id=1, source_target_pairs={{0,8},{4,12},{8,0},{12,4},{16,24},{20,28},{24,16},{28,20},{1,9},{5... | collective-permute-start | bytes 331784 | tf_op jit(solution)/shard_map/ppermute | solution.py:46
  358.4 11.8 %collective-permute-start.50 = (bf16[48,1152]{1,0:T(8,128)(2,1)}, bf16[48,1152]{1,0:T(8,128)(2,1)S(1)}, u32[]{:S(2)}, u32[]{:S(2)}) collective-permute-start(bf16[48,1152]{1,0:T(8,128)(2,1)} %get-tuple-element.362), channel_id=1, source_target_pairs={{0,16},{4,20},{8,24},{12,28},{16,0},{20,4},{24,8},{28,12},{1,17},{... | collective-permute-start | bytes 331784 | tf_op jit(solution)/shard_map/ppermute | solution.py:46
  360.8 9.4 %collective-permute-start.51 = (bf16[48,1152]{1,0:T(8,128)(2,1)}, bf16[48,1152]{1,0:T(8,128)(2,1)S(1)}, u32[]{:S(2)}, u32[]{:S(2)}) collective-permute-start(bf16[48,1152]{1,0:T(8,128)(2,1)} %get-tuple-element.363), channel_id=1, source_target_pairs={{0,24},{4,28},{8,16},{12,20},{16,8},{20,12},{24,0},{28,4},{1,25},{... | collective-permute-start | bytes 331784 | tf_op jit(solution)/shard_map/ppermute | solution.py:46
  (50 other events, 501.1 us)

commit v3 on v2

--- a/solution.py
+++ b/solution.py
@@ -707,6 +707,7 @@
 
 
 def norm_back(grad, unit, scale, gain):
+    unit = unit.astype(F32)
     e = grad * gain
     part = jnp.mean(e * unit, axis=-1, keepdims=True)
     return (e - jnp.mean(e, axis=-1, keepdims=True) - unit * part) * scale
@@ -751,8 +752,9 @@
     def body(at, sums):
         branch = acc[at] + rows[2:3]
         residual = x[at].astype(F32) + branch
-        unit[at], scale[at] = norm_parts(residual)
-        normed[at] = unit[at] * rows[6:7] + rows[3:4]
+        value, scale[at] = norm_parts(residual)
+        unit[at] = value.astype(BF)
+        normed[at] = value * rows[6:7] + rows[3:4]
         low[at] = normed[at].astype(BF)
         return tuple(
             s + column_sum(valid[at] * value * value) for s, value in zip(sums, (residual, branch))
@@ -764,7 +766,7 @@
 
 def branch_layer(context, w_out, inputs, rows, valid):
     t, d = inputs.shape
-    outs = [((t, d), F32), ((t, d), BF), ((t, d), F32), ((t, 1), F32), ((2, 128), F32)]
+    outs = [((t, d), F32), ((t, d), BF), ((t, d), BF), ((t, 1), F32), ((2, 128), F32)]
     scratch = [pltpu.VMEM((t, d), F32)]
     return calls(branch_kernel, outs, 5, scratch_shapes=scratch)(
         context, w_out, inputs, rows, valid
@@ -812,8 +814,9 @@
         def body(at, sums):
             ffn_out = acc[at] + rows[4:5]
             residual = normed[at] + ffn_out
-            unit[at], scale[at] = norm_parts(residual)
-            low[at] = (unit[at] * rows[7:8] + rows[5:6]).astype(BF)
+            value, scale[at] = norm_parts(residual)
+            unit[at] = value.astype(BF)
+            low[at] = (value * rows[7:8] + rows[5:6]).astype(BF)
             values = (valid[at] * residual * residual, valid[at] * ffn_out * ffn_out)
             return tuple(s + column_sum(value) for s, value in zip(sums, values))
 
@@ -830,7 +833,7 @@
 def output_layer(place, active, pieces, plan, normed, rows, valid, hot):
     t, ff = active.shape
     d = normed.shape[1]
-    outs = [((t, d), BF), ((t, d), F32), ((t, 1), F32), ((hot.shape[0], d), BF), ((3, 128), F32)]
+    outs = [((t, d), BF), ((t, d), BF), ((t, 1), F32), ((hot.shape[0], d), BF), ((3, 128), F32)]
     outs.append(((ff, d), BF))
     return calls(
         functools.partial(output_kernel, plan, place.wide * place.narrow // LEVELS),
@@ -861,7 +864,7 @@
         )
         grad[at] = norm_back(grad_out, unit[at], scale[at], rows[7:8])
         low[at] = grad[at].astype(BF)
-        values = (grad_out * unit[at], grad_out, low[at].astype(F32))
+        values = (grad_out * unit[at].astype(F32), grad_out, low[at].astype(F32))
         return tuple(t + column_sum(value) for t, value in zip(totals, values))
 
     for i, value in enumerate(by_rows(grad.shape[0], body, (zero,) * 3)):
@@ -899,7 +902,7 @@
             value = acc[at]
             branch[at] = norm_back(value, unit[at], scale[at], rows[6:7]).astype(BF)
             store_blocks(blocks, at, branch[at])
-            values = (value * unit[at], value, branch[at].astype(F32))
+            values = (value * unit[at].astype(F32), value, branch[at].astype(F32))
             return tuple(t + column_sum(value) for t, value in zip(totals, values))
 
         for i, value in enumerate(by_rows(acc.shape[0], body, (zero,) * 3)):
@@ -1295,7 +1298,7 @@
         swapped = swap_out(place, in_four)
         packed = pack_sums(devices, sums_qkv, sums_one, sums_two, inb_sums, stats_one, stats_two)
         grad_w_back = finish_back(levels_c)
-        columns_a, swapped, packed, levels_b = phase(columns_a, swapped, packed, levels_b)
+        columns_a, swapped, packed = phase(columns_a, swapped, packed)
 
         packed = lax.all_to_all(packed, BOTH, 0, 0, tiled=True)
         levels_a = swap_shares(place, level_shares(place, columns_a))

time: 374 us -> 372 us (level)
  waiting for transfers between devices: 77.9 us -> 82.3 us
    ppermute x21, waiting for transfers between devices: 12.7 us -> 17.1 us  [flip_both(): return lax.ppermute(x, BOTH, [(i, i ^ mask) for i in range(wide * narrow)])]
    ppermute x28, starting transfers between devices: 26.5 us -> 22.7 us  [flip(): return lax.ppermute(x, axis, [(i, i ^ mask) for i in range(size)])]
  transfers between devices with their start and end apart: 63 -> 63, of which waited for: 28 -> 30; matrix products, arithmetic and copies ran while one was open for 5% -> 5% of each run, Pallas kernels for 39% -> 39%
where the time goes in v3:
time: 372 us; the launch traced here: 370 us
  Pallas kernels  155 us (42%)
  starting transfers between devices  96.9 us (26%)
  waiting for transfers between devices  82.3 us (22%)
  other arithmetic  23 us (6%)
  local copies, waits for them, and re-layouts  12 us (3%)
    ppermute x28, waiting for transfers between devices, flip(): return lax.ppermute(x, axis, [(i, i ^ mask) for i in range(size)])  40.5 us
    ppermute x21, starting transfers between devices, flip_both(): return lax.ppermute(x, BOTH, [(i, i ^ mask) for i in range(wide * narrow)])  24.6 us
    ppermute x28, starting transfers between devices, flip(): return lax.ppermute(x, axis, [(i, i ^ mask) for i in range(size)])  22.7 us
    all_to_all x6, starting transfers between devices, across_levels(): return lax.all_to_all(x, 'wide', 0, 0, axis_index_groups=groups, tiled=True)  22.6 us
    pallas_call x1, Pallas kernels, attend_back(): pl.pallas_call(attend_back_kernel, grid=(d // width,), in_specs=[pl.Block...  20.3 us
    ppermute x21, waiting for transfers between devices, flip_both(): return lax.ppermute(x, BOTH, [(i, i ^ mask) for i in range(wide * narrow)])  17.1 us
    pallas_call x2, Pallas kernels, products(): pl.pallas_call(functools.partial(product_kernel, step), grid_spec=grid_sp...  16 us
    ppermute x3, waiting for transfers between devices, swap_levels(): return lax.ppermute(x, 'wide', pairs)  15.8 us
  transfers between devices with their start and end apart: 63, of which 30 were waited for; matrix products, arithmetic and copies ran while one was open for 5% of the time, Pallas kernels for 39%

profile of v3, /device:TPU:0, one launch (start us, length us, event | category | flops | bytes accessed | tf_op | source)
XLA Modules:
  0.0 370.3 jit_solution(7670558627818266330)
XLA Ops:
  7.1 5.0 %collective-permute-start.2 = (bf16[80,768]{1,0:T(8,128)(2,1)}, bf16[80,768]{1,0:T(8,128)(2,1)S(1)}, u32[]{:S(2)}, u32[]{:S(2)}) collective-permute-start(bf16[80,768]{1,0:T(8,128)(2,1)} %get-tuple-element.190), channel_id=1, source_target_pairs={{0,24},{4,28},{8,16},{12,20},{16,8},{20,12},{24,0},{28,4},{1,25},{... | collective-permute-start | bytes 368648 | tf_op jit(solution)/shard_map/ppermute | solution.py:46
  12.8 3.8 %collective-permute-done.2 = bf16[80,768]{1,0:T(8,128)(2,1)S(1)} collective-permute-done((bf16[80,768]{1,0:T(8,128)(2,1)}, bf16[80,768]{1,0:T(8,128)(2,1)S(1)}, u32[]{:S(2)}, u32[]{:S(2)}) %collective-permute-start.2) | collective-permute-done | bytes 122912 | tf_op jit(solution)/shard_map/ppermute | solution.py:46
  16.6 2.8 collective-permute-done
  19.4 3.3 collective-permute-done.1
  24.8 3.7 %all-to-all-start = ((bf16[4,24,3840]{2,1,0:T(8,128)(2,1)}), bf16[4,24,3840]{2,1,0:T(8,128)(2,1)S(1)}, u32[]{:S(2)}, u32[]{:S(2)}) async-start(bf16[4,24,3840]{2,1,0:T(8,128)(2,1)} %broadcast_select_fusion.2), calls=%async_computation | async-start | bytes 1474560 | tf_op jit(solution)/shard_map/all_to_all | solution.py:61
  32.1 3.9 %collective-permute-start.6 = (bf16[128,768]{1,0:T(8,128)(2,1)S(1)}, bf16[128,768]{1,0:T(8,128)(2,1)S(1)}, u32[]{:S(2)}, u32[]{:S(2)}) collective-permute-start(bf16[128,768]{1,0:T(8,128)(2,1)S(1)} %get-tuple-element.415), channel_id=1, source_target_pairs={{0,8},{8,0},{4,12},{12,4},{1,9},{9,1},{5,13},{13,5},{2,10},{10,2},... | collective-permute-start | bytes 589832 | tf_op jit(solution)/shard_map/ppermute | solution.py:68
  37.9 8.0 %collective-permute-done.6 = bf16[128,768]{1,0:T(8,128)(2,1)S(1)} collective-permute-done((bf16[128,768]{1,0:T(8,128)(2,1)S(1)}, bf16[128,768]{1,0:T(8,128)(2,1)S(1)}, u32[]{:S(2)}, u32[]{:S(2)}) %collective-permute-start.6) | collective-permute-done | bytes 196640 | tf_op jit(solution)/shard_map/ppermute | solution.py:68
  47.9 7.8 %collective-permute-done.7 = bf16[128,768]{1,0:T(8,128)(2,1)S(1)} collective-permute-done((bf16[128,768]{1,0:T(8,128)(2,1)S(1)}, bf16[128,768]{1,0:T(8,128)(2,1)S(1)}, u32[]{:S(2)}, u32[]{:S(2)}) %collective-permute-start.7) | collective-permute-done | bytes 196640 | tf_op jit(solution)/shard_map/ppermute | solution.py:68
  62.0 3.5 all-to-all-start.1
  65.6 2.9 collective-permute-start.13
  69.2 8.4 %all-to-all-done.1 = bf16[4,128,768]{2,1,0:T(8,128)(2,1)S(1)} async-done(((bf16[4,128,768]{2,1,0:T(8,128)(2,1)}), bf16[4,128,768]{2,1,0:T(8,128)(2,1)S(1)}, u32[]{:S(2)}, u32[]{:S(2)}) %all-to-all-start.1) | async-done | bytes 786464 | tf_op jit(solution)/shard_map/all_to_all | solution.py:107
  77.6 5.4 %shard_map.239 = (bf16[3,32,24,768]{3,2,1,0:T(8,128)(2,1)}, bf16[1,32,8,768]{3,2,1,0:T(8,128)(2,1)}) custom-call(s32[1]{0:T(128)} %bitcast.21.me_ref, bf16[4,80,768]{2,1,0:T(8,128)(2,1)} %copy-done.5, bf16[4,80,768]{2,1,0:T(8,128)(2,1)} %copy-done.11, bf16[4,80,768]{2,1,0:T(8,128)(2,1)} %copy-done.12, bf16[4,80,768]{2,1,0:T(8,128)(2,1)} %collective-permute-done.5.refs_3_, ...), custom_call_target="tpu_custom_call" | custom-call | flops 115000000 | bytes 1024 | tf_op jit(solution)/shard_map/pallas_call | solution.py:157
  84.9 3.5 all-to-all-start.2
  92.3 13.2 %shard_map.241 = (bf16[3,512,768]{2,1,0:T(8,128)(2,1)}, bf16[512,768]{1,0:T(8,128)(2,1)}, f32[3,4,512]{2,1,0:T(4,128)}) custom-call(bf16[512,768]{1,0:T(8,128)(2,1)} %bitcast.112, bf16[3,768,768]{2,1,0:T(8,128)(2,1)} %bitcast.110, f32[8,768]{1,0:T(8,128)} %get-tuple-element.226.rows_ref.rows, s32[1,512]{1,0:T(1,128)} %bitcast.136, s32[512,1]{1,0:T(8,128)} %copy.58.seg_col_ref), custom_call_target="tpu_custom_call" | custom-call | flops 115000000 | bytes 1024 | tf_op jit(solution)/shard_map/pallas_call | solution.py:565
  105.5 3.3 collective-permute-done.14.refs_2_
  119.1 3.5 all-to-all-start.3
  122.6 6.7 %shard_map.242 = (bf16[1,32,24,768]{3,2,1,0:T(8,128)(2,1)}, bf16[4,32,24,768]{3,2,1,0:T(8,128)(2,1)}) custom-call(s32[1]{0:T(128)} %bitcast.21.me_ref, bf16[4,24,3840]{2,1,0:T(8,128)(2,1)} %copy-done.1, bf16[4,24,3840]{2,1,0:T(8,128)(2,1)} %copy-done.9, bf16[4,24,3840]{2,1,0:T(8,128)(2,1)} %collective-permute-done.14.refs_2_, ...), custom_call_target="tpu_custom_call" | custom-call | flops 115000000 | bytes 1024 | tf_op jit(solution)/shard_map/pallas_call | solution.py:157
  129.4 5.5 %shard_map.243 = (f32[512,768]{1,0:T(8,128)}, bf16[512,768]{1,0:T(8,128)(2,1)}, bf16[512,768]{1,0:T(8,128)(2,1)}, f32[512,1]{1,0:T(8,128)}, f32[2,128]{1,0:T(2,128)}) custom-call(bf16[512,768]{1,0:T(8,128)(2,1)} %get-tuple-element.230.ctx.refs_0_, bf16[1,768,768]{2,1,0:T(8,128)(2,1)} %bitcast.144, bf16[512,768]{1,0:T(8,128)(2,1)} %bitcast.113, ...), custom_call_target="tpu_custom_call" | custom-call | flops 5750000128 | bytes 1024 | tf_op jit(solution)/shard_map/pallas_call | solution.py:771
  134.9 9.2 %shard_map.244 = (bf16[512,3072]{1,0:T(8,128)(2,1)}, bf16[512,3072]{1,0:T(8,128)(2,1)}) custom-call(bf16[512,768]{1,0:T(8,128)(2,1)} %get-tuple-element.247.x_ref.refs_2_, bf16[4,768,768]{2,1,0:T(8,128)(2,1)} %bitcast.142, f32[1,3072]{1,0:T(1,128)} %get-tuple-element.249.bias_ref), custom_call_target="tpu_custom_call" | custom-call | flops 9200000000 | bytes 1024 | tf_op jit(solution)/shard_map/pallas_call | solution.py:686
  147.1 3.7 all-to-all-start.4
  150.8 12.6 %shard_map.245 = (bf16[512,768]{1,0:T(8,128)(2,1)}, bf16[512,768]{1,0:T(8,128)(2,1)}, f32[512,1]{1,0:T(8,128)}, bf16[32,768]{1,0:T(8,128)(2,1)}, f32[3,128]{1,0:T(4,128)}, /*index=5*/bf16[3072,768]{1,0:T(8,128)(2,1)}) custom-call(s32[1]{0:T(128)} %bitcast.21.me_ref, bf16[512,3072]{1,0:T(8,128)(2,1)} %get-tuple-element.254.active.left_ref, ...), custom_call_target="tpu_custom_call" | custom-call | flops 10350000128 | bytes 1024 | tf_op jit(solution)/shard_map/pallas_call | solution.py:838
  163.4 3.8 %collective-permute-start.27 = (bf16[32,768]{1,0:T(8,128)(2,1)}, bf16[32,768]{1,0:T(8,128)(2,1)S(1)}, u32[]{:S(2)}, u32[]{:S(2)}) collective-permute-start(bf16[32,768]{1,0:T(8,128)(2,1)} %get-tuple-element.263), channel_id=1, source_target_pairs={{0,24},{4,28},{8,16},{12,20},{16,8},{20,12},{24,0},{28,4},{1,25},{... | collective-permute-start | bytes 147464 | tf_op jit(solution)/shard_map/ppermute | solution.py:46
  169.8 2.8 collective-permute-done.28
  173.4 2.7 collective-permute-start.30
  182.8 2.6 shard_map.246.pool
  185.4 3.5 all-to-all-start.5
  188.9 5.8 %shard_map.247 = (f32[512,768]{1,0:T(8,128)}, bf16[512,768]{1,0:T(8,128)(2,1)}, f32[3,768]{1,0:T(4,128)}) custom-call(bf16[512,768]{1,0:T(8,128)(2,1)} %bitcast.120, f32[512,1]{1,0:T(8,128)} %compare_convert_fusion.valid, f32[32,512]{1,0:T(8,128)} %fusion.14.hot, f32[32,768]{1,0:T(8,128)} %shard_map.246.pool, bf16[512,768]{1,0:T(8,128)(2,1)} %get-tuple-element.266.unit, ...), custom_call_target="tpu_custom_call" | custom-call | flops 6899999744 | bytes 1024 | tf_op jit(solution)/shard_map/pallas_call | solution.py:877
  194.7 7.2 %shard_map.248 = (bf16[2,8,192,384]{3,2,1,0:T(8,128)(2,1)}, bf16[2,8,192,384]{3,2,1,0:T(8,128)(2,1)}) custom-call(s32[1]{0:T(128)} %bitcast.34.core_ref, bf16[512,3072]{1,0:T(8,128)(2,1)} %get-tuple-element.254.active.left_ref, bf16[512,768]{1,0:T(8,128)(2,1)} %get-tuple-element.277.right_ref.low), custom_call_target="tpu_custom_call" | custom-call | flops 8049999872 | bytes 1024 | tf_op jit(solution)/shard_map/pallas_call | solution.py:434
  204.0 3.5 all-to-all-start.6
  207.5 4.3 %shard_map.249 = (bf16[4,192,384]{2,1,0:T(8,128)(2,1)}, bf16[4,192,384]{2,1,0:T(8,128)(2,1)}, bf16[4,192,384]{2,1,0:T(8,128)(2,1)}, bf16[4,192,384]{2,1,0:T(8,128)(2,1)}) custom-call(s32[2]{0:T(128)} %pad_add_fusion.1.at_ref, bf16[2,4,2,192,384]{4,3,2,1,0:T(8,128)(2,1)} %bitcast.116, bf16[2,4,2,192,384]{4,3,2,1,0:T(8,128)(2,1)} %bitcast.46.got_ref), custom_call_target="tpu_custom_call" | custom-call | flops 1150000000 | bytes 1024 | tf_op jit(solution)/shard_map/pallas_call | solution.py:292
  215.4 13.7 %shard_map.250 = (bf16[512,3072]{1,0:T(8,128)(2,1)}, f32[1,3072]{1,0:T(1,128)}, bf16[512,768]{1,0:T(8,128)(2,1)}, bf16[4,512,192]{2,1,0:T(8,128)(2,1)}, f32[3,768]{1,0:T(4,128)}) custom-call(bf16[512,768]{1,0:T(8,128)(2,1)} %get-tuple-element.277.right_ref.low, bf16[3072,768]{1,0:T(8,128)(2,1)} %get-tuple-element.278.w_back, ...), custom_call_target="tpu_custom_call" | custom-call | flops 16099999744 | bytes 1024 | tf_op jit(solution)/shard_map/pallas_call | solution.py:923
  229.1 9.3 %shard_map.251 = (bf16[2,8,120,768]{3,2,1,0:T(8,128)(2,1)}, bf16[2,8,120,768]{3,2,1,0:T(8,128)(2,1)}) custom-call(s32[1]{0:T(128)} %bitcast.me_ref, bf16[512,768]{1,0:T(8,128)(2,1)} %get-tuple-element.230.ctx.refs_0_, bf16[4,512,192]{2,1,0:T(8,128)(2,1)} %get-tuple-element.283.refs_1_, bf16[512,768]{1,0:T(8,128)(2,1)} %get-tuple-element.247.x_ref.refs_2_, ...), custom_call_target="tpu_custom_call" | custom-call | flops 9200000000 | bytes 1024 | tf_op jit(solution)/shard_map/pallas_call | solution.py:387
  241.7 2.7 shard_map.253
  246.6 4.9 %shard_map.252 = (bf16[4,120,768]{2,1,0:T(8,128)(2,1)}, bf16[4,120,768]{2,1,0:T(8,128)(2,1)}, bf16[4,120,768]{2,1,0:T(8,128)(2,1)}, bf16[4,120,768]{2,1,0:T(8,128)(2,1)}) custom-call(s32[2]{0:T(128)} %pad_add_fusion.1.at_ref, bf16[2,4,2,120,768]{4,3,2,1,0:T(8,128)(2,1)} %bitcast.115, bf16[2,4,2,120,768]{4,3,2,1,0:T(8,128)(2,1)} %bitcast.49.got_ref), custom_call_target="tpu_custom_call" | custom-call | flops 1150000000 | bytes 1024 | tf_op jit(solution)/shard_map/pallas_call | solution.py:292
  255.0 4.8 %all-to-all-start.7 = ((bf16[4,192,384]{2,1,0:T(8,128)(2,1)}), bf16[4,192,384]{2,1,0:T(8,128)(2,1)S(1)}, u32[]{:S(2)}, u32[]{:S(2)}) async-start(bf16[4,192,384]{2,1,0:T(8,128)(2,1)} %shard_map.253), calls=%async_computation.7 | async-start | bytes 1179648 | tf_op jit(solution)/shard_map/all_to_all | solution.py:61
  259.8 20.3 %shard_map.254 = (bf16[3,512,768]{2,1,0:T(8,128)(2,1)}, bf16[4,512,576]{2,1,0:T(8,128)(2,1)}, f32[2,768]{1,0:T(2,128)}) custom-call(bf16[512,768]{1,0:T(8,128)(2,1)} %get-tuple-element.303.gb_ref.residual, bf16[768,768]{1,0:T(8,128)(2,1)} %bitcast.145, bf16[3,512,768]{2,1,0:T(8,128)(2,1)} %get-tuple-element.304.qkv_ref, ...), custom_call_target="tpu_custom_call" | custom-call | flops 23000000512 | bytes 1024 | tf_op jit(solution)/shard_map/pallas_call | solution.py:640
  280.1 6.8 %shard_map.255 = (bf16[2,8,48,1152]{3,2,1,0:T(8,128)(2,1)}, bf16[2,8,48,1152]{3,2,1,0:T(8,128)(2,1)}) custom-call(s32[1]{0:T(128)} %bitcast.me_ref, bf16[512,768]{1,0:T(8,128)(2,1)} %bitcast.114, bf16[4,512,576]{2,1,0:T(8,128)(2,1)} %get-tuple-element.306.refs_1_), custom_call_target="tpu_custom_call" | custom-call | flops 9200000000 | bytes 1024 | tf_op jit(solution)/shard_map/pallas_call | solution.py:387
  287.1 6.1 %shard_map.256 = bf16[512,768]{1,0:T(8,128)(2,1)} custom-call(bf16[3,512,768]{2,1,0:T(8,128)(2,1)} %get-tuple-element.316.grad, bf16[3,768,768]{2,1,0:T(8,128)(2,1)} %bitcast.111, bf16[512,768]{1,0:T(8,128)(2,1)} %get-tuple-element.303.gb_ref.residual), custom_call_target="tpu_custom_call" | custom-call | flops 6899999744 | bytes 1024 | tf_op jit(solution)/shard_map/pallas_call | solution.py:960
  293.2 3.5 all-to-all-start.8
  297.6 3.1 shard_map.258
  305.7 3.8 %shard_map.257 = (bf16[4,48,1152]{2,1,0:T(8,128)(2,1)}, bf16[4,48,1152]{2,1,0:T(8,128)(2,1)}, bf16[4,48,1152]{2,1,0:T(8,128)(2,1)}, bf16[4,48,1152]{2,1,0:T(8,128)(2,1)}) custom-call(s32[2]{0:T(128)} %pad_add_fusion.1.at_ref, bf16[2,4,2,48,1152]{4,3,2,1,0:T(8,128)(2,1)} %bitcast.147, bf16[2,4,2,48,1152]{4,3,2,1,0:T(8,128)(2,1)} %bitcast.52.got_ref), custom_call_target="tpu_custom_call" | custom-call | flops 1150000000 | bytes 1024 | tf_op jit(solution)/shard_map/pallas_call | solution.py:292
  311.6 7.6 %collective-permute-done.44 = bf16[120,768]{1,0:T(8,128)(2,1)S(1)} collective-permute-done((bf16[120,768]{1,0:T(8,128)(2,1)}, bf16[120,768]{1,0:T(8,128)(2,1)S(1)}, u32[]{:S(2)}, u32[]{:S(2)}) %collective-permute-start.44) | collective-permute-done | bytes 184352 | tf_op jit(solution)/shard_map/ppermute | solution.py:46
  320.2 3.6 all-to-all-start.9
  330.5 4.7 %shard_map.259 = f32[32,384]{1,0:T(8,128)} custom-call(f32[2,768]{1,0:T(2,128)} %get-tuple-element.341.attn, f32[3,768]{1,0:T(4,128)} %get-tuple-element.342.out, f32[3,768]{1,0:T(4,128)} %get-tuple-element.343.ffn, f32[1,3072]{1,0:T(1,128)} %get-tuple-element.344.inb, f32[2,128]{1,0:T(2,128)} %get-tuple-element.345.stats_a, f32[3,128]{1,0:T(4,128)} %get-tuple-element.346.stats_b), custom_call_target="tpu_custom_call" | custom-call | flops 4600000000 | bytes 1024 | tf_op jit(solution)/shard_map/pallas_call | solution.py:1044
  335.2 2.9 collective-permute-done.45.refs_0_
  338.2 6.2 %collective-permute-done.46.refs_1_ = bf16[4,48,1152]{2,1,0:T(8,128)(2,1)} collective-permute-done((bf16[4,48,1152]{2,1,0:T(8,128)(2,1)}, bf16[4,48,1152]{2,1,0:T(8,128)(2,1)}, u32[]{:S(2)}, u32[]{:S(2)}) %collective-permute-start.46) | collective-permute-done | bytes 442400 | tf_op jit(solution)/shard_map/ppermute | solution.py:52
  347.2 5.1 %all-to-all-start.10 = ((f32[32,1,384]{2,1,0:T(1,128)}), f32[32,1,384]{2,1,0:T(1,128)S(1)}, u32[]{:S(2)}, u32[]{:S(2)}) async-start(f32[32,1,384]{2,1,0:T(1,128)} %copy.65), calls=%async_computation.10 | async-start | bytes 98304 | tf_op jit(solution)/shard_map/all_to_all | solution.py:1303
  362.5 5.7 %collective-permute-done.49 = bf16[48,1152]{1,0:T(8,128)(2,1)S(1)} collective-permute-done((bf16[48,1152]{1,0:T(8,128)(2,1)}, bf16[48,1152]{1,0:T(8,128)(2,1)S(1)}, u32[]{:S(2)}, u32[]{:S(2)}) %collective-permute-start.49) | collective-permute-done | bytes 110624 | tf_op jit(solution)/shard_map/ppermute | solution.py:46
  (259 shorter events, 97.8 us)
Async XLA Ops:
  7.1 9.5 %collective-permute-start.2 = (bf16[80,768]{1,0:T(8,128)(2,1)}, bf16[80,768]{1,0:T(8,128)(2,1)S(1)}, u32[]{:S(2)}, u32[]{:S(2)}) collective-permute-start(bf16[80,768]{1,0:T(8,128)(2,1)} %get-tuple-element.190), channel_id=1, source_target_pairs={{0,24},{4,28},{8,16},{12,20},{16,8},{20,12},{24,0},{28,4},{1,25},{... | collective-permute-start | bytes 368648 | tf_op jit(solution)/shard_map/ppermute | solution.py:46
  12.2 7.2 %collective-permute-start = (bf16[80,768]{1,0:T(8,128)(2,1)}, bf16[80,768]{1,0:T(8,128)(2,1)S(1)}, u32[]{:S(2)}, u32[]{:S(2)}) collective-permute-start(bf16[80,768]{1,0:T(8,128)(2,1)} %get-tuple-element.188), channel_id=1, source_target_pairs={{0,8},{4,12},{8,0},{12,4},{16,24},{20,28},{24,16},{28,20},{1,9},{5... | collective-permute-start | bytes 368648 | tf_op jit(solution)/shard_map/ppermute | solution.py:46
  12.2 10.6 %collective-permute-start.1 = (bf16[80,768]{1,0:T(8,128)(2,1)}, bf16[80,768]{1,0:T(8,128)(2,1)S(1)}, u32[]{:S(2)}, u32[]{:S(2)}) collective-permute-start(bf16[80,768]{1,0:T(8,128)(2,1)} %get-tuple-element.189), channel_id=1, source_target_pairs={{0,16},{4,20},{8,24},{12,28},{16,0},{20,4},{24,8},{28,12},{1,17},{... | collective-permute-start | bytes 368648 | tf_op jit(solution)/shard_map/ppermute | solution.py:46
  24.8 31.7 %all-to-all-start = ((bf16[4,24,3840]{2,1,0:T(8,128)(2,1)}), bf16[4,24,3840]{2,1,0:T(8,128)(2,1)S(1)}, u32[]{:S(2)}, u32[]{:S(2)}) async-start(bf16[4,24,3840]{2,1,0:T(8,128)(2,1)} %broadcast_select_fusion.2), calls=%async_computation | async-start | bytes 1474560 | tf_op jit(solution)/shard_map/all_to_all | solution.py:61
  28.5 27.1 %collective-permute-start.3 = (bf16[4,80,768]{2,1,0:T(8,128)(2,1)S(1)}, bf16[4,80,768]{2,1,0:T(8,128)(2,1)S(1)}, u32[]{:S(2)}, u32[]{:S(2)}) collective-permute-start(bf16[4,80,768]{2,1,0:T(8,128)(2,1)S(1)} %pad_maximum_fusion.2.refs_0_), channel_id=1, source_target_pairs={{0,6},{1,7},{2,4},{3,5},{4,2},{5,3},{6,0},{7,1},{8,14},{9,15},{10,... | collective-permute-start | bytes 1474568 | tf_op jit(solution)/shard_map/ppermute | solution.py:52
  31.0 24.7 %collective-permute-start.4 = (bf16[4,80,768]{2,1,0:T(8,128)(2,1)S(1)}, bf16[4,80,768]{2,1,0:T(8,128)(2,1)S(1)}, u32[]{:S(2)}, u32[]{:S(2)}) collective-permute-start(bf16[4,80,768]{2,1,0:T(8,128)(2,1)S(1)} %pad_maximum_fusion.2.refs_0_), channel_id=1, source_target_pairs={{0,2},{1,3},{2,0},{3,1},{4,6},{5,7},{6,4},{7,5},{8,10},{9,11},{10,... | collective-permute-start | bytes 1474568 | tf_op jit(solution)/shard_map/ppermute | solution.py:52
  31.5 25.0 %collective-permute-start.5 = (bf16[4,80,768]{2,1,0:T(8,128)(2,1)S(1)}, bf16[4,80,768]{2,1,0:T(8,128)(2,1)}, u32[]{:S(2)}, u32[]{:S(2)}) collective-permute-start(bf16[4,80,768]{2,1,0:T(8,128)(2,1)S(1)} %pad_maximum_fusion.2.refs_0_), channel_id=1, source_target_pairs={{0,4},{1,5},{2,6},{3,7},{4,0},{5,1},{6,2},{7,3},{8,12},{9,13},{10,... | collective-permute-start | bytes 1474568 | tf_op jit(solution)/shard_map/ppermute | solution.py:52
  32.1 13.9 %collective-permute-start.6 = (bf16[128,768]{1,0:T(8,128)(2,1)S(1)}, bf16[128,768]{1,0:T(8,128)(2,1)S(1)}, u32[]{:S(2)}, u32[]{:S(2)}) collective-permute-start(bf16[128,768]{1,0:T(8,128)(2,1)S(1)} %get-tuple-element.415), channel_id=1, source_target_pairs={{0,8},{8,0},{4,12},{12,4},{1,9},{9,1},{5,13},{13,5},{2,10},{10,2},... | collective-permute-start | bytes 589832 | tf_op jit(solution)/shard_map/ppermute | solution.py:68
  36.0 19.7 %collective-permute-start.7 = (bf16[128,768]{1,0:T(8,128)(2,1)S(1)}, bf16[128,768]{1,0:T(8,128)(2,1)S(1)}, u32[]{:S(2)}, u32[]{:S(2)}) collective-permute-start(bf16[128,768]{1,0:T(8,128)(2,1)S(1)} %get-tuple-element.414), channel_id=1, source_target_pairs={{0,16},{16,0},{4,20},{20,4},{1,17},{17,1},{5,21},{21,5},{2,18},{18... | collective-permute-start | bytes 589832 | tf_op jit(solution)/shard_map/ppermute | solution.py:68
  46.0 9.7 %collective-permute-start.8 = (bf16[128,768]{1,0:T(8,128)(2,1)S(1)}, bf16[128,768]{1,0:T(8,128)(2,1)S(1)}, u32[]{:S(2)}, u32[]{:S(2)}) collective-permute-start(bf16[128,768]{1,0:T(8,128)(2,1)S(1)} %get-tuple-element.413), channel_id=1, source_target_pairs={{0,24},{24,0},{4,28},{28,4},{1,25},{25,1},{5,29},{29,5},{2,26},{26... | collective-permute-start | bytes 589832 | tf_op jit(solution)/shard_map/ppermute | solution.py:68
  62.0 15.6 %all-to-all-start.1 = ((bf16[4,128,768]{2,1,0:T(8,128)(2,1)}), bf16[4,128,768]{2,1,0:T(8,128)(2,1)S(1)}, u32[]{:S(2)}, u32[]{:S(2)}) async-start(bf16[4,128,768]{2,1,0:T(8,128)(2,1)} %maximum_select_fusion), calls=%async_computation.1 | async-start | bytes 1572864 | tf_op jit(solution)/shard_map/all_to_all | solution.py:107
  65.6 39.9 %collective-permute-start.13 = (bf16[4,24,3840]{2,1,0:T(8,128)(2,1)S(1)}, bf16[4,24,3840]{2,1,0:T(8,128)(2,1)S(1)}, u32[]{:S(2)}, u32[]{:S(2)}) collective-permute-start(bf16[4,24,3840]{2,1,0:T(8,128)(2,1)S(1)} %all-to-all-done.refs_0_), channel_id=1, source_target_pairs={{0,6},{1,7},{2,4},{3,5},{4,2},{5,3},{6,0},{7,1},{8,14},{9,15},{10,... | collective-permute-start | bytes 2211848 | tf_op jit(solution)/shard_map/ppermute | solution.py:52
  68.5 40.3 %collective-permute-start.14 = (bf16[4,24,3840]{2,1,0:T(8,128)(2,1)S(1)}, bf16[4,24,3840]{2,1,0:T(8,128)(2,1)}, u32[]{:S(2)}, u32[]{:S(2)}) collective-permute-start(bf16[4,24,3840]{2,1,0:T(8,128)(2,1)S(1)} %all-to-all-done.refs_0_), channel_id=1, source_target_pairs={{0,2},{1,3},{2,0},{3,1},{4,6},{5,7},{6,4},{7,5},{8,10},{9,11},{10,... | collective-permute-start | bytes 2211848 | tf_op jit(solution)/shard_map/ppermute | solution.py:52
  68.6 40.2 %collective-permute-start.15 = (bf16[4,24,3840]{2,1,0:T(8,128)(2,1)S(1)}, bf16[4,24,3840]{2,1,0:T(8,128)(2,1)}, u32[]{:S(2)}, u32[]{:S(2)}) collective-permute-start(bf16[4,24,3840]{2,1,0:T(8,128)(2,1)S(1)} %all-to-all-done.refs_0_), channel_id=1, source_target_pairs={{0,4},{1,5},{2,6},{3,7},{4,0},{5,1},{6,2},{7,3},{8,12},{9,13},{10,... | collective-permute-start | bytes 2211848 | tf_op jit(solution)/shard_map/ppermute | solution.py:52
  84.9 24.0 %all-to-all-start.2 = ((bf16[4,96,768]{2,1,0:T(8,128)(2,1)}), bf16[4,96,768]{2,1,0:T(8,128)(2,1)S(1)}, u32[]{:S(2)}, u32[]{:S(2)}) async-start(bf16[4,96,768]{2,1,0:T(8,128)(2,1)} %broadcast_select_fusion.3), calls=%async_computation.2 | async-start | bytes 1179648 | tf_op jit(solution)/shard_map/all_to_all | solution.py:61
  114.6 29.5 %collective-permute-start.20 = (bf16[4,96,768]{2,1,0:T(8,128)(2,1)S(1)}, bf16[4,96,768]{2,1,0:T(8,128)(2,1)S(1)}, u32[]{:S(2)}, u32[]{:S(2)}) collective-permute-start(bf16[4,96,768]{2,1,0:T(8,128)(2,1)S(1)} %all-to-all-done.2.refs_0_), channel_id=1, source_target_pairs={{0,6},{1,7},{2,4},{3,5},{4,2},{5,3},{6,0},{7,1},{8,14},{9,15},{10,... | collective-permute-start | bytes 1769480 | tf_op jit(solution)/shard_map/ppermute | solution.py:52
  116.0 28.2 %collective-permute-start.21 = (bf16[4,96,768]{2,1,0:T(8,128)(2,1)S(1)}, bf16[4,96,768]{2,1,0:T(8,128)(2,1)}, u32[]{:S(2)}, u32[]{:S(2)}) collective-permute-start(bf16[4,96,768]{2,1,0:T(8,128)(2,1)S(1)} %all-to-all-done.2.refs_0_), channel_id=1, source_target_pairs={{0,2},{1,3},{2,0},{3,1},{4,6},{5,7},{6,4},{7,5},{8,10},{9,11},{10,... | collective-permute-start | bytes 1769480 | tf_op jit(solution)/shard_map/ppermute | solution.py:52
  117.6 26.6 %collective-permute-start.22 = (bf16[4,96,768]{2,1,0:T(8,128)(2,1)S(1)}, bf16[4,96,768]{2,1,0:T(8,128)(2,1)}, u32[]{:S(2)}, u32[]{:S(2)}) collective-permute-start(bf16[4,96,768]{2,1,0:T(8,128)(2,1)S(1)} %all-to-all-done.2.refs_0_), channel_id=1, source_target_pairs={{0,4},{1,5},{2,6},{3,7},{4,0},{5,1},{6,2},{7,3},{8,12},{9,13},{10,... | collective-permute-start | bytes 1769480 | tf_op jit(solution)/shard_map/ppermute | solution.py:52
  119.1 25.1 %all-to-all-start.3 = ((bf16[4,128,768]{2,1,0:T(8,128)(2,1)}), bf16[4,128,768]{2,1,0:T(8,128)(2,1)S(1)}, u32[]{:S(2)}, u32[]{:S(2)}) async-start(bf16[4,128,768]{2,1,0:T(8,128)(2,1)} %maximum_select_fusion.1), calls=%async_computation.3 | async-start | bytes 1572864 | tf_op jit(solution)/shard_map/all_to_all | solution.py:61
  144.2 6.5 %collective-permute-start.23 = (bf16[4,96,768]{2,1,0:T(8,128)(2,1)S(1)}, bf16[4,96,768]{2,1,0:T(8,128)(2,1)}, u32[]{:S(2)}, u32[]{:S(2)}) collective-permute-start(bf16[4,96,768]{2,1,0:T(8,128)(2,1)S(1)} %all-to-all-done.2.refs_0_), channel_id=1, source_target_pairs={{0,1},{1,0},{2,3},{3,2},{4,5},{5,4},{6,7},{7,6},{8,9},{9,8},{10,11... | collective-permute-start | bytes 1769480 | tf_op jit(solution)/shard_map/ppermute | solution.py:46
  144.3 6.5 %collective-permute-start.24 = (bf16[4,96,768]{2,1,0:T(8,128)(2,1)S(1)}, bf16[4,96,768]{2,1,0:T(8,128)(2,1)}, u32[]{:S(2)}, u32[]{:S(2)}) collective-permute-start(bf16[4,96,768]{2,1,0:T(8,128)(2,1)S(1)} %collective-permute-done.20.refs_1_), channel_id=1, source_target_pairs={{0,1},{1,0},{2,3},{3,2},{4,5},{5,4},{6,7},{7,6},{8,9},{9,8},{10,11... | collective-permute-start | bytes 1769480 | tf_op jit(solution)/shard_map/ppermute | solution.py:46
  144.8 6.0 %collective-permute-start.25 = (bf16[4,96,768]{2,1,0:T(8,128)(2,1)}, bf16[4,96,768]{2,1,0:T(8,128)(2,1)}, u32[]{:S(2)}, u32[]{:S(2)}) collective-permute-start(bf16[4,96,768]{2,1,0:T(8,128)(2,1)} %collective-permute-done.21.refs_2_), channel_id=1, source_target_pairs={{0,1},{1,0},{2,3},{3,2},{4,5},{5,4},{6,7},{7,6},{8,9},{9,8},{10,11... | collective-permute-start | bytes 1769480 | tf_op jit(solution)/shard_map/ppermute | solution.py:46
  144.9 5.9 %collective-permute-start.26 = (bf16[4,96,768]{2,1,0:T(8,128)(2,1)}, bf16[4,96,768]{2,1,0:T(8,128)(2,1)}, u32[]{:S(2)}, u32[]{:S(2)}) collective-permute-start(bf16[4,96,768]{2,1,0:T(8,128)(2,1)} %collective-permute-done.22.refs_3_), channel_id=1, source_target_pairs={{0,1},{1,0},{2,3},{3,2},{4,5},{5,4},{6,7},{7,6},{8,9},{9,8},{10,11... | collective-permute-start | bytes 1769480 | tf_op jit(solution)/shard_map/ppermute | solution.py:46
  147.1 16.4 %all-to-all-start.4 = ((bf16[4,128,768]{2,1,0:T(8,128)(2,1)}), bf16[4,128,768]{2,1,0:T(8,128)(2,1)S(1)}, u32[]{:S(2)}, u32[]{:S(2)}) async-start(bf16[4,128,768]{2,1,0:T(8,128)(2,1)} %maximum_select_fusion.2), calls=%async_computation.4 | async-start | bytes 1572864 | tf_op jit(solution)/shard_map/all_to_all | solution.py:107
  163.4 6.3 %collective-permute-start.27 = (bf16[32,768]{1,0:T(8,128)(2,1)}, bf16[32,768]{1,0:T(8,128)(2,1)S(1)}, u32[]{:S(2)}, u32[]{:S(2)}) collective-permute-start(bf16[32,768]{1,0:T(8,128)(2,1)} %get-tuple-element.263), channel_id=1, source_target_pairs={{0,24},{4,28},{8,16},{12,20},{16,8},{20,12},{24,0},{28,4},{1,25},{... | collective-permute-start | bytes 147464 | tf_op jit(solution)/shard_map/ppermute | solution.py:46
  173.4 5.8 %collective-permute-start.30 = (bf16[1,32,768]{2,1,0:T(8,128)(2,1)S(1)}, bf16[1,32,768]{2,1,0:T(8,128)(2,1)S(1)}, u32[]{:S(2)}, u32[]{:S(2)}) collective-permute-start(bf16[1,32,768]{2,1,0:T(8,128)(2,1)S(1)} %get-tuple-element.406), channel_id=1, source_target_pairs={{0,6},{1,7},{2,4},{3,5},{4,2},{5,3},{6,0},{7,1},{8,14},{9,15},{10,... | collective-permute-start | bytes 147464 | tf_op jit(solution)/shard_map/ppermute | solution.py:52
  185.4 16.5 %all-to-all-start.5 = ((bf16[4,128,768]{2,1,0:T(8,128)(2,1)}), bf16[4,128,768]{2,1,0:T(8,128)(2,1)S(1)}, u32[]{:S(2)}, u32[]{:S(2)}) async-start(bf16[4,128,768]{2,1,0:T(8,128)(2,1)} %bitcast.45), calls=%async_computation.5 | async-start | bytes 1572864 | tf_op jit(solution)/shard_map/all_to_all | solution.py:112
  204.0 34.3 %all-to-all-start.6 = ((bf16[4,128,768]{2,1,0:T(8,128)(2,1)}), bf16[4,128,768]{2,1,0:T(8,128)(2,1)S(1)}, u32[]{:S(2)}, u32[]{:S(2)}) async-start(bf16[4,128,768]{2,1,0:T(8,128)(2,1)} %broadcast_select_fusion.1), calls=%async_computation.6 | async-start | bytes 1572864 | tf_op jit(solution)/shard_map/all_to_all | solution.py:61
  211.9 26.5 %collective-permute-start.35 = (bf16[4,192,384]{2,1,0:T(8,128)(2,1)}, bf16[4,192,384]{2,1,0:T(8,128)(2,1)S(1)}, u32[]{:S(2)}, u32[]{:S(2)}) collective-permute-start(bf16[4,192,384]{2,1,0:T(8,128)(2,1)} %get-tuple-element.287), channel_id=1, source_target_pairs={{0,6},{1,7},{2,4},{3,5},{4,2},{5,3},{6,0},{7,1},{8,14},{9,15},{10,... | collective-permute-start | bytes 1769480 | tf_op jit(solution)/shard_map/ppermute | solution.py:52
  213.5 26.8 %collective-permute-start.36 = (bf16[4,192,384]{2,1,0:T(8,128)(2,1)}, bf16[4,192,384]{2,1,0:T(8,128)(2,1)S(1)}, u32[]{:S(2)}, u32[]{:S(2)}) collective-permute-start(bf16[4,192,384]{2,1,0:T(8,128)(2,1)} %get-tuple-element.288), channel_id=1, source_target_pairs={{0,2},{1,3},{2,0},{3,1},{4,6},{5,7},{6,4},{7,5},{8,10},{9,11},{10,... | collective-permute-start | bytes 1769480 | tf_op jit(solution)/shard_map/ppermute | solution.py:52
  213.8 27.1 %collective-permute-start.37 = (bf16[4,192,384]{2,1,0:T(8,128)(2,1)}, bf16[4,192,384]{2,1,0:T(8,128)(2,1)S(1)}, u32[]{:S(2)}, u32[]{:S(2)}) collective-permute-start(bf16[4,192,384]{2,1,0:T(8,128)(2,1)} %get-tuple-element.289), channel_id=1, source_target_pairs={{0,4},{1,5},{2,6},{3,7},{4,0},{5,1},{6,2},{7,3},{8,12},{9,13},{10,... | collective-permute-start | bytes 1769480 | tf_op jit(solution)/shard_map/ppermute | solution.py:52
  251.5 35.3 %collective-permute-start.39 = (bf16[4,120,768]{2,1,0:T(8,128)(2,1)}, bf16[4,120,768]{2,1,0:T(8,128)(2,1)S(1)}, u32[]{:S(2)}, u32[]{:S(2)}) collective-permute-start(bf16[4,120,768]{2,1,0:T(8,128)(2,1)} %get-tuple-element.311), channel_id=1, source_target_pairs={{0,6},{1,7},{2,4},{3,5},{4,2},{5,3},{6,0},{7,1},{8,14},{9,15},{10,... | collective-permute-start | bytes 2211848 | tf_op jit(solution)/shard_map/ppermute | solution.py:52
  253.6 33.3 %collective-permute-start.40 = (bf16[4,120,768]{2,1,0:T(8,128)(2,1)}, bf16[4,120,768]{2,1,0:T(8,128)(2,1)}, u32[]{:S(2)}, u32[]{:S(2)}) collective-permute-start(bf16[4,120,768]{2,1,0:T(8,128)(2,1)} %get-tuple-element.312), channel_id=1, source_target_pairs={{0,2},{1,3},{2,0},{3,1},{4,6},{5,7},{6,4},{7,5},{8,10},{9,11},{10,... | collective-permute-start | bytes 2211848 | tf_op jit(solution)/shard_map/ppermute | solution.py:52
  253.8 33.3 %collective-permute-start.41 = (bf16[4,120,768]{2,1,0:T(8,128)(2,1)}, bf16[4,120,768]{2,1,0:T(8,128)(2,1)}, u32[]{:S(2)}, u32[]{:S(2)}) collective-permute-start(bf16[4,120,768]{2,1,0:T(8,128)(2,1)} %get-tuple-element.313), channel_id=1, source_target_pairs={{0,4},{1,5},{2,6},{3,7},{4,0},{5,1},{6,2},{7,3},{8,12},{9,13},{10,... | collective-permute-start | bytes 2211848 | tf_op jit(solution)/shard_map/ppermute | solution.py:52
  255.0 32.1 %all-to-all-start.7 = ((bf16[4,192,384]{2,1,0:T(8,128)(2,1)}), bf16[4,192,384]{2,1,0:T(8,128)(2,1)S(1)}, u32[]{:S(2)}, u32[]{:S(2)}) async-start(bf16[4,192,384]{2,1,0:T(8,128)(2,1)} %shard_map.253), calls=%async_computation.7 | async-start | bytes 1179648 | tf_op jit(solution)/shard_map/all_to_all | solution.py:61
  287.1 6.1 %collective-permute-start.42 = (bf16[2,8,48,1152]{3,2,1,0:T(8,128)(2,1)}, bf16[2,8,48,1152]{3,2,1,0:T(8,128)(2,1)}, u32[]{:S(2)}, u32[]{:S(2)}) collective-permute-start(bf16[2,8,48,1152]{3,2,1,0:T(8,128)(2,1)} %get-tuple-element.315), channel_id=1, source_target_pairs={{0,1},{1,0},{2,3},{3,2},{4,5},{5,4},{6,7},{7,6},{8,9},{9,8},{10,11... | collective-permute-start | bytes 5308424 | tf_op jit(solution)/shard_map/ppermute | solution.py:46
  293.2 26.0 %all-to-all-start.8 = ((bf16[4,128,768]{2,1,0:T(8,128)(2,1)}), bf16[4,128,768]{2,1,0:T(8,128)(2,1)S(1)}, u32[]{:S(2)}, u32[]{:S(2)}) async-start(bf16[4,128,768]{2,1,0:T(8,128)(2,1)} %bitcast.121), calls=%async_computation.8 | async-start | bytes 1572864 | tf_op jit(solution)/shard_map/all_to_all | solution.py:112
  300.7 11.0 %collective-permute-start.43 = (bf16[120,768]{1,0:T(8,128)(2,1)}, bf16[120,768]{1,0:T(8,128)(2,1)S(1)}, u32[]{:S(2)}, u32[]{:S(2)}) collective-permute-start(bf16[120,768]{1,0:T(8,128)(2,1)} %get-tuple-element.331), channel_id=1, source_target_pairs={{0,8},{4,12},{8,0},{12,4},{16,24},{20,28},{24,16},{28,20},{1,9},{5... | collective-permute-start | bytes 552968 | tf_op jit(solution)/shard_map/ppermute | solution.py:46
  302.7 16.5 %collective-permute-start.44 = (bf16[120,768]{1,0:T(8,128)(2,1)}, bf16[120,768]{1,0:T(8,128)(2,1)S(1)}, u32[]{:S(2)}, u32[]{:S(2)}) collective-permute-start(bf16[120,768]{1,0:T(8,128)(2,1)} %get-tuple-element.332), channel_id=1, source_target_pairs={{0,16},{4,20},{8,24},{12,28},{16,0},{20,4},{24,8},{28,12},{1,17},{... | collective-permute-start | bytes 552968 | tf_op jit(solution)/shard_map/ppermute | solution.py:46
  305.7 21.7 %collective-permute-start.51 = (bf16[120,768]{1,0:T(8,128)(2,1)}, bf16[120,768]{1,0:T(8,128)(2,1)S(1)}, u32[]{:S(2)}, u32[]{:S(2)}) collective-permute-start(bf16[120,768]{1,0:T(8,128)(2,1)} %get-tuple-element.359), channel_id=1, source_target_pairs={{0,24},{4,28},{8,16},{12,20},{16,8},{20,12},{24,0},{28,4},{1,25},{... | collective-permute-start | bytes 552968 | tf_op jit(solution)/shard_map/ppermute | solution.py:46
  320.2 24.7 %all-to-all-start.9 = ((bf16[4,128,768]{2,1,0:T(8,128)(2,1)}), bf16[4,128,768]{2,1,0:T(8,128)(2,1)S(1)}, u32[]{:S(2)}, u32[]{:S(2)}) async-start(bf16[4,128,768]{2,1,0:T(8,128)(2,1)} %broadcast_select_fusion), calls=%async_computation.9 | async-start | bytes 1572864 | tf_op jit(solution)/shard_map/all_to_all | solution.py:61
  323.8 14.3 %collective-permute-start.45 = (bf16[4,48,1152]{2,1,0:T(8,128)(2,1)}, bf16[4,48,1152]{2,1,0:T(8,128)(2,1)}, u32[]{:S(2)}, u32[]{:S(2)}) collective-permute-start(bf16[4,48,1152]{2,1,0:T(8,128)(2,1)} %get-tuple-element.337), channel_id=1, source_target_pairs={{0,6},{1,7},{2,4},{3,5},{4,2},{5,3},{6,0},{7,1},{8,14},{9,15},{10,... | collective-permute-start | bytes 1327112 | tf_op jit(solution)/shard_map/ppermute | solution.py:52
  326.0 18.3 %collective-permute-start.46 = (bf16[4,48,1152]{2,1,0:T(8,128)(2,1)}, bf16[4,48,1152]{2,1,0:T(8,128)(2,1)}, u32[]{:S(2)}, u32[]{:S(2)}) collective-permute-start(bf16[4,48,1152]{2,1,0:T(8,128)(2,1)} %get-tuple-element.338), channel_id=1, source_target_pairs={{0,2},{1,3},{2,0},{3,1},{4,6},{5,7},{6,4},{7,5},{8,10},{9,11},{10,... | collective-permute-start | bytes 1327112 | tf_op jit(solution)/shard_map/ppermute | solution.py:52
  326.1 18.8 %collective-permute-start.47 = (bf16[4,48,1152]{2,1,0:T(8,128)(2,1)}, bf16[4,48,1152]{2,1,0:T(8,128)(2,1)}, u32[]{:S(2)}, u32[]{:S(2)}) collective-permute-start(bf16[4,48,1152]{2,1,0:T(8,128)(2,1)} %get-tuple-element.339), channel_id=1, source_target_pairs={{0,4},{1,5},{2,6},{3,7},{4,0},{5,1},{6,2},{7,3},{8,12},{9,13},{10,... | collective-permute-start | bytes 1327112 | tf_op jit(solution)/shard_map/ppermute | solution.py:52
  347.2 12.4 %all-to-all-start.10 = ((f32[32,1,384]{2,1,0:T(1,128)}), f32[32,1,384]{2,1,0:T(1,128)S(1)}, u32[]{:S(2)}, u32[]{:S(2)}) async-start(f32[32,1,384]{2,1,0:T(1,128)} %copy.65), calls=%async_computation.10 | async-start | bytes 98304 | tf_op jit(solution)/shard_map/all_to_all | solution.py:1303
  354.7 7.9 %collective-permute-start.48 = (bf16[48,1152]{1,0:T(8,128)(2,1)}, bf16[48,1152]{1,0:T(8,128)(2,1)S(1)}, u32[]{:S(2)}, u32[]{:S(2)}) collective-permute-start(bf16[48,1152]{1,0:T(8,128)(2,1)} %get-tuple-element.353), channel_id=1, source_target_pairs={{0,8},{4,12},{8,0},{12,4},{16,24},{20,28},{24,16},{28,20},{1,9},{5... | collective-permute-start | bytes 331784 | tf_op jit(solution)/shard_map/ppermute | solution.py:46
  356.4 11.8 %collective-permute-start.49 = (bf16[48,1152]{1,0:T(8,128)(2,1)}, bf16[48,1152]{1,0:T(8,128)(2,1)S(1)}, u32[]{:S(2)}, u32[]{:S(2)}) collective-permute-start(bf16[48,1152]{1,0:T(8,128)(2,1)} %get-tuple-element.354), channel_id=1, source_target_pairs={{0,16},{4,20},{8,24},{12,28},{16,0},{20,4},{24,8},{28,12},{1,17},{... | collective-permute-start | bytes 331784 | tf_op jit(solution)/shard_map/ppermute | solution.py:46
  358.8 9.4 %collective-permute-start.50 = (bf16[48,1152]{1,0:T(8,128)(2,1)}, bf16[48,1152]{1,0:T(8,128)(2,1)S(1)}, u32[]{:S(2)}, u32[]{:S(2)}) collective-permute-start(bf16[48,1152]{1,0:T(8,128)(2,1)} %get-tuple-element.355), channel_id=1, source_target_pairs={{0,24},{4,28},{8,16},{12,20},{16,8},{20,12},{24,0},{28,4},{1,25},{... | collective-permute-start | bytes 331784 | tf_op jit(solution)/shard_map/ppermute | solution.py:46
  (41 other events, 453.2 us)

commit v4 on v3

--- a/solution.py
+++ b/solution.py
@@ -539,13 +539,9 @@
 def attend_kernel(x_ref, w_ref, rows_ref, seg_row_ref, seg_col_ref, qkv_ref, ctx_ref, lse_ref):
     x = x_ref[...]
     same = seg_col_ref[...] == seg_row_ref[...]
-
-    def project(part, carry):
-        bias = jnp.where(part == 0, rows_ref[0:1], jnp.where(part == 2, rows_ref[1:2], 0.0))
-        qkv_ref[part] = (matmul(x, w_ref[part]) + bias).astype(BF)
-        return carry
-
-    lax.fori_loop(0, 3, project, 0)
+    qkv_ref[0] = (matmul(x, w_ref[0]) + rows_ref[0:1]).astype(BF)
+    qkv_ref[1] = matmul(x, w_ref[1]).astype(BF)
+    qkv_ref[2] = (matmul(x, w_ref[2]) + rows_ref[1:2]).astype(BF)
     for h in range(GROUP):
         lanes = slice(h * HEAD_DIM, (h + 1) * HEAD_DIM)
         q, k, v = qkv_ref[0, :, lanes], qkv_ref[1, :, lanes], qkv_ref[2, :, lanes]
@@ -664,18 +660,12 @@
     )(grad_branch, w_out, qkv, lse, segment.reshape(1, t), segment.reshape(t, 1))
 
 
-def hidden_kernel(x_ref, w_ref, bias_ref, active_ref, slope_ref, pre_ref):
-    pre_ref[...] = matmul(x_ref[...], w_ref[0]) + bias_ref[...]
-
-    def body(at, carry):
-        pre = pre_ref[at]
-        below = 0.5 + 0.5 * lax.erf(pre * 0.5**0.5)
-        active_ref[at] = (pre * below).astype(BF)
-        density = jnp.exp(-0.5 * pre * pre) * (2.0 * math.pi) ** (-0.5)
-        slope_ref[at] = (below + pre * density).astype(BF)
-        return carry
-
-    by_rows(pre_ref.shape[0], body)
+def hidden_kernel(x_ref, w_ref, bias_ref, active_ref, slope_ref):
+    pre = matmul(x_ref[...], w_ref[0]) + bias_ref[...]
+    below = 0.5 + 0.5 * lax.erf(pre * 0.5**0.5)
+    active_ref[...] = (pre * below).astype(BF)
+    density = jnp.exp(-0.5 * pre * pre) * (2.0 * math.pi) ** (-0.5)
+    slope_ref[...] = (below + pre * density).astype(BF)
 
 
 def hidden_layer(x, w_in, in_bias):
@@ -693,7 +683,6 @@
         ],
         out_specs=[block, block],
         out_shape=[shape, shape],
-        scratch_shapes=[pltpu.VMEM((t, width), F32)],
         compiler_params=pltpu.CompilerParams(vmem_limit_bytes=VMEM),
         cost_estimate=cost(8),
     )(x, w_in, in_bias)
@@ -1300,8 +1289,10 @@
         grad_w_back = finish_back(levels_c)
         columns_a, swapped, packed = phase(columns_a, swapped, packed)
 
+        level_a = level_shares(place, columns_a)
+        level_a, packed = phase(level_a, packed)
+        levels_a = swap_shares(place, level_a)
         packed = lax.all_to_all(packed, BOTH, 0, 0, tiled=True)
-        levels_a = swap_shares(place, level_shares(place, columns_a))
         grad_w_out, grad_w_in = finish_out_in(place, levels_b, model_width // place.wide)
         passage_grad, query_grad = from_row(place, in_four, swapped)
         grad_w_qkv = finish_qkv(place, levels_a)

time: 372 us -> 370 us (level)
  transfers between devices with their start and end apart: 63 -> 63, of which waited for: 30 -> 31; matrix products, arithmetic and copies ran while one was open for 5% -> 6% of each run, Pallas kernels for 39% -> 38%
where the time goes in v4:
time: 370 us; the launch traced here: 368 us
  Pallas kernels  152 us (41%)
  starting transfers between devices  96.9 us (26%)
  waiting for transfers between devices  83.3 us (23%)
  other arithmetic  23.2 us (6%)
  local copies, waits for them, and re-layouts  12.1 us (3%)
    ppermute x28, waiting for transfers between devices, flip(): return lax.ppermute(x, axis, [(i, i ^ mask) for i in range(size)])  39 us
    ppermute x21, starting transfers between devices, flip_both(): return lax.ppermute(x, BOTH, [(i, i ^ mask) for i in range(wide * narrow)])  24.6 us
    ppermute x28, starting transfers between devices, flip(): return lax.ppermute(x, axis, [(i, i ^ mask) for i in range(size)])  22.7 us
    all_to_all x6, starting transfers between devices, across_levels(): return lax.all_to_all(x, 'wide', 0, 0, axis_index_groups=groups, tiled=True)  22.6 us
    pallas_call x1, Pallas kernels, attend_back(): pl.pallas_call(attend_back_kernel, grid=(d // width,), in_specs=[pl.Block...  20.3 us
    ppermute x21, waiting for transfers between devices, flip_both(): return lax.ppermute(x, BOTH, [(i, i ^ mask) for i in range(wide * narrow)])  18.7 us
    pallas_call x2, Pallas kernels, products(): pl.pallas_call(functools.partial(product_kernel, step), grid_spec=grid_sp...  16 us
    ppermute x3, waiting for transfers between devices, swap_levels(): return lax.ppermute(x, 'wide', pairs)  15.8 us
  transfers between devices with their start and end apart: 63, of which 31 were waited for; matrix products, arithmetic and copies ran while one was open for 6% of the time, Pallas kernels for 38%

profile of v4, /device:TPU:0, one launch (start us, length us, event | category | flops | bytes accessed | tf_op | source)
XLA Modules:
  0.0 368.4 jit_solution(5077216999280822177)
XLA Ops:
  7.1 5.0 %collective-permute-start.2 = (bf16[80,768]{1,0:T(8,128)(2,1)}, bf16[80,768]{1,0:T(8,128)(2,1)S(1)}, u32[]{:S(2)}, u32[]{:S(2)}) collective-permute-start(bf16[80,768]{1,0:T(8,128)(2,1)} %get-tuple-element.195), channel_id=1, source_target_pairs={{0,24},{4,28},{8,16},{12,20},{16,8},{20,12},{24,0},{28,4},{1,25},{... | collective-permute-start | bytes 368648 | tf_op jit(solution)/shard_map/ppermute | solution.py:46
  12.8 3.8 %collective-permute-done.2 = bf16[80,768]{1,0:T(8,128)(2,1)S(1)} collective-permute-done((bf16[80,768]{1,0:T(8,128)(2,1)}, bf16[80,768]{1,0:T(8,128)(2,1)S(1)}, u32[]{:S(2)}, u32[]{:S(2)}) %collective-permute-start.2) | collective-permute-done | bytes 122912 | tf_op jit(solution)/shard_map/ppermute | solution.py:46
  16.6 2.8 collective-permute-done
  19.4 3.3 collective-permute-done.1
  24.8 3.7 %all-to-all-start = ((bf16[4,24,3840]{2,1,0:T(8,128)(2,1)}), bf16[4,24,3840]{2,1,0:T(8,128)(2,1)S(1)}, u32[]{:S(2)}, u32[]{:S(2)}) async-start(bf16[4,24,3840]{2,1,0:T(8,128)(2,1)} %broadcast_select_fusion.2), calls=%async_computation | async-start | bytes 1474560 | tf_op jit(solution)/shard_map/all_to_all | solution.py:61
  28.5 2.4 collective-permute-start.3
  32.1 3.9 %collective-permute-start.6 = (bf16[128,768]{1,0:T(8,128)(2,1)S(1)}, bf16[128,768]{1,0:T(8,128)(2,1)S(1)}, u32[]{:S(2)}, u32[]{:S(2)}) collective-permute-start(bf16[128,768]{1,0:T(8,128)(2,1)S(1)} %get-tuple-element.425), channel_id=1, source_target_pairs={{0,8},{8,0},{4,12},{12,4},{1,9},{9,1},{5,13},{13,5},{2,10},{10,2},... | collective-permute-start | bytes 589832 | tf_op jit(solution)/shard_map/ppermute | solution.py:68
  37.9 8.0 %collective-permute-done.6 = bf16[128,768]{1,0:T(8,128)(2,1)S(1)} collective-permute-done((bf16[128,768]{1,0:T(8,128)(2,1)S(1)}, bf16[128,768]{1,0:T(8,128)(2,1)S(1)}, u32[]{:S(2)}, u32[]{:S(2)}) %collective-permute-start.6) | collective-permute-done | bytes 196640 | tf_op jit(solution)/shard_map/ppermute | solution.py:68
  47.9 7.8 %collective-permute-done.7 = bf16[128,768]{1,0:T(8,128)(2,1)S(1)} collective-permute-done((bf16[128,768]{1,0:T(8,128)(2,1)S(1)}, bf16[128,768]{1,0:T(8,128)(2,1)S(1)}, u32[]{:S(2)}, u32[]{:S(2)}) %collective-permute-start.7) | collective-permute-done | bytes 196640 | tf_op jit(solution)/shard_map/ppermute | solution.py:68
  62.0 3.5 all-to-all-start.1
  65.6 2.9 collective-permute-start.13
  69.2 8.4 %all-to-all-done.1 = bf16[4,128,768]{2,1,0:T(8,128)(2,1)S(1)} async-done(((bf16[4,128,768]{2,1,0:T(8,128)(2,1)}), bf16[4,128,768]{2,1,0:T(8,128)(2,1)S(1)}, u32[]{:S(2)}, u32[]{:S(2)}) %all-to-all-start.1) | async-done | bytes 786464 | tf_op jit(solution)/shard_map/all_to_all | solution.py:107
  77.6 5.4 %shard_map.239 = (bf16[3,32,24,768]{3,2,1,0:T(8,128)(2,1)}, bf16[1,32,8,768]{3,2,1,0:T(8,128)(2,1)}) custom-call(s32[1]{0:T(128)} %bitcast.21.me_ref, bf16[4,80,768]{2,1,0:T(8,128)(2,1)} %copy-done.5, bf16[4,80,768]{2,1,0:T(8,128)(2,1)} %copy-done.11, bf16[4,80,768]{2,1,0:T(8,128)(2,1)} %copy-done.12, bf16[4,80,768]{2,1,0:T(8,128)(2,1)} %collective-permute-done.5.refs_3_, ...), custom_call_target="tpu_custom_call" | custom-call | flops 115000000 | bytes 1024 | tf_op jit(solution)/shard_map/pallas_call | solution.py:157
  84.9 3.5 all-to-all-start.2
  92.3 11.2 %shard_map.241 = (bf16[3,512,768]{2,1,0:T(8,128)(2,1)}, bf16[512,768]{1,0:T(8,128)(2,1)}, f32[3,4,512]{2,1,0:T(4,128)}) custom-call(bf16[512,768]{1,0:T(8,128)(2,1)} %bitcast.112, bf16[3,768,768]{2,1,0:T(8,128)(2,1)} %bitcast.110, f32[8,768]{1,0:T(8,128)} %get-tuple-element.231.rows_ref.rows, s32[1,512]{1,0:T(1,128)} %bitcast.136, s32[512,1]{1,0:T(8,128)} %copy.58.seg_col_ref), custom_call_target="tpu_custom_call" | custom-call | flops 115000000 | bytes 1024 | tf_op jit(solution)/shard_map/pallas_call | solution.py:561
  103.5 5.4 %collective-permute-done.14.refs_2_ = bf16[4,24,3840]{2,1,0:T(8,128)(2,1)} collective-permute-done((bf16[4,24,3840]{2,1,0:T(8,128)(2,1)S(1)}, bf16[4,24,3840]{2,1,0:T(8,128)(2,1)}, u32[]{:S(2)}, u32[]{:S(2)}) %collective-permute-start.14) | collective-permute-done | bytes 737312 | tf_op jit(solution)/shard_map/ppermute | solution.py:52
  119.2 3.5 all-to-all-start.3
  122.7 6.7 %shard_map.242 = (bf16[1,32,24,768]{3,2,1,0:T(8,128)(2,1)}, bf16[4,32,24,768]{3,2,1,0:T(8,128)(2,1)}) custom-call(s32[1]{0:T(128)} %bitcast.21.me_ref, bf16[4,24,3840]{2,1,0:T(8,128)(2,1)} %copy-done.1, bf16[4,24,3840]{2,1,0:T(8,128)(2,1)} %copy-done.9, bf16[4,24,3840]{2,1,0:T(8,128)(2,1)} %collective-permute-done.14.refs_2_, ...), custom_call_target="tpu_custom_call" | custom-call | flops 115000000 | bytes 1024 | tf_op jit(solution)/shard_map/pallas_call | solution.py:157
  129.4 5.5 %shard_map.243 = (f32[512,768]{1,0:T(8,128)}, bf16[512,768]{1,0:T(8,128)(2,1)}, bf16[512,768]{1,0:T(8,128)(2,1)}, f32[512,1]{1,0:T(8,128)}, f32[2,128]{1,0:T(2,128)}) custom-call(bf16[512,768]{1,0:T(8,128)(2,1)} %get-tuple-element.235.ctx.refs_0_, bf16[1,768,768]{2,1,0:T(8,128)(2,1)} %bitcast.144, bf16[512,768]{1,0:T(8,128)(2,1)} %bitcast.113, ...), custom_call_target="tpu_custom_call" | custom-call | flops 5750000128 | bytes 1024 | tf_op jit(solution)/shard_map/pallas_call | solution.py:760
  135.0 8.3 %shard_map.244 = (bf16[512,3072]{1,0:T(8,128)(2,1)}, bf16[512,3072]{1,0:T(8,128)(2,1)}) custom-call(bf16[512,768]{1,0:T(8,128)(2,1)} %get-tuple-element.252.x_ref.refs_2_, bf16[4,768,768]{2,1,0:T(8,128)(2,1)} %bitcast.142, f32[1,3072]{1,0:T(1,128)} %get-tuple-element.254.bias_ref), custom_call_target="tpu_custom_call" | custom-call | flops 9200000000 | bytes 1024 | tf_op jit(solution)/shard_map/pallas_call | solution.py:676
  146.7 3.7 all-to-all-start.4
  150.4 12.6 %shard_map.245 = (bf16[512,768]{1,0:T(8,128)(2,1)}, bf16[512,768]{1,0:T(8,128)(2,1)}, f32[512,1]{1,0:T(8,128)}, bf16[32,768]{1,0:T(8,128)(2,1)}, f32[3,128]{1,0:T(4,128)}, /*index=5*/bf16[3072,768]{1,0:T(8,128)(2,1)}) custom-call(s32[1]{0:T(128)} %bitcast.21.me_ref, bf16[512,3072]{1,0:T(8,128)(2,1)} %get-tuple-element.259.active.left_ref, ...), custom_call_target="tpu_custom_call" | custom-call | flops 10350000128 | bytes 1024 | tf_op jit(solution)/shard_map/pallas_call | solution.py:827
  163.1 3.3 collective-permute-start.27
  172.5 2.7 collective-permute-start.30
  181.9 2.6 shard_map.246.pool
  184.5 3.5 all-to-all-start.5
  188.0 5.8 %shard_map.247 = (f32[512,768]{1,0:T(8,128)}, bf16[512,768]{1,0:T(8,128)(2,1)}, f32[3,768]{1,0:T(4,128)}) custom-call(bf16[512,768]{1,0:T(8,128)(2,1)} %bitcast.120, f32[512,1]{1,0:T(8,128)} %compare_convert_fusion.valid, f32[32,512]{1,0:T(8,128)} %fusion.14.hot, f32[32,768]{1,0:T(8,128)} %shard_map.246.pool, bf16[512,768]{1,0:T(8,128)(2,1)} %get-tuple-element.271.unit, ...), custom_call_target="tpu_custom_call" | custom-call | flops 6899999744 | bytes 1024 | tf_op jit(solution)/shard_map/pallas_call | solution.py:866
  193.8 7.2 %shard_map.248 = (bf16[2,8,192,384]{3,2,1,0:T(8,128)(2,1)}, bf16[2,8,192,384]{3,2,1,0:T(8,128)(2,1)}) custom-call(s32[1]{0:T(128)} %bitcast.34.core_ref, bf16[512,3072]{1,0:T(8,128)(2,1)} %get-tuple-element.259.active.left_ref, bf16[512,768]{1,0:T(8,128)(2,1)} %get-tuple-element.282.right_ref.low), custom_call_target="tpu_custom_call" | custom-call | flops 8049999872 | bytes 1024 | tf_op jit(solution)/shard_map/pallas_call | solution.py:434
  203.1 3.5 all-to-all-start.6
  206.7 4.3 %shard_map.249 = (bf16[4,192,384]{2,1,0:T(8,128)(2,1)}, bf16[4,192,384]{2,1,0:T(8,128)(2,1)}, bf16[4,192,384]{2,1,0:T(8,128)(2,1)}, bf16[4,192,384]{2,1,0:T(8,128)(2,1)}) custom-call(s32[2]{0:T(128)} %pad_add_fusion.1.at_ref, bf16[2,4,2,192,384]{4,3,2,1,0:T(8,128)(2,1)} %bitcast.116, bf16[2,4,2,192,384]{4,3,2,1,0:T(8,128)(2,1)} %bitcast.46.got_ref), custom_call_target="tpu_custom_call" | custom-call | flops 1150000000 | bytes 1024 | tf_op jit(solution)/shard_map/pallas_call | solution.py:292
  214.5 13.8 %shard_map.250 = (bf16[512,3072]{1,0:T(8,128)(2,1)}, f32[1,3072]{1,0:T(1,128)}, bf16[512,768]{1,0:T(8,128)(2,1)}, bf16[4,512,192]{2,1,0:T(8,128)(2,1)}, f32[3,768]{1,0:T(4,128)}) custom-call(bf16[512,768]{1,0:T(8,128)(2,1)} %get-tuple-element.282.right_ref.low, bf16[3072,768]{1,0:T(8,128)(2,1)} %get-tuple-element.283.w_back, ...), custom_call_target="tpu_custom_call" | custom-call | flops 16099999744 | bytes 1024 | tf_op jit(solution)/shard_map/pallas_call | solution.py:912
  228.2 9.3 %shard_map.251 = (bf16[2,8,120,768]{3,2,1,0:T(8,128)(2,1)}, bf16[2,8,120,768]{3,2,1,0:T(8,128)(2,1)}) custom-call(s32[1]{0:T(128)} %bitcast.me_ref, bf16[512,768]{1,0:T(8,128)(2,1)} %get-tuple-element.235.ctx.refs_0_, bf16[4,512,192]{2,1,0:T(8,128)(2,1)} %get-tuple-element.288.refs_1_, bf16[512,768]{1,0:T(8,128)(2,1)} %get-tuple-element.252.x_ref.refs_2_, ...), custom_call_target="tpu_custom_call" | custom-call | flops 9200000000 | bytes 1024 | tf_op jit(solution)/shard_map/pallas_call | solution.py:387
  240.8 2.7 shard_map.253
  245.7 4.9 %shard_map.252 = (bf16[4,120,768]{2,1,0:T(8,128)(2,1)}, bf16[4,120,768]{2,1,0:T(8,128)(2,1)}, bf16[4,120,768]{2,1,0:T(8,128)(2,1)}, bf16[4,120,768]{2,1,0:T(8,128)(2,1)}) custom-call(s32[2]{0:T(128)} %pad_add_fusion.1.at_ref, bf16[2,4,2,120,768]{4,3,2,1,0:T(8,128)(2,1)} %bitcast.115, bf16[2,4,2,120,768]{4,3,2,1,0:T(8,128)(2,1)} %bitcast.49.got_ref), custom_call_target="tpu_custom_call" | custom-call | flops 1150000000 | bytes 1024 | tf_op jit(solution)/shard_map/pallas_call | solution.py:292
  254.1 4.8 %all-to-all-start.7 = ((bf16[4,192,384]{2,1,0:T(8,128)(2,1)}), bf16[4,192,384]{2,1,0:T(8,128)(2,1)S(1)}, u32[]{:S(2)}, u32[]{:S(2)}) async-start(bf16[4,192,384]{2,1,0:T(8,128)(2,1)} %shard_map.253), calls=%async_computation.7 | async-start | bytes 1179648 | tf_op jit(solution)/shard_map/all_to_all | solution.py:61
  258.9 20.3 %shard_map.254 = (bf16[3,512,768]{2,1,0:T(8,128)(2,1)}, bf16[4,512,576]{2,1,0:T(8,128)(2,1)}, f32[2,768]{1,0:T(2,128)}) custom-call(bf16[512,768]{1,0:T(8,128)(2,1)} %get-tuple-element.308.gb_ref.residual, bf16[768,768]{1,0:T(8,128)(2,1)} %bitcast.145, bf16[3,512,768]{2,1,0:T(8,128)(2,1)} %get-tuple-element.309.qkv_ref, ...), custom_call_target="tpu_custom_call" | custom-call | flops 23000000512 | bytes 1024 | tf_op jit(solution)/shard_map/pallas_call | solution.py:636
  279.2 6.8 %shard_map.255 = (bf16[2,8,48,1152]{3,2,1,0:T(8,128)(2,1)}, bf16[2,8,48,1152]{3,2,1,0:T(8,128)(2,1)}) custom-call(s32[1]{0:T(128)} %bitcast.me_ref, bf16[512,768]{1,0:T(8,128)(2,1)} %bitcast.114, bf16[4,512,576]{2,1,0:T(8,128)(2,1)} %get-tuple-element.311.refs_1_), custom_call_target="tpu_custom_call" | custom-call | flops 9200000000 | bytes 1024 | tf_op jit(solution)/shard_map/pallas_call | solution.py:387
  286.2 6.0 %shard_map.256 = bf16[512,768]{1,0:T(8,128)(2,1)} custom-call(bf16[3,512,768]{2,1,0:T(8,128)(2,1)} %get-tuple-element.321.grad, bf16[3,768,768]{2,1,0:T(8,128)(2,1)} %bitcast.111, bf16[512,768]{1,0:T(8,128)(2,1)} %get-tuple-element.308.gb_ref.residual), custom_call_target="tpu_custom_call" | custom-call | flops 6899999744 | bytes 1024 | tf_op jit(solution)/shard_map/pallas_call | solution.py:949
  292.2 3.5 all-to-all-start.8
  296.6 3.1 shard_map.258
  304.8 3.8 %shard_map.257 = (bf16[4,48,1152]{2,1,0:T(8,128)(2,1)}, bf16[4,48,1152]{2,1,0:T(8,128)(2,1)}, bf16[4,48,1152]{2,1,0:T(8,128)(2,1)}, bf16[4,48,1152]{2,1,0:T(8,128)(2,1)}) custom-call(s32[2]{0:T(128)} %pad_add_fusion.1.at_ref, bf16[2,4,2,48,1152]{4,3,2,1,0:T(8,128)(2,1)} %bitcast.147, bf16[2,4,2,48,1152]{4,3,2,1,0:T(8,128)(2,1)} %bitcast.52.got_ref), custom_call_target="tpu_custom_call" | custom-call | flops 1150000000 | bytes 1024 | tf_op jit(solution)/shard_map/pallas_call | solution.py:292
  310.7 7.7 %collective-permute-done.44 = bf16[120,768]{1,0:T(8,128)(2,1)} collective-permute-done((bf16[120,768]{1,0:T(8,128)(2,1)}, bf16[120,768]{1,0:T(8,128)(2,1)}, u32[]{:S(2)}, u32[]{:S(2)}) %collective-permute-start.44) | collective-permute-done | bytes 184352 | tf_op jit(solution)/shard_map/ppermute | solution.py:46
  319.4 3.6 all-to-all-start.9
  330.7 4.7 %shard_map.259 = f32[32,384]{1,0:T(8,128)} custom-call(f32[2,768]{1,0:T(2,128)} %get-tuple-element.346.attn, f32[3,768]{1,0:T(4,128)} %get-tuple-element.347.out, f32[3,768]{1,0:T(4,128)} %get-tuple-element.348.ffn, f32[1,3072]{1,0:T(1,128)} %get-tuple-element.349.inb, f32[2,128]{1,0:T(2,128)} %get-tuple-element.350.stats_a, f32[3,128]{1,0:T(4,128)} %get-tuple-element.351.stats_b), custom_call_target="tpu_custom_call" | custom-call | flops 4600000000 | bytes 1024 | tf_op jit(solution)/shard_map/pallas_call | solution.py:1033
  337.3 6.2 %collective-permute-done.46.refs_1_ = bf16[4,48,1152]{2,1,0:T(8,128)(2,1)} collective-permute-done((bf16[4,48,1152]{2,1,0:T(8,128)(2,1)}, bf16[4,48,1152]{2,1,0:T(8,128)(2,1)}, u32[]{:S(2)}, u32[]{:S(2)}) %collective-permute-start.46) | collective-permute-done | bytes 442400 | tf_op jit(solution)/shard_map/ppermute | solution.py:52
  347.2 5.1 %all-to-all-start.10 = ((f32[32,1,384]{2,1,0:T(1,128)}), f32[32,1,384]{2,1,0:T(1,128)S(1)}, u32[]{:S(2)}, u32[]{:S(2)}) async-start(f32[32,1,384]{2,1,0:T(1,128)} %copy.65), calls=%async_computation.10 | async-start | bytes 98304 | tf_op jit(solution)/shard_map/all_to_all | solution.py:1295
  355.6 2.4 collective-permute-start.49
  362.6 4.7 %collective-permute-done.49 = bf16[48,1152]{1,0:T(8,128)(2,1)S(1)} collective-permute-done((bf16[48,1152]{1,0:T(8,128)(2,1)S(1)}, bf16[48,1152]{1,0:T(8,128)(2,1)S(1)}, u32[]{:S(2)}, u32[]{:S(2)}) %collective-permute-start.49) | collective-permute-done | bytes 110624 | tf_op jit(solution)/shard_map/ppermute | solution.py:46
  (267 shorter events, 99.1 us)
Async XLA Ops:
  7.1 9.5 %collective-permute-start.2 = (bf16[80,768]{1,0:T(8,128)(2,1)}, bf16[80,768]{1,0:T(8,128)(2,1)S(1)}, u32[]{:S(2)}, u32[]{:S(2)}) collective-permute-start(bf16[80,768]{1,0:T(8,128)(2,1)} %get-tuple-element.195), channel_id=1, source_target_pairs={{0,24},{4,28},{8,16},{12,20},{16,8},{20,12},{24,0},{28,4},{1,25},{... | collective-permute-start | bytes 368648 | tf_op jit(solution)/shard_map/ppermute | solution.py:46
  12.2 7.2 %collective-permute-start = (bf16[80,768]{1,0:T(8,128)(2,1)}, bf16[80,768]{1,0:T(8,128)(2,1)S(1)}, u32[]{:S(2)}, u32[]{:S(2)}) collective-permute-start(bf16[80,768]{1,0:T(8,128)(2,1)} %get-tuple-element.193), channel_id=1, source_target_pairs={{0,8},{4,12},{8,0},{12,4},{16,24},{20,28},{24,16},{28,20},{1,9},{5... | collective-permute-start | bytes 368648 | tf_op jit(solution)/shard_map/ppermute | solution.py:46
  12.2 10.6 %collective-permute-start.1 = (bf16[80,768]{1,0:T(8,128)(2,1)}, bf16[80,768]{1,0:T(8,128)(2,1)S(1)}, u32[]{:S(2)}, u32[]{:S(2)}) collective-permute-start(bf16[80,768]{1,0:T(8,128)(2,1)} %get-tuple-element.194), channel_id=1, source_target_pairs={{0,16},{4,20},{8,24},{12,28},{16,0},{20,4},{24,8},{28,12},{1,17},{... | collective-permute-start | bytes 368648 | tf_op jit(solution)/shard_map/ppermute | solution.py:46
  24.8 31.8 %all-to-all-start = ((bf16[4,24,3840]{2,1,0:T(8,128)(2,1)}), bf16[4,24,3840]{2,1,0:T(8,128)(2,1)S(1)}, u32[]{:S(2)}, u32[]{:S(2)}) async-start(bf16[4,24,3840]{2,1,0:T(8,128)(2,1)} %broadcast_select_fusion.2), calls=%async_computation | async-start | bytes 1474560 | tf_op jit(solution)/shard_map/all_to_all | solution.py:61
  28.5 27.1 %collective-permute-start.3 = (bf16[4,80,768]{2,1,0:T(8,128)(2,1)S(1)}, bf16[4,80,768]{2,1,0:T(8,128)(2,1)S(1)}, u32[]{:S(2)}, u32[]{:S(2)}) collective-permute-start(bf16[4,80,768]{2,1,0:T(8,128)(2,1)S(1)} %pad_maximum_fusion.2.refs_0_), channel_id=1, source_target_pairs={{0,6},{1,7},{2,4},{3,5},{4,2},{5,3},{6,0},{7,1},{8,14},{9,15},{10,... | collective-permute-start | bytes 1474568 | tf_op jit(solution)/shard_map/ppermute | solution.py:52
  31.0 24.7 %collective-permute-start.4 = (bf16[4,80,768]{2,1,0:T(8,128)(2,1)S(1)}, bf16[4,80,768]{2,1,0:T(8,128)(2,1)S(1)}, u32[]{:S(2)}, u32[]{:S(2)}) collective-permute-start(bf16[4,80,768]{2,1,0:T(8,128)(2,1)S(1)} %pad_maximum_fusion.2.refs_0_), channel_id=1, source_target_pairs={{0,2},{1,3},{2,0},{3,1},{4,6},{5,7},{6,4},{7,5},{8,10},{9,11},{10,... | collective-permute-start | bytes 1474568 | tf_op jit(solution)/shard_map/ppermute | solution.py:52
  31.5 25.0 %collective-permute-start.5 = (bf16[4,80,768]{2,1,0:T(8,128)(2,1)S(1)}, bf16[4,80,768]{2,1,0:T(8,128)(2,1)}, u32[]{:S(2)}, u32[]{:S(2)}) collective-permute-start(bf16[4,80,768]{2,1,0:T(8,128)(2,1)S(1)} %pad_maximum_fusion.2.refs_0_), channel_id=1, source_target_pairs={{0,4},{1,5},{2,6},{3,7},{4,0},{5,1},{6,2},{7,3},{8,12},{9,13},{10,... | collective-permute-start | bytes 1474568 | tf_op jit(solution)/shard_map/ppermute | solution.py:52
  32.1 13.9 %collective-permute-start.6 = (bf16[128,768]{1,0:T(8,128)(2,1)S(1)}, bf16[128,768]{1,0:T(8,128)(2,1)S(1)}, u32[]{:S(2)}, u32[]{:S(2)}) collective-permute-start(bf16[128,768]{1,0:T(8,128)(2,1)S(1)} %get-tuple-element.425), channel_id=1, source_target_pairs={{0,8},{8,0},{4,12},{12,4},{1,9},{9,1},{5,13},{13,5},{2,10},{10,2},... | collective-permute-start | bytes 589832 | tf_op jit(solution)/shard_map/ppermute | solution.py:68
  36.0 19.7 %collective-permute-start.7 = (bf16[128,768]{1,0:T(8,128)(2,1)S(1)}, bf16[128,768]{1,0:T(8,128)(2,1)S(1)}, u32[]{:S(2)}, u32[]{:S(2)}) collective-permute-start(bf16[128,768]{1,0:T(8,128)(2,1)S(1)} %get-tuple-element.424), channel_id=1, source_target_pairs={{0,16},{16,0},{4,20},{20,4},{1,17},{17,1},{5,21},{21,5},{2,18},{18... | collective-permute-start | bytes 589832 | tf_op jit(solution)/shard_map/ppermute | solution.py:68
  46.0 9.7 %collective-permute-start.8 = (bf16[128,768]{1,0:T(8,128)(2,1)S(1)}, bf16[128,768]{1,0:T(8,128)(2,1)S(1)}, u32[]{:S(2)}, u32[]{:S(2)}) collective-permute-start(bf16[128,768]{1,0:T(8,128)(2,1)S(1)} %get-tuple-element.423), channel_id=1, source_target_pairs={{0,24},{24,0},{4,28},{28,4},{1,25},{25,1},{5,29},{29,5},{2,26},{26... | collective-permute-start | bytes 589832 | tf_op jit(solution)/shard_map/ppermute | solution.py:68
  62.0 15.6 %all-to-all-start.1 = ((bf16[4,128,768]{2,1,0:T(8,128)(2,1)}), bf16[4,128,768]{2,1,0:T(8,128)(2,1)S(1)}, u32[]{:S(2)}, u32[]{:S(2)}) async-start(bf16[4,128,768]{2,1,0:T(8,128)(2,1)} %maximum_select_fusion), calls=%async_computation.1 | async-start | bytes 1572864 | tf_op jit(solution)/shard_map/all_to_all | solution.py:107
  65.6 37.8 %collective-permute-start.13 = (bf16[4,24,3840]{2,1,0:T(8,128)(2,1)S(1)}, bf16[4,24,3840]{2,1,0:T(8,128)(2,1)S(1)}, u32[]{:S(2)}, u32[]{:S(2)}) collective-permute-start(bf16[4,24,3840]{2,1,0:T(8,128)(2,1)S(1)} %all-to-all-done.refs_0_), channel_id=1, source_target_pairs={{0,6},{1,7},{2,4},{3,5},{4,2},{5,3},{6,0},{7,1},{8,14},{9,15},{10,... | collective-permute-start | bytes 2211848 | tf_op jit(solution)/shard_map/ppermute | solution.py:52
  68.6 40.3 %collective-permute-start.14 = (bf16[4,24,3840]{2,1,0:T(8,128)(2,1)S(1)}, bf16[4,24,3840]{2,1,0:T(8,128)(2,1)}, u32[]{:S(2)}, u32[]{:S(2)}) collective-permute-start(bf16[4,24,3840]{2,1,0:T(8,128)(2,1)S(1)} %all-to-all-done.refs_0_), channel_id=1, source_target_pairs={{0,2},{1,3},{2,0},{3,1},{4,6},{5,7},{6,4},{7,5},{8,10},{9,11},{10,... | collective-permute-start | bytes 2211848 | tf_op jit(solution)/shard_map/ppermute | solution.py:52
  68.7 40.2 %collective-permute-start.15 = (bf16[4,24,3840]{2,1,0:T(8,128)(2,1)S(1)}, bf16[4,24,3840]{2,1,0:T(8,128)(2,1)}, u32[]{:S(2)}, u32[]{:S(2)}) collective-permute-start(bf16[4,24,3840]{2,1,0:T(8,128)(2,1)S(1)} %all-to-all-done.refs_0_), channel_id=1, source_target_pairs={{0,4},{1,5},{2,6},{3,7},{4,0},{5,1},{6,2},{7,3},{8,12},{9,13},{10,... | collective-permute-start | bytes 2211848 | tf_op jit(solution)/shard_map/ppermute | solution.py:52
  84.9 24.0 %all-to-all-start.2 = ((bf16[4,96,768]{2,1,0:T(8,128)(2,1)}), bf16[4,96,768]{2,1,0:T(8,128)(2,1)S(1)}, u32[]{:S(2)}, u32[]{:S(2)}) async-start(bf16[4,96,768]{2,1,0:T(8,128)(2,1)} %broadcast_select_fusion.3), calls=%async_computation.2 | async-start | bytes 1179648 | tf_op jit(solution)/shard_map/all_to_all | solution.py:61
  114.7 28.5 %collective-permute-start.20 = (bf16[4,96,768]{2,1,0:T(8,128)(2,1)S(1)}, bf16[4,96,768]{2,1,0:T(8,128)(2,1)S(1)}, u32[]{:S(2)}, u32[]{:S(2)}) collective-permute-start(bf16[4,96,768]{2,1,0:T(8,128)(2,1)S(1)} %all-to-all-done.2.refs_0_), channel_id=1, source_target_pairs={{0,6},{1,7},{2,4},{3,5},{4,2},{5,3},{6,0},{7,1},{8,14},{9,15},{10,... | collective-permute-start | bytes 1769480 | tf_op jit(solution)/shard_map/ppermute | solution.py:52
  116.0 27.8 %collective-permute-start.21 = (bf16[4,96,768]{2,1,0:T(8,128)(2,1)S(1)}, bf16[4,96,768]{2,1,0:T(8,128)(2,1)}, u32[]{:S(2)}, u32[]{:S(2)}) collective-permute-start(bf16[4,96,768]{2,1,0:T(8,128)(2,1)S(1)} %all-to-all-done.2.refs_0_), channel_id=1, source_target_pairs={{0,2},{1,3},{2,0},{3,1},{4,6},{5,7},{6,4},{7,5},{8,10},{9,11},{10,... | collective-permute-start | bytes 1769480 | tf_op jit(solution)/shard_map/ppermute | solution.py:52
  117.7 26.1 %collective-permute-start.22 = (bf16[4,96,768]{2,1,0:T(8,128)(2,1)S(1)}, bf16[4,96,768]{2,1,0:T(8,128)(2,1)}, u32[]{:S(2)}, u32[]{:S(2)}) collective-permute-start(bf16[4,96,768]{2,1,0:T(8,128)(2,1)S(1)} %all-to-all-done.2.refs_0_), channel_id=1, source_target_pairs={{0,4},{1,5},{2,6},{3,7},{4,0},{5,1},{6,2},{7,3},{8,12},{9,13},{10,... | collective-permute-start | bytes 1769480 | tf_op jit(solution)/shard_map/ppermute | solution.py:52
  119.2 24.6 %all-to-all-start.3 = ((bf16[4,128,768]{2,1,0:T(8,128)(2,1)}), bf16[4,128,768]{2,1,0:T(8,128)(2,1)S(1)}, u32[]{:S(2)}, u32[]{:S(2)}) async-start(bf16[4,128,768]{2,1,0:T(8,128)(2,1)} %maximum_select_fusion.1), calls=%async_computation.3 | async-start | bytes 1572864 | tf_op jit(solution)/shard_map/all_to_all | solution.py:61
  143.8 6.5 %collective-permute-start.23 = (bf16[4,96,768]{2,1,0:T(8,128)(2,1)S(1)}, bf16[4,96,768]{2,1,0:T(8,128)(2,1)}, u32[]{:S(2)}, u32[]{:S(2)}) collective-permute-start(bf16[4,96,768]{2,1,0:T(8,128)(2,1)S(1)} %all-to-all-done.2.refs_0_), channel_id=1, source_target_pairs={{0,1},{1,0},{2,3},{3,2},{4,5},{5,4},{6,7},{7,6},{8,9},{9,8},{10,11... | collective-permute-start | bytes 1769480 | tf_op jit(solution)/shard_map/ppermute | solution.py:46
  143.9 6.5 %collective-permute-start.24 = (bf16[4,96,768]{2,1,0:T(8,128)(2,1)S(1)}, bf16[4,96,768]{2,1,0:T(8,128)(2,1)}, u32[]{:S(2)}, u32[]{:S(2)}) collective-permute-start(bf16[4,96,768]{2,1,0:T(8,128)(2,1)S(1)} %collective-permute-done.20.refs_1_), channel_id=1, source_target_pairs={{0,1},{1,0},{2,3},{3,2},{4,5},{5,4},{6,7},{7,6},{8,9},{9,8},{10,11... | collective-permute-start | bytes 1769480 | tf_op jit(solution)/shard_map/ppermute | solution.py:46
  144.4 6.0 %collective-permute-start.25 = (bf16[4,96,768]{2,1,0:T(8,128)(2,1)}, bf16[4,96,768]{2,1,0:T(8,128)(2,1)}, u32[]{:S(2)}, u32[]{:S(2)}) collective-permute-start(bf16[4,96,768]{2,1,0:T(8,128)(2,1)} %collective-permute-done.21.refs_2_), channel_id=1, source_target_pairs={{0,1},{1,0},{2,3},{3,2},{4,5},{5,4},{6,7},{7,6},{8,9},{9,8},{10,11... | collective-permute-start | bytes 1769480 | tf_op jit(solution)/shard_map/ppermute | solution.py:46
  144.5 5.9 %collective-permute-start.26 = (bf16[4,96,768]{2,1,0:T(8,128)(2,1)}, bf16[4,96,768]{2,1,0:T(8,128)(2,1)}, u32[]{:S(2)}, u32[]{:S(2)}) collective-permute-start(bf16[4,96,768]{2,1,0:T(8,128)(2,1)} %collective-permute-done.22.refs_3_), channel_id=1, source_target_pairs={{0,1},{1,0},{2,3},{3,2},{4,5},{5,4},{6,7},{7,6},{8,9},{9,8},{10,11... | collective-permute-start | bytes 1769480 | tf_op jit(solution)/shard_map/ppermute | solution.py:46
  146.7 16.4 %all-to-all-start.4 = ((bf16[4,128,768]{2,1,0:T(8,128)(2,1)}), bf16[4,128,768]{2,1,0:T(8,128)(2,1)S(1)}, u32[]{:S(2)}, u32[]{:S(2)}) async-start(bf16[4,128,768]{2,1,0:T(8,128)(2,1)} %maximum_select_fusion.2), calls=%async_computation.4 | async-start | bytes 1572864 | tf_op jit(solution)/shard_map/all_to_all | solution.py:107
  163.1 6.4 %collective-permute-start.27 = (bf16[32,768]{1,0:T(8,128)(2,1)}, bf16[32,768]{1,0:T(8,128)(2,1)S(1)}, u32[]{:S(2)}, u32[]{:S(2)}) collective-permute-start(bf16[32,768]{1,0:T(8,128)(2,1)} %get-tuple-element.268), channel_id=1, source_target_pairs={{0,24},{4,28},{8,16},{12,20},{16,8},{20,12},{24,0},{28,4},{1,25},{... | collective-permute-start | bytes 147464 | tf_op jit(solution)/shard_map/ppermute | solution.py:46
  172.5 5.8 %collective-permute-start.30 = (bf16[1,32,768]{2,1,0:T(8,128)(2,1)S(1)}, bf16[1,32,768]{2,1,0:T(8,128)(2,1)S(1)}, u32[]{:S(2)}, u32[]{:S(2)}) collective-permute-start(bf16[1,32,768]{2,1,0:T(8,128)(2,1)S(1)} %get-tuple-element.416), channel_id=1, source_target_pairs={{0,6},{1,7},{2,4},{3,5},{4,2},{5,3},{6,0},{7,1},{8,14},{9,15},{10,... | collective-permute-start | bytes 147464 | tf_op jit(solution)/shard_map/ppermute | solution.py:52
  184.5 16.5 %all-to-all-start.5 = ((bf16[4,128,768]{2,1,0:T(8,128)(2,1)}), bf16[4,128,768]{2,1,0:T(8,128)(2,1)S(1)}, u32[]{:S(2)}, u32[]{:S(2)}) async-start(bf16[4,128,768]{2,1,0:T(8,128)(2,1)} %bitcast.45), calls=%async_computation.5 | async-start | bytes 1572864 | tf_op jit(solution)/shard_map/all_to_all | solution.py:112
  203.1 34.4 %all-to-all-start.6 = ((bf16[4,128,768]{2,1,0:T(8,128)(2,1)}), bf16[4,128,768]{2,1,0:T(8,128)(2,1)S(1)}, u32[]{:S(2)}, u32[]{:S(2)}) async-start(bf16[4,128,768]{2,1,0:T(8,128)(2,1)} %broadcast_select_fusion.1), calls=%async_computation.6 | async-start | bytes 1572864 | tf_op jit(solution)/shard_map/all_to_all | solution.py:61
  211.0 26.5 %collective-permute-start.35 = (bf16[4,192,384]{2,1,0:T(8,128)(2,1)}, bf16[4,192,384]{2,1,0:T(8,128)(2,1)S(1)}, u32[]{:S(2)}, u32[]{:S(2)}) collective-permute-start(bf16[4,192,384]{2,1,0:T(8,128)(2,1)} %get-tuple-element.292), channel_id=1, source_target_pairs={{0,6},{1,7},{2,4},{3,5},{4,2},{5,3},{6,0},{7,1},{8,14},{9,15},{10,... | collective-permute-start | bytes 1769480 | tf_op jit(solution)/shard_map/ppermute | solution.py:52
  212.6 26.8 %collective-permute-start.36 = (bf16[4,192,384]{2,1,0:T(8,128)(2,1)}, bf16[4,192,384]{2,1,0:T(8,128)(2,1)S(1)}, u32[]{:S(2)}, u32[]{:S(2)}) collective-permute-start(bf16[4,192,384]{2,1,0:T(8,128)(2,1)} %get-tuple-element.293), channel_id=1, source_target_pairs={{0,2},{1,3},{2,0},{3,1},{4,6},{5,7},{6,4},{7,5},{8,10},{9,11},{10,... | collective-permute-start | bytes 1769480 | tf_op jit(solution)/shard_map/ppermute | solution.py:52
  212.9 27.1 %collective-permute-start.37 = (bf16[4,192,384]{2,1,0:T(8,128)(2,1)}, bf16[4,192,384]{2,1,0:T(8,128)(2,1)S(1)}, u32[]{:S(2)}, u32[]{:S(2)}) collective-permute-start(bf16[4,192,384]{2,1,0:T(8,128)(2,1)} %get-tuple-element.294), channel_id=1, source_target_pairs={{0,4},{1,5},{2,6},{3,7},{4,0},{5,1},{6,2},{7,3},{8,12},{9,13},{10,... | collective-permute-start | bytes 1769480 | tf_op jit(solution)/shard_map/ppermute | solution.py:52
  250.6 35.3 %collective-permute-start.39 = (bf16[4,120,768]{2,1,0:T(8,128)(2,1)}, bf16[4,120,768]{2,1,0:T(8,128)(2,1)S(1)}, u32[]{:S(2)}, u32[]{:S(2)}) collective-permute-start(bf16[4,120,768]{2,1,0:T(8,128)(2,1)} %get-tuple-element.316), channel_id=1, source_target_pairs={{0,6},{1,7},{2,4},{3,5},{4,2},{5,3},{6,0},{7,1},{8,14},{9,15},{10,... | collective-permute-start | bytes 2211848 | tf_op jit(solution)/shard_map/ppermute | solution.py:52
  252.7 33.2 %collective-permute-start.40 = (bf16[4,120,768]{2,1,0:T(8,128)(2,1)}, bf16[4,120,768]{2,1,0:T(8,128)(2,1)}, u32[]{:S(2)}, u32[]{:S(2)}) collective-permute-start(bf16[4,120,768]{2,1,0:T(8,128)(2,1)} %get-tuple-element.317), channel_id=1, source_target_pairs={{0,2},{1,3},{2,0},{3,1},{4,6},{5,7},{6,4},{7,5},{8,10},{9,11},{10,... | collective-permute-start | bytes 2211848 | tf_op jit(solution)/shard_map/ppermute | solution.py:52
  252.9 33.3 %collective-permute-start.41 = (bf16[4,120,768]{2,1,0:T(8,128)(2,1)}, bf16[4,120,768]{2,1,0:T(8,128)(2,1)}, u32[]{:S(2)}, u32[]{:S(2)}) collective-permute-start(bf16[4,120,768]{2,1,0:T(8,128)(2,1)} %get-tuple-element.318), channel_id=1, source_target_pairs={{0,4},{1,5},{2,6},{3,7},{4,0},{5,1},{6,2},{7,3},{8,12},{9,13},{10,... | collective-permute-start | bytes 2211848 | tf_op jit(solution)/shard_map/ppermute | solution.py:52
  254.1 32.1 %all-to-all-start.7 = ((bf16[4,192,384]{2,1,0:T(8,128)(2,1)}), bf16[4,192,384]{2,1,0:T(8,128)(2,1)S(1)}, u32[]{:S(2)}, u32[]{:S(2)}) async-start(bf16[4,192,384]{2,1,0:T(8,128)(2,1)} %shard_map.253), calls=%async_computation.7 | async-start | bytes 1179648 | tf_op jit(solution)/shard_map/all_to_all | solution.py:61
  286.2 6.1 %collective-permute-start.42 = (bf16[2,8,48,1152]{3,2,1,0:T(8,128)(2,1)}, bf16[2,8,48,1152]{3,2,1,0:T(8,128)(2,1)}, u32[]{:S(2)}, u32[]{:S(2)}) collective-permute-start(bf16[2,8,48,1152]{3,2,1,0:T(8,128)(2,1)} %get-tuple-element.320), channel_id=1, source_target_pairs={{0,1},{1,0},{2,3},{3,2},{4,5},{5,4},{6,7},{7,6},{8,9},{9,8},{10,11... | collective-permute-start | bytes 5308424 | tf_op jit(solution)/shard_map/ppermute | solution.py:46
  292.2 26.1 %all-to-all-start.8 = ((bf16[4,128,768]{2,1,0:T(8,128)(2,1)}), bf16[4,128,768]{2,1,0:T(8,128)(2,1)S(1)}, u32[]{:S(2)}, u32[]{:S(2)}) async-start(bf16[4,128,768]{2,1,0:T(8,128)(2,1)} %bitcast.121), calls=%async_computation.8 | async-start | bytes 1572864 | tf_op jit(solution)/shard_map/all_to_all | solution.py:112
  299.7 11.0 %collective-permute-start.43 = (bf16[120,768]{1,0:T(8,128)(2,1)}, bf16[120,768]{1,0:T(8,128)(2,1)S(1)}, u32[]{:S(2)}, u32[]{:S(2)}) collective-permute-start(bf16[120,768]{1,0:T(8,128)(2,1)} %get-tuple-element.336), channel_id=1, source_target_pairs={{0,8},{4,12},{8,0},{12,4},{16,24},{20,28},{24,16},{28,20},{1,9},{5... | collective-permute-start | bytes 552968 | tf_op jit(solution)/shard_map/ppermute | solution.py:46
  301.7 16.6 %collective-permute-start.44 = (bf16[120,768]{1,0:T(8,128)(2,1)}, bf16[120,768]{1,0:T(8,128)(2,1)}, u32[]{:S(2)}, u32[]{:S(2)}) collective-permute-start(bf16[120,768]{1,0:T(8,128)(2,1)} %get-tuple-element.337), channel_id=1, source_target_pairs={{0,16},{4,20},{8,24},{12,28},{16,0},{20,4},{24,8},{28,12},{1,17},{... | collective-permute-start | bytes 552968 | tf_op jit(solution)/shard_map/ppermute | solution.py:46
  304.8 21.8 %collective-permute-start.51 = (bf16[120,768]{1,0:T(8,128)(2,1)}, bf16[120,768]{1,0:T(8,128)(2,1)}, u32[]{:S(2)}, u32[]{:S(2)}) collective-permute-start(bf16[120,768]{1,0:T(8,128)(2,1)} %get-tuple-element.369), channel_id=1, source_target_pairs={{0,24},{4,28},{8,16},{12,20},{16,8},{20,12},{24,0},{28,4},{1,25},{... | collective-permute-start | bytes 552968 | tf_op jit(solution)/shard_map/ppermute | solution.py:46
  319.4 24.7 %all-to-all-start.9 = ((bf16[4,128,768]{2,1,0:T(8,128)(2,1)}), bf16[4,128,768]{2,1,0:T(8,128)(2,1)S(1)}, u32[]{:S(2)}, u32[]{:S(2)}) async-start(bf16[4,128,768]{2,1,0:T(8,128)(2,1)} %broadcast_select_fusion), calls=%async_computation.9 | async-start | bytes 1572864 | tf_op jit(solution)/shard_map/all_to_all | solution.py:61
  323.0 14.3 %collective-permute-start.45 = (bf16[4,48,1152]{2,1,0:T(8,128)(2,1)}, bf16[4,48,1152]{2,1,0:T(8,128)(2,1)}, u32[]{:S(2)}, u32[]{:S(2)}) collective-permute-start(bf16[4,48,1152]{2,1,0:T(8,128)(2,1)} %get-tuple-element.342), channel_id=1, source_target_pairs={{0,6},{1,7},{2,4},{3,5},{4,2},{5,3},{6,0},{7,1},{8,14},{9,15},{10,... | collective-permute-start | bytes 1327112 | tf_op jit(solution)/shard_map/ppermute | solution.py:52
  325.2 18.3 %collective-permute-start.46 = (bf16[4,48,1152]{2,1,0:T(8,128)(2,1)}, bf16[4,48,1152]{2,1,0:T(8,128)(2,1)}, u32[]{:S(2)}, u32[]{:S(2)}) collective-permute-start(bf16[4,48,1152]{2,1,0:T(8,128)(2,1)} %get-tuple-element.343), channel_id=1, source_target_pairs={{0,2},{1,3},{2,0},{3,1},{4,6},{5,7},{6,4},{7,5},{8,10},{9,11},{10,... | collective-permute-start | bytes 1327112 | tf_op jit(solution)/shard_map/ppermute | solution.py:52
  325.3 18.8 %collective-permute-start.47 = (bf16[4,48,1152]{2,1,0:T(8,128)(2,1)}, bf16[4,48,1152]{2,1,0:T(8,128)(2,1)}, u32[]{:S(2)}, u32[]{:S(2)}) collective-permute-start(bf16[4,48,1152]{2,1,0:T(8,128)(2,1)} %get-tuple-element.344), channel_id=1, source_target_pairs={{0,4},{1,5},{2,6},{3,7},{4,0},{5,1},{6,2},{7,3},{8,12},{9,13},{10,... | collective-permute-start | bytes 1327112 | tf_op jit(solution)/shard_map/ppermute | solution.py:52
  347.2 12.4 %all-to-all-start.10 = ((f32[32,1,384]{2,1,0:T(1,128)}), f32[32,1,384]{2,1,0:T(1,128)S(1)}, u32[]{:S(2)}, u32[]{:S(2)}) async-start(f32[32,1,384]{2,1,0:T(1,128)} %copy.65), calls=%async_computation.10 | async-start | bytes 98304 | tf_op jit(solution)/shard_map/all_to_all | solution.py:1295
  353.9 8.7 %collective-permute-start.48 = (bf16[48,1152]{1,0:T(8,128)(2,1)S(1)}, bf16[48,1152]{1,0:T(8,128)(2,1)S(1)}, u32[]{:S(2)}, u32[]{:S(2)}) collective-permute-start(bf16[48,1152]{1,0:T(8,128)(2,1)S(1)} %copy-done.29), channel_id=1, source_target_pairs={{0,8},{4,12},{8,0},{12,4},{16,24},{20,28},{24,16},{28,20},{1,9},{5... | collective-permute-start | bytes 331784 | tf_op jit(solution)/shard_map/ppermute | solution.py:46
  355.6 11.6 %collective-permute-start.49 = (bf16[48,1152]{1,0:T(8,128)(2,1)S(1)}, bf16[48,1152]{1,0:T(8,128)(2,1)S(1)}, u32[]{:S(2)}, u32[]{:S(2)}) collective-permute-start(bf16[48,1152]{1,0:T(8,128)(2,1)S(1)} %copy-done.28), channel_id=1, source_target_pairs={{0,16},{4,20},{8,24},{12,28},{16,0},{20,4},{24,8},{28,12},{1,17},{... | collective-permute-start | bytes 331784 | tf_op jit(solution)/shard_map/ppermute | solution.py:46
  358.1 9.2 %collective-permute-start.50 = (bf16[48,1152]{1,0:T(8,128)(2,1)S(1)}, bf16[48,1152]{1,0:T(8,128)(2,1)S(1)}, u32[]{:S(2)}, u32[]{:S(2)}) collective-permute-start(bf16[48,1152]{1,0:T(8,128)(2,1)S(1)} %copy-done.27), channel_id=1, source_target_pairs={{0,24},{4,28},{8,16},{12,20},{16,8},{20,12},{24,0},{28,4},{1,25},{... | collective-permute-start | bytes 331784 | tf_op jit(solution)/shard_map/ppermute | solution.py:46
  (45 other events, 503.6 us)
